TPU v7x, 128 devices: a whole 4x4x4 slice. The times are simulated.
128 devices in a mesh: row: 8 (over x_hi, z), col: 16 (over x_lo, y, core).
Axes of the slice: x: 4 (x_hi: 2, x_lo: 2; x = x_hi * 2 + x_lo), y: 4, z: 4, core: 2. Of those that a mesh axis runs over, the one named last changes fastest.
Arguments:
- left: float32 [2, 8192, 2560], P(None, 'row', 'col'), may hold values from -6 to 6
- right: float32 [2, 2560, 8192], P(None, 'row', 'col'), may hold values from -0.078125 to 0.078125
- prefix_owner: int32 [64], replicated, may hold values from 0 to 63, each once
- qubit_order: int32 [7], replicated, may hold values from 0 to 6, each once
Outputs:
- relaid: float32 [2, 8192, 8192], P(None, ('row', 'col'))
Inputs may be any that keep to these rules, and one draw needn't show every extreme that they name: `prefix_owner`: each prefix has exactly one owner, each owner one prefix. `qubit_order`: each open qubit appears once.
All inputs are finite; a program needn't handle non-finite values.
Results may differ from a plain program's by a relative error of at most 0.00007.
Values sent between devices are 32-bit elements; how exact they have to be, the bound alone decides.
A program may use at most 192 MiB of HBM per device.

v0:
```python
import jax
import jax.numpy as jnp
from jax import lax
from jax.sharding import PartitionSpec as P

LOW_BITS = 7
PREFIXES = 64


def source_rows(prefix_owner, qubit_order, total, low_bits, prefixes):
    span = 2**low_bits
    index = jnp.arange(total, dtype=jnp.int32)
    owner = index // span
    offset = index % span
    labels = jnp.arange(prefixes, dtype=jnp.int32)
    match = (prefix_owner[None, :] == labels[:, None]).astype(jnp.int32)
    inverse = jnp.sum(match * labels[None, :], axis=1)
    prefix = jnp.take(inverse, owner, axis=0)
    bits = jnp.bitwise_and(jnp.right_shift(offset[:, None], qubit_order[None, :]), 1)
    powers = jnp.left_shift(jnp.ones((low_bits,), jnp.int32), jnp.arange(low_bits, dtype=jnp.int32))
    inner = jnp.sum(bits * powers[None, :], axis=1)
    return prefix * span + inner


def accumulate(left_re, left_im, right_re, right_im):
    highest = lax.Precision.HIGHEST
    real_add = jnp.dot(
        left_re, right_re, preferred_element_type=jnp.float32, precision=highest
    ) - jnp.dot(left_im, right_im, preferred_element_type=jnp.float32, precision=highest)
    imag_add = jnp.dot(
        left_re, right_im, preferred_element_type=jnp.float32, precision=highest
    ) + jnp.dot(left_im, right_re, preferred_element_type=jnp.float32, precision=highest)
    return (real_add, imag_add)


def body(left, right, prefix_owner, qubit_order):
    rows = left.shape[1]
    cols = right.shape[2]
    right_whole = lax.all_gather(right, "row", axis=1, tiled=True)
    piece = lax.all_gather(left, "col", axis=2, tiled=True)
    real_part, imag_part = accumulate(piece[0], piece[1], right_whole[0], right_whole[1])
    row_count = lax.axis_size("row")
    col_count = lax.axis_size("col")
    width = cols // row_count
    total = rows * row_count
    tile = jnp.stack(
        [real_part.reshape(rows, row_count, width), imag_part.reshape(rows, row_count, width)],
        axis=2,
    )
    tile = tile.reshape(rows, row_count, 2 * width)
    middle = lax.all_to_all(tile, "row", split_axis=1, concat_axis=0, tiled=True).reshape(
        total, 2 * width
    )
    source = source_rows(prefix_owner, qubit_order, total, LOW_BITS, PREFIXES)
    ordered = jnp.take(middle, source, axis=0).reshape(total, 1, 2 * width)
    received = lax.all_to_all(ordered, ("row", "col"), split_axis=0, concat_axis=1, tiled=True)
    owned = received.shape[0]
    received = received.reshape(owned, row_count, col_count, 2, width)
    received = jnp.transpose(received, (3, 0, 2, 1, 4))
    return received.reshape(2, owned, col_count * row_count * width)


def solution(mesh):
    in_specs = (P(None, "row", "col"), P(None, "row", "col"), P(), P())
    out_specs = P(None, ("row", "col"), None)
    return jax.shard_map(body, mesh=mesh, in_specs=in_specs, out_specs=out_specs, check_vma=False)
```

profile of v0, /device:TPU:1, one launch (start us, length us, event | category | flops | bytes accessed | tf_op | source)
XLA Modules:
  0.0 526.0 jit_solution(3803993535598130873)
XLA Ops:
  6.5 0.7 all-gather.5.cloned.1.call-update
  11.0 0.8 select_reduce_fusion
  11.7 0.7 fusion.19
  12.4 126.2 %all-gather.5.cloned.1.call-done = f32[2,2560,512]{2,1,0:T(8,128)} async-done(((f32[2,320,512]{2,1,0:T(8,128)}), f32[2,2560,512]{2,1,0:T(8,128)}) %all-gather.5.cloned.1.call-update) | async-done | bytes 10485776 | tf_op jit(solution)/shard_map/all_gather | solution.py:39
  138.7 111.6 %all-gather.3.cloned.1.call-done = f32[2,1024,2560]{1,2,0:T(8,128)} async-done(((f32[2,1024,160]{1,2,0:T(8,128)}), f32[2,1024,2560]{1,2,0:T(8,128)}) %all-gather.3.cloned.1.call-update) | async-done | bytes 20971536 | tf_op jit(solution)/shard_map/all_gather | solution.py:40
  250.3 20.4 %fusion = f32[1024,512]{0,1:T(8,128)S(1)} fusion(f32[2,1024,2560]{1,2,0:T(8,128)} %all-gather.3.cloned.1.call-done, f32[2,2560,512]{2,1,0:T(8,128)} %all-gather.5.cloned.1.call-done), kind=kOutput, calls=%fused_computation.3 | convolution fusion | flops 16106127360 | bytes 17825792 | tf_op jit(solution)/shard_map/dot_general | solution.py:30
  270.7 19.8 %fusion.1 = f32[1024,512]{0,1:T(8,128)S(1)} fusion(f32[2,1024,2560]{1,2,0:T(8,128)} %all-gather.3.cloned.1.call-done, f32[2,2560,512]{2,1,0:T(8,128)S(1)} %copy-done.1), kind=kOutput, calls=%fused_computation.4 | convolution fusion | flops 16106127360 | bytes 17825792 | tf_op jit(solution)/shard_map/dot_general | solution.py:27
  290.5 19.9 %fusion.5 = f32[1024,512]{0,1:T(8,128)S(1)} fusion(f32[1024,512]{0,1:T(8,128)S(1)} %fusion, f32[2,2560,512]{2,1,0:T(8,128)S(1)} %copy-done.1, f32[2,1024,2560]{1,2,0:T(8,128)} %all-gather.3.cloned.1.call-done), kind=kOutput, calls=%fused_computation.13 | convolution fusion | flops 16106651648 | bytes 19922944 | tf_op jit(solution)/shard_map/dot_general | solution.py:32
  310.4 20.1 %fusion.4 = f32[1024,512]{0,1:T(8,128)S(1)} fusion(f32[1024,512]{0,1:T(8,128)S(1)} %fusion.1, f32[2,2560,512]{2,1,0:T(8,128)S(1)} %copy-done.1, f32[2,1024,2560]{1,2,0:T(8,128)} %all-gather.3.cloned.1.call-done), kind=kOutput, calls=%fused_computation.12 | convolution fusion | flops 16106651648 | bytes 19922944 | tf_op jit(solution)/shard_map/dot_general | solution.py:29
  330.5 2.3 pad_maximum_fusion
  332.8 6.7 %all-to-all-start = ((f32[1024,8,128]{0,2,1:T(8,128)}), f32[1024,8,128]{0,2,1:T(8,128)}, u32[]{:S(2)}, u32[]{:S(2)}) async-start(f32[1024,8,128]{0,2,1:T(8,128)} %bitcast.122), calls=%async_computation | async-start | bytes 8388608 | tf_op jit(solution)/shard_map/all_to_all | solution.py:51
  339.7 0.7 fusion.18
  340.4 0.7 fusion.17
  341.1 0.7 fusion.16
  342.1 4.5 compare_select_fusion.2
  346.6 35.8 %compare_and_fusion = (pred[8192]{0:T(1024)(128)(4,1)S(1)}, s32[8192]{0:T(1024)S(1)}) fusion(s32[8192]{0:T(1024)S(1)} %multiply_reduce_fusion, pred[8192]{0:T(1024)(128)(4,1)S(1)} %compare_reduce_fusion, pred[8192]{0:T(1024)(128)(4,1)S(1)} %compare_reduce_fusion.1, pred[8192]{0:T(1024)(128)(4,1)S(1)} %compare_reduce_fusion.2, ...), kind=kLoop, calls=%fused_computation.104 | loop fusion | flops 655360 | bytes 573668 | tf_op jit(solution)/shard_map/jit(_take)/and | solution.py:55
  382.5 5.8 %all-to-all-done = f32[1024,8,128]{0,2,1:T(8,128)} async-done(((f32[1024,8,128]{0,2,1:T(8,128)}), f32[1024,8,128]{0,2,1:T(8,128)}, u32[]{:S(2)}, u32[]{:S(2)}) %all-to-all-start) | async-done | bytes 4194336 | tf_op jit(solution)/shard_map/all_to_all | solution.py:51
  388.3 5.3 %copy.17 = f32[8,1024,1,128]{3,1,0,2:T(8,128)} copy(f32[8,1024,1,128]{1,3,0,2:T(8,128)} %bitcast.75) | data formatting | bytes 8388608 | tf_op jit(solution)/shard_map/all_to_all | solution.py:51
  393.6 29.9 %gather_fusion = f32[8192,128]{1,0:T(8,128)} fusion(f32[8192,128]{1,0:T(8,128)} %bitcast.118, s32[8192]{0:T(1024)S(1)} %broadcast_clamp_fusion), kind=kCustom, calls=%fused_computation | custom fusion | bytes 8421376 | tf_op jit(solution)/shard_map/jit(_take)/gather | solution.py:55
  423.5 6.2 %bitcast_select_fusion = f32[8192,1,128]{2,0,1:T(8,128)S(1)} fusion(f32[8192,128]{1,0:T(8,128)} %gather_fusion, pred[8192]{0:T(1024)(128)(4,1)S(1)} %get-tuple-element.5), kind=kLoop, calls=%fused_computation.11 | loop fusion | flops 1048576 | bytes 8396800 | tf_op jit(solution)/shard_map/jit(_take)/select_n | solution.py:55
  429.7 60.7 %all_to_all.30 = f32[8192,1,128]{2,1,0:T(1,128)} all-to-all(f32[8192,1,128]{2,1,0:T(1,128)S(1)} %bitcast.121), channel_id=1, replica_groups=mesh['row'=8,'col'=16] {'row','col'}, dimensions={0} | all-to-all | bytes 8388608 | tf_op jit(solution)/shard_map/all_to_all | solution.py:56
  490.5 9.2 %reshape.146 = f32[64,8,16,2,64]{4,3,0,2,1:T(2,128)} reshape(f32[64,128,1,128]{3,0,1,2:T(8,128)} %bitcast.120) | data formatting | bytes 8388608 | tf_op jit(solution)/shard_map/reshape | solution.py:58
  499.6 11.4 %copy.21 = f32[64,8,16,2,64]{4,1,2,0,3:T(8,128)} copy(f32[64,8,16,2,64]{4,3,0,2,1:T(2,128)} %reshape.146) | data formatting | bytes 8388608 | tf_op jit(solution)/shard_map/reshape | solution.py:58
  511.1 7.9 %reshape.147 = f32[2,64,8192]{2,1,0:T(8,128)} reshape(f32[2,64,16,8,64]{4,3,2,1,0:T(8,128)} %bitcast.119) | data formatting | bytes 8388608 | tf_op jit(solution)/shard_map/reshape | solution.py:60
  (69 shorter events, 4.1 us)
Async XLA Ops:
  6.5 132.1 %all-gather.5.cloned.1.call-start = ((), (), s32[]{:S(2)}) async-start(), calls=%async_computation.3 | async-start | bytes 11796480 | tf_op jit(solution)/shard_map/all_gather | solution.py:39
  7.3 243.0 %all-gather.3.cloned.1.call-start = ((), (), s32[]{:S(2)}) async-start(), calls=%async_computation.2 | async-start | bytes 22282240 | tf_op jit(solution)/shard_map/all_gather | solution.py:40
  250.3 20.4 %copy-start.1 = (f32[2,2560,512]{2,1,0:T(8,128)S(1)}, f32[2,2560,512]{2,1,0:T(8,128)}, u32[]{:S(2)}) copy-start(f32[2,2560,512]{2,1,0:T(8,128)} %all-gather.5.cloned.1.call-done) | copy-start | bytes 31457284
  332.8 9.0 %copy-start = (s32[7]{0:T(128)S(1)}, s32[7]{0:T(128)}, u32[]{:S(2)}) copy-start(s32[7]{0:T(128)} %param.7) | copy-start | bytes 88
  332.8 55.5 %all-to-all-start = ((f32[1024,8,128]{0,2,1:T(8,128)}), f32[1024,8,128]{0,2,1:T(8,128)}, u32[]{:S(2)}, u32[]{:S(2)}) async-start(f32[1024,8,128]{0,2,1:T(8,128)} %bitcast.122), calls=%async_computation | async-start | bytes 8388608 | tf_op jit(solution)/shard_map/all_to_all | solution.py:51
Sparse Core Ops, SparseCore 0:
  9.7 128.9 all-gather.4
  140.3 109.8 all-gather.2
where the time goes:
time: 536 us; the launch traced here: 526 us
  waiting for transfers between devices  245 us (46%)
  matrix products  80.2 us (15%)
  local copies, waits for them, and re-layouts  66.5 us (12%)
  blocking collectives  60.7 us (11%)
  other arithmetic  53 us (10%)
  between operations  13.7 us (3%)
  starting transfers between devices  6.73 us (1%)
    all_gather x1, waiting for transfers between devices, body(): right_whole = lax.all_gather(right, 'row', axis=1, tiled=True)  126 us
    all_gather x1, waiting for transfers between devices, body(): piece = lax.all_gather(left, 'col', axis=2, tiled=True)  112 us
    all_to_all x1, blocking collectives, body(): lax.all_to_all(ordered, ('row', 'col'), split_axis=0, concat_axis=1, tile...  60.7 us
    and x1, other arithmetic, body(): ordered = jnp.take(middle, source, axis=0).reshape(total, 1, 2 * width)  35.8 us
    gather x1, local copies, waits for them, and re-layouts, body(): ordered = jnp.take(middle, source, axis=0).reshape(total, 1, 2 * width)  29.9 us
    reshape x2, local copies, waits for them, and re-layouts, body(): received = received.reshape(owned, row_count, col_count, 2, width)  20.6 us
    dot_general x1, matrix products, accumulate(): jnp.dot(left_re, right_im, preferred_element_type=jnp.float32, precision=...  20.4 us
    dot_general x1, matrix products, accumulate(): jnp.dot(left_im, right_im, preferred_element_type=jnp.float32, precision=...  20.1 us
  transfers between devices with their start and end apart: 3, of which 3 were waited for; matrix products, arithmetic and copies ran while one was open for 9% of the time, Pallas kernels for 0%

commit v1 on v0

v1 whole, which is shorter than its diff:
```python
import jax
import jax.numpy as jnp
import numpy as np
from jax import lax
from jax.sharding import Mesh
from jax.sharding import PartitionSpec as P

LOW_BITS = 7
PREFIXES = 64

ROW = ("xh", "z")
CHIPS = ("xl", "y")
CORE = "core"
COL = ("xl", "y", "core")


def inverse_owner(prefix_owner, prefixes):
    labels = jnp.arange(prefixes, dtype=jnp.int32)
    match = (prefix_owner[None, :] == labels[:, None]).astype(jnp.int32)
    return jnp.sum(match * labels[None, :], axis=1)


def inner_order(qubit_order, low_bits):
    span = 2**low_bits
    offset = jnp.arange(span, dtype=jnp.int32)
    bits = jnp.bitwise_and(jnp.right_shift(offset[:, None], qubit_order[None, :]), 1)
    powers = jnp.left_shift(jnp.ones((low_bits,), jnp.int32), jnp.arange(low_bits, dtype=jnp.int32))
    return jnp.sum(bits * powers[None, :], axis=1)


def permute_left(left, prefix_owner, qubit_order, row_count):
    _, rows, kcols = left.shape
    span = 2**LOW_BITS
    local = rows // span
    sub = span // row_count
    x = left.reshape(2, local, row_count, sub, kcols)
    x = lax.all_to_all(x, ROW, split_axis=2, concat_axis=2, tiled=True)
    x = x.reshape(2, local * row_count, sub, kcols)
    inv = inverse_owner(prefix_owner, PREFIXES)
    pick = (inv % local) * row_count + inv // local
    y = jnp.take(x, pick, axis=1)
    y = y.reshape(2, row_count, local, sub, kcols)
    y = lax.all_to_all(y, ROW, split_axis=1, concat_axis=1, tiled=True)
    y = y.reshape(2, row_count * local * sub, kcols)
    s = inner_order(qubit_order, LOW_BITS)
    o_local = jnp.arange(local, dtype=jnp.int32)
    idx = (s[None, :] // sub) * (local * sub) + o_local[:, None] * sub + s[None, :] % sub
    return jnp.take(y, idx.reshape(-1), axis=1)


def body(left, right, prefix_owner, qubit_order):
    row_count = lax.axis_size(ROW)
    col_count = lax.axis_size(COL)
    rows = left.shape[1]
    cols = right.shape[2]
    lp = permute_left(left, prefix_owner, qubit_order, row_count)
    lp = lax.all_gather(lp, CHIPS, axis=2, tiled=True)
    lp = lax.all_gather(lp, CORE, axis=2, tiled=True)
    depth = right.shape[1]
    halves = lax.axis_size(CORE)
    rr = right.reshape(2, halves, depth // halves, cols)
    rr = lax.all_gather(rr, ROW, axis=2, tiled=True)
    rr = rr.reshape(2, -1, cols)
    high = lax.Precision.HIGH
    dot = lambda a, b: jnp.dot(a, b, preferred_element_type=jnp.float32, precision=high)
    t1 = dot(lp[0], rr[0])
    t2 = dot(lp[1], rr[1])
    t3 = dot(lp[0] + lp[1], rr[0] + rr[1])
    tile = jnp.stack([t1 - t2, t3 - t1 - t2], axis=0)
    tile = tile.reshape(2, col_count, rows // col_count, cols)
    out = lax.all_to_all(tile, COL, split_axis=1, concat_axis=3, tiled=True)
    return out.reshape(2, rows // col_count, col_count * cols)


def solution(mesh):
    devices = np.asarray(mesh.devices)
    nr, nc = devices.shape
    fine = Mesh(devices.reshape(2, nr // 2, 2, nc // 4, 2), ("xh", "z", "xl", "y", "core"))
    in_specs = (P(None, ROW, COL), P(None, ROW, COL), P(), P())
    out_specs = P(None, ROW + COL, None)
    return jax.shard_map(body, mesh=fine, in_specs=in_specs, out_specs=out_specs, check_vma=False)
```

time: 536 us -> 521 us (0.972); the launches traced: 526 us -> 520 us
  waiting for transfers between devices: 245 us -> 317 us
  matrix products: 80.2 us -> 40.6 us
  local copies, waits for them, and re-layouts: 66.5 us -> 30.5 us
  starting transfers between devices: 6.73 us -> 13.6 us
  blocking collectives: 60.7 us -> 54.4 us
    all_to_all x1 -> x2, waiting for transfers between devices: 5.8 us -> 51.7 us  [the longest x1 25.9 us: permute_left(): y = lax.all_to_all(y, ROW, split_axis=1, concat_axis=1, tiled=True)]
    add x0 -> x3, other arithmetic: none -> 44.1 us  [the longest x2 44 us: body(): t3 = dot(lp[0] + lp[1], rr[0] + rr[1])]
    dot_general x4 -> x3, matrix products: 80.2 us -> 40.6 us  [body(): jnp.dot(a, b, preferred_element_type=jnp.float32, precision=high)]
    and x1 -> x2, other arithmetic: 35.8 us -> 0.1 us  [the longest x1 0.08 us: permute_left(): return jnp.take(y, idx.reshape(-1), axis=1)]
    all_gather x2 -> x3, waiting for transfers between devices: 238 us -> 264 us  [the longest x1 127 us: body(): rr = lax.all_gather(rr, ROW, axis=2, tiled=True)]
    gather x5 -> x2, local copies, waits for them, and re-layouts: 32.8 us -> 8.02 us  [the longest x1 5.75 us: permute_left(): return jnp.take(y, idx.reshape(-1), axis=1)]
    reshape x3, local copies, waits for them, and re-layouts: 28.5 us -> 9.43 us  [the longest x1 4.94 us: body(): return out.reshape(2, rows // col_count, col_count * cols)]
    gather x59 -> x2, other arithmetic: 7.61 us -> 0.01 us  [the longest x1 0.01 us: permute_left(): return jnp.take(y, idx.reshape(-1), axis=1)]
  transfers between devices with their start and end apart: 3 -> 5, of which waited for: 3 -> 5; matrix products, arithmetic and copies ran while one was open for 9% -> 2% of each run, Pallas kernels for 0% -> 0%
where the time goes in v1:
time: 521 us; the launch traced here: 520 us
  waiting for transfers between devices  317 us (61%)
  blocking collectives  54.4 us (10%)
  other arithmetic  50.9 us (10%)
  matrix products  40.6 us (8%)
  local copies, waits for them, and re-layouts  30.5 us (6%)
  starting transfers between devices  13.6 us (3%)
  between operations  13.3 us (3%)
    all_gather x1, waiting for transfers between devices, body(): rr = lax.all_gather(rr, ROW, axis=2, tiled=True)  127 us
    all_gather x1, waiting for transfers between devices, body(): lp = lax.all_gather(lp, CHIPS, axis=2, tiled=True)  111 us
    all_to_all x1, blocking collectives, body(): out = lax.all_to_all(tile, COL, split_axis=1, concat_axis=3, tiled=True)  54.4 us
    add x2, other arithmetic, body(): t3 = dot(lp[0] + lp[1], rr[0] + rr[1])  44 us
    dot_general x3, matrix products, body(): jnp.dot(a, b, preferred_element_type=jnp.float32, precision=high)  40.6 us
    all_gather x1, waiting for transfers between devices, body(): lp = lax.all_gather(lp, CORE, axis=2, tiled=True)  26.8 us
    all_to_all x1, waiting for transfers between devices, permute_left(): y = lax.all_to_all(y, ROW, split_axis=1, concat_axis=1, tiled=True)  25.9 us
    all_to_all x1, waiting for transfers between devices, permute_left(): x = lax.all_to_all(x, ROW, split_axis=2, concat_axis=2, tiled=True)  25.8 us
  transfers between devices with their start and end apart: 5, of which 5 were waited for; matrix products, arithmetic and copies ran while one was open for 2% of the time, Pallas kernels for 0%

profile of v1, /device:TPU:1, one launch (start us, length us, event | category | flops | bytes accessed | tf_op | source)
XLA Modules:
  0.0 520.3 jit_solution(5980896625807978667)
XLA Ops:
  6.5 1.8 copy.39
  8.3 1.6 copy.40
  9.9 8.3 %all-to-all-start = ((f32[2,8,8,16,160]{4,3,1,0,2:T(8,128)}), f32[2,8,8,16,160]{4,3,1,0,2:T(8,128)S(1)}, u32[]{:S(2)}, u32[]{:S(2)}) async-start(f32[2,8,8,16,160]{4,3,1,0,2:T(8,128)} %copy.40), calls=%async_computation | async-start | bytes 4194304 | tf_op jit(solution)/shard_map/all_to_all | solution.py:37
  18.6 25.8 %all-to-all-done = f32[2,8,8,16,160]{4,3,1,0,2:T(8,128)S(1)} async-done(((f32[2,8,8,16,160]{4,3,1,0,2:T(8,128)}), f32[2,8,8,16,160]{4,3,1,0,2:T(8,128)S(1)}, u32[]{:S(2)}, u32[]{:S(2)}) %all-to-all-start) | async-done | bytes 1310752 | tf_op jit(solution)/shard_map/all_to_all | solution.py:37
  44.4 1.6 copy.41
  45.9 2.3 gather_fusion
  48.2 1.5 copy_select_fusion
  49.7 5.2 %all-to-all-start.1 = ((f32[2,8,8,16,160]{4,3,2,0,1:T(8,128)}), f32[2,8,8,16,160]{4,3,2,0,1:T(8,128)S(1)}, u32[]{:S(2)}, u32[]{:S(2)}) async-start(f32[2,8,8,16,160]{4,3,2,0,1:T(8,128)} %copy_select_fusion), calls=%async_computation.1 | async-start | bytes 4194304 | tf_op jit(solution)/shard_map/all_to_all | solution.py:43
  55.2 25.9 %all-to-all-done.1 = f32[2,8,8,16,160]{4,3,2,0,1:T(8,128)S(1)} async-done(((f32[2,8,8,16,160]{4,3,2,0,1:T(8,128)}), f32[2,8,8,16,160]{4,3,2,0,1:T(8,128)S(1)}, u32[]{:S(2)}, u32[]{:S(2)}) %all-to-all-start.1) | async-done | bytes 1310752 | tf_op jit(solution)/shard_map/all_to_all | solution.py:43
  81.4 2.9 copy.44
  84.3 5.8 %gather_fusion.1 = f32[1024,2,160]{2,1,0:T(2,128)S(1)} fusion(f32[2,1024,160]{2,0,1:T(2,128)} %copy.44, s32[1024]{0:T(1024)S(1)} %broadcast_clamp_fusion), kind=kCustom, calls=%fused_computation.1 | custom fusion | bytes 2625536 | tf_op jit(solution)/shard_map/jit(_take)/gather | solution.py:48
  90.1 4.5 select_bitcast_fusion
  94.5 5.0 copy.45
  100.3 110.8 %all-gather.4.cloned.1.call-done = f32[2,1024,1280]{1,0,2:T(2,128)} async-done(((f32[2,1024,160]{1,0,2:T(2,128)}), f32[2,1024,1280]{1,0,2:T(2,128)}) %all-gather.4.cloned.1.call-update) | async-done | bytes 10485776 | tf_op jit(solution)/shard_map/all_gather | solution.py:57
  211.2 126.9 %all-gather.8.cloned.1.call-done = f32[2,2,1280,512]{3,2,1,0:T(8,128)} async-done(((f32[2,2,160,512]{3,2,1,0:T(8,128)}), f32[2,2,1280,512]{3,2,1,0:T(8,128)}) %all-gather.8.cloned.1.call-update) | async-done | bytes 10485776 | tf_op jit(solution)/shard_map/all_gather | solution.py:62
  338.1 12.1 %slice_add_fusion = (f32[1,2,1280,512]{3,2,1,0:T(8,128)}, f32[1,2,1280,512]{3,2,1,0:T(8,128)}, f32[1,2,1280,512]{3,2,1,0:T(8,128)}) fusion(f32[2,2,1280,512]{3,2,1,0:T(8,128)} %all-gather.8.cloned.1.call-done), kind=kLoop, calls=%fused_computation.56 | loop fusion | flops 1310720 | bytes 26214400 | tf_op jit(solution)/shard_map/add | solution.py:68
  350.2 26.8 %all-gather.6.cloned.1.call-done = f32[2,1024,2560]{1,0,2:T(2,128)} async-done(((f32[2,1024,1280]{1,0,2:T(2,128)}), f32[2,1024,2560]{1,0,2:T(2,128)}) %all-gather.6.cloned.1.call-update) | async-done | bytes 20971536 | tf_op jit(solution)/shard_map/all_gather | solution.py:58
  376.9 31.9 %slice_add_fusion.1 = (f32[1,1024,2560]{1,0,2:T(1,128)}, f32[1,1024,2560]{1,0,2:T(1,128)}, f32[1,1024,2560]{1,0,2:T(1,128)}) fusion(f32[2,1024,2560]{1,0,2:T(2,128)} %all-gather.6.cloned.1.call-done), kind=kLoop, calls=%fused_computation.57 | loop fusion | flops 2621440 | bytes 52428800 | tf_op jit(solution)/shard_map/add | solution.py:68
  408.9 15.5 %fusion.3 = f32[1024,512]{1,0:T(8,128)} fusion(f32[2560,512]{1,0:T(8,128)} %bitcast.74, f32[1,1024,2560]{1,0,2:T(1,128)} %get-tuple-element.6), kind=kOutput, calls=%fused_computation.5 | convolution fusion | flops 8053063680 | bytes 17825792 | tf_op jit(solution)/shard_map/dot_general | solution.py:65
  424.4 11.8 %fusion.21 = (f32[1024,512]{1,0:T(8,128)S(1)}, f32[1024,512]{1,0:T(8,128)}) fusion(f32[1024,512]{1,0:T(8,128)} %fusion.3, f32[2560,512]{1,0:T(8,128)S(1)} %bitcast.64, f32[1,1024,2560]{1,0,2:T(1,128)S(1)} %copy-done), kind=kOutput, calls=%fused_computation.58 | convolution fusion | flops 8053587968 | bytes 22020096 | tf_op jit(solution)/shard_map/dot_general | solution.py:65
  436.2 13.4 %subtract_subtract_fusion = f32[1024,512]{1,0:T(8,128)S(1)} fusion(f32[1024,512]{1,0:T(8,128)} %fusion.3, f32[1024,512]{1,0:T(8,128)} %get-tuple-element.14, f32[2560,512]{1,0:T(8,128)S(1)} %bitcast.73, f32[1,1024,2560]{1,0,2:T(1,128)} %get-tuple-element.5), kind=kOutput, calls=%fused_computation.14 | convolution fusion | flops 8054112256 | bytes 22020096 | tf_op jit(solution)/shard_map/dot_general | solution.py:65
  450.0 54.4 %all_to_all.25 = f32[2,16,64,512]{3,2,0,1:T(8,128)S(1)} all-to-all(f32[2,16,64,512]{3,2,0,1:T(8,128)S(1)} %pad_maximum_fusion), channel_id=1, replica_groups=mesh['xh'=2,'z'=4,'xl'=2,'y'=4,'core'=2] {'xl','y','core'}, dimensions={1} | all-to-all | bytes 8388608 | tf_op jit(solution)/shard_map/all_to_all | solution.py:71
  504.5 4.4 copy.48
  508.9 4.9 reshape.245
  (34 shorter events, 2.1 us)
Async XLA Ops:
  8.3 9.9 %copy-start.2 = (s32[64]{0:T(128)S(1)}, s32[64]{0:T(128)}, u32[]{:S(2)}) copy-start(s32[64]{0:T(128)} %param.6) | copy-start | bytes 772
  8.3 10.1 %copy-start.3 = (s32[7]{0:T(128)S(1)}, s32[7]{0:T(128)}, u32[]{:S(2)}) copy-start(s32[7]{0:T(128)} %param.7) | copy-start | bytes 88
  9.9 34.5 %all-to-all-start = ((f32[2,8,8,16,160]{4,3,1,0,2:T(8,128)}), f32[2,8,8,16,160]{4,3,1,0,2:T(8,128)S(1)}, u32[]{:S(2)}, u32[]{:S(2)}) async-start(f32[2,8,8,16,160]{4,3,1,0,2:T(8,128)} %copy.40), calls=%async_computation | async-start | bytes 4194304 | tf_op jit(solution)/shard_map/all_to_all | solution.py:37
  49.7 31.4 %all-to-all-start.1 = ((f32[2,8,8,16,160]{4,3,2,0,1:T(8,128)}), f32[2,8,8,16,160]{4,3,2,0,1:T(8,128)S(1)}, u32[]{:S(2)}, u32[]{:S(2)}) async-start(f32[2,8,8,16,160]{4,3,2,0,1:T(8,128)} %copy_select_fusion), calls=%async_computation.1 | async-start | bytes 4194304 | tf_op jit(solution)/shard_map/all_to_all | solution.py:43
  55.0 156.2 %all-gather.4.cloned.1.call-start = ((), (), s32[]{:S(2)}) async-start(), calls=%async_computation.3 | async-start | bytes 11796480 | tf_op jit(solution)/shard_map/all_gather | solution.py:57
  99.5 238.5 %all-gather.8.cloned.1.call-start = ((), (), s32[]{:S(2)}) async-start(), calls=%async_computation.5 | async-start | bytes 11796480 | tf_op jit(solution)/shard_map/all_gather | solution.py:62
  100.3 276.6 %all-gather.6.cloned.1.call-start = ((), (), s32[]{:S(2)}) async-start(), calls=%async_computation.4 | async-start | bytes 31457280 | tf_op jit(solution)/shard_map/all_gather | solution.py:58
  408.9 15.5 %copy-start = (f32[1,1024,2560]{1,0,2:T(1,128)S(1)}, f32[1,1024,2560]{1,0,2:T(1,128)}, u32[]{:S(2)}) copy-start(f32[1,1024,2560]{1,0,2:T(1,128)} %get-tuple-element.7) | copy-start | bytes 31457284
  408.9 15.5 %copy-start.1 = (f32[1,2,1280,512]{3,2,1,0:T(8,128)S(1)}, f32[1,2,1280,512]{3,2,1,0:T(8,128)}, u32[]{:S(2)}) copy-start(f32[1,2,1280,512]{3,2,1,0:T(8,128)} %get-tuple-element.10) | copy-start | bytes 15728644
  408.9 27.3 %slice-start = ((s8[5242880]{0:T(1024)(128)(4,1)}), s8[4194304]{0:T(1024)(128)(4,1)S(1)}, s32[]{:S(2)}) async-start(s8[5242880]{0:T(1024)(128)(4,1)} %bitcast.71), calls=%async_computation.6 | async-start | bytes 8388608
  424.4 11.8 %slice-start.1 = ((s8[5242880]{0:T(1024)(128)(4,1)}), s8[1048576]{0:T(1024)(128)(4,1)S(1)}, s32[]{:S(2)}) async-start(s8[5242880]{0:T(1024)(128)(4,1)} %bitcast.71), calls=%async_computation.7 | async-start | bytes 2097152
Sparse Core Ops, SparseCore 0:
  99.7 111.4 all-gather.3
  213.5 124.5 all-gather.7
  339.7 37.1 all-gather.5

commit v2 on v1

--- a/solution.py
+++ b/solution.py
@@ -1,7 +1,11 @@
+import functools
+
 import jax
 import jax.numpy as jnp
 import numpy as np
 from jax import lax
+from jax.experimental import pallas as pl
+from jax.experimental.pallas import tpu as pltpu
 from jax.sharding import Mesh
 from jax.sharding import PartitionSpec as P
 
@@ -48,24 +52,93 @@
     return jnp.take(y, idx.reshape(-1), axis=1)
 
 
+MESH_ID = pl.DeviceIdType.MESH
+
+
+def gather_kernel(nrow, ncol, lt_ref, rt_ref, lall_ref, rall_ref, lsend, lrecv, rsend, rrecv, own):
+    xh, z = lax.axis_index("xh"), lax.axis_index("z")
+    xl, y, core = lax.axis_index("xl"), lax.axis_index("y"), lax.axis_index("core")
+    zs, ys = nrow // 2, ncol // 4
+    me_r = xh * zs + z
+    me_c = (xl * ys + y) * 2 + core
+    kl = lt_ref.shape[1]
+    kr = rt_ref.shape[1]
+
+    def col_dev(j):
+        return (xh, z, j // (ys * 2), (j // 2) % ys, j % 2)
+
+    def row_dev(j):
+        return (j // zs, j % zs, xl, y, core)
+
+    barrier = pltpu.get_barrier_semaphore()
+    for off in range(1, ncol):
+        pl.semaphore_signal(barrier, 1, device_id=col_dev((me_c + off) % ncol), device_id_type=MESH_ID)
+    for off in range(1, nrow):
+        pl.semaphore_signal(barrier, 1, device_id=row_dev((me_r + off) % nrow), device_id_type=MESH_ID)
+    pl.semaphore_wait(barrier, ncol - 1 + nrow - 1)
+
+    lwin = lall_ref.at[:, pl.ds(pl.multiple_of(me_c * kl, 8), kl), :]
+    rwin = rall_ref.at[:, pl.ds(pl.multiple_of(me_r * kr, 8), kr), :]
+    local_l = pltpu.make_async_copy(lt_ref, lwin, own.at[0])
+    local_r = pltpu.make_async_copy(rt_ref, rwin, own.at[1])
+    local_l.start()
+    local_r.start()
+    copies = []
+    for off in range(1, max(ncol, nrow)):
+        if off < ncol:
+            c = pltpu.make_async_remote_copy(
+                lt_ref, lwin, lsend.at[off], lrecv.at[off],
+                device_id=col_dev((me_c + off) % ncol), device_id_type=MESH_ID)
+            c.start()
+            copies.append(c)
+        if off < nrow:
+            c = pltpu.make_async_remote_copy(
+                rt_ref, rwin, rsend.at[off], rrecv.at[off],
+                device_id=row_dev((me_r + off) % nrow), device_id_type=MESH_ID)
+            c.start()
+            copies.append(c)
+    local_l.wait()
+    local_r.wait()
+    for c in copies:
+        c.wait()
+
+
+def gather_operands(lt, rt, nrow, ncol):
+    b, kl, m = lt.shape
+    _, kr, n = rt.shape
+    return pl.pallas_call(
+        functools.partial(gather_kernel, nrow, ncol),
+        out_shape=(
+            jax.ShapeDtypeStruct((b, kl * ncol, m), lt.dtype),
+            jax.ShapeDtypeStruct((b, kr * nrow, n), rt.dtype),
+        ),
+        in_specs=[pl.BlockSpec(memory_space=pl.ANY)] * 2,
+        out_specs=[pl.BlockSpec(memory_space=pl.ANY)] * 2,
+        scratch_shapes=[
+            pltpu.SemaphoreType.DMA((ncol,)),
+            pltpu.SemaphoreType.DMA((ncol,)),
+            pltpu.SemaphoreType.DMA((nrow,)),
+            pltpu.SemaphoreType.DMA((nrow,)),
+            pltpu.SemaphoreType.DMA((2,)),
+        ],
+        compiler_params=pltpu.CompilerParams(collective_id=0, has_side_effects=True),
+    )(lt, rt)
+
+
 def body(left, right, prefix_owner, qubit_order):
     row_count = lax.axis_size(ROW)
     col_count = lax.axis_size(COL)
     rows = left.shape[1]
     cols = right.shape[2]
     lp = permute_left(left, prefix_owner, qubit_order, row_count)
-    lp = lax.all_gather(lp, CHIPS, axis=2, tiled=True)
-    lp = lax.all_gather(lp, CORE, axis=2, tiled=True)
-    depth = right.shape[1]
-    halves = lax.axis_size(CORE)
-    rr = right.reshape(2, halves, depth // halves, cols)
-    rr = lax.all_gather(rr, ROW, axis=2, tiled=True)
-    rr = rr.reshape(2, -1, cols)
+    lt = jnp.swapaxes(lp, 1, 2)
+    lall, rall = gather_operands(lt, right, row_count, col_count)
     high = lax.Precision.HIGH
-    dot = lambda a, b: jnp.dot(a, b, preferred_element_type=jnp.float32, precision=high)
-    t1 = dot(lp[0], rr[0])
-    t2 = dot(lp[1], rr[1])
-    t3 = dot(lp[0] + lp[1], rr[0] + rr[1])
+    dims = (((0,), (0,)), ((), ()))
+    dot = lambda a, b: lax.dot_general(a, b, dims, preferred_element_type=jnp.float32, precision=high)
+    t1 = dot(lall[0], rall[0])
+    t2 = dot(lall[1], rall[1])
+    t3 = dot(lall[0] + lall[1], rall[0] + rall[1])
     tile = jnp.stack([t1 - t2, t3 - t1 - t2], axis=0)
     tile = tile.reshape(2, col_count, rows // col_count, cols)
     out = lax.all_to_all(tile, COL, split_axis=1, concat_axis=3, tiled=True)

time: 521 us -> 692 us (1.33)
  the two profiles are of different devices: /device:TPU:1 before, /device:TPU:96 now
where the time goes in v2:
time: 692 us; the launch traced here: 691 us
  Pallas kernels  487 us (70%)
  blocking collectives  60.7 us (9%)
  waiting for transfers between devices  52 us (8%)
  matrix products  43.7 us (6%)
  local copies, waits for them, and re-layouts  29.9 us (4%)
  starting transfers between devices  12.1 us (2%)
    pallas_call x1, Pallas kernels, gather_operands(): pl.pallas_call(functools.partial(gather_kernel, nrow, ncol), out_shape=(j...  487 us
    all_to_all x1, blocking collectives, body(): out = lax.all_to_all(tile, COL, split_axis=1, concat_axis=3, tiled=True)  60.7 us
    dot_general x3, matrix products, body(): lax.dot_general(a, b, dims, preferred_element_type=jnp.float32, precision...  43.7 us
    all_to_all x1, waiting for transfers between devices, permute_left(): y = lax.all_to_all(y, ROW, split_axis=1, concat_axis=1, tiled=True)  26.2 us
    all_to_all x1, waiting for transfers between devices, permute_left(): x = lax.all_to_all(x, ROW, split_axis=2, concat_axis=2, tiled=True)  25.8 us
  transfers between devices with their start and end apart: 2, of which 2 were waited for; matrix products, arithmetic and copies ran while one was open for 0% of the time, Pallas kernels for 0%

profile of v2, /device:TPU:96, one launch (start us, length us, event | category | flops | bytes accessed | tf_op | source)
XLA Modules:
  0.0 691.2 jit_solution(10449516040291566306)
XLA Ops:
  0.0 1.8 copy.30
  1.8 1.6 copy.31
  3.4 7.1 %all-to-all-start = ((f32[2,8,8,16,160]{4,3,1,0,2:T(8,128)}), f32[2,8,8,16,160]{4,3,1,0,2:T(8,128)S(1)}, u32[]{:S(2)}, u32[]{:S(2)}) async-start(f32[2,8,8,16,160]{4,3,1,0,2:T(8,128)} %copy.31), calls=%async_computation | async-start | bytes 4194304 | tf_op jit(solution)/shard_map/all_to_all | solution.py:41
  10.5 0.1 select_reduce_fusion
  10.7 0.1 multiply_reduce_fusion
  10.8 25.8 %all-to-all-done = f32[2,8,8,16,160]{4,3,1,0,2:T(8,128)S(1)} async-done(((f32[2,8,8,16,160]{4,3,1,0,2:T(8,128)}), f32[2,8,8,16,160]{4,3,1,0,2:T(8,128)S(1)}, u32[]{:S(2)}, u32[]{:S(2)}) %all-to-all-start) | async-done | bytes 1310752 | tf_op jit(solution)/shard_map/all_to_all | solution.py:41
  36.7 1.6 copy.32
  38.2 2.3 gather_fusion
  40.5 1.5 copy_select_fusion
  42.0 5.0 all-to-all-start.1
  47.2 26.2 %all-to-all-done.1 = f32[2,8,8,16,160]{4,3,2,0,1:T(8,128)S(1)} async-done(((f32[2,8,8,16,160]{4,3,2,0,1:T(8,128)}), f32[2,8,8,16,160]{4,3,2,0,1:T(8,128)S(1)}, u32[]{:S(2)}, u32[]{:S(2)}) %all-to-all-start.1) | async-done | bytes 1310752 | tf_op jit(solution)/shard_map/all_to_all | solution.py:47
  73.4 0.2 copy.34
  73.6 1.6 copy.35
  75.2 8.8 %gather_fusion.1 = f32[1024,2,160]{2,1,0:T(2,128)} fusion(f32[2,1024,160]{2,0,1:T(2,128)S(1)} %copy.35, s32[1024]{0:T(1024)S(1)} %broadcast_clamp_fusion), kind=kCustom, calls=%fused_computation.1 | custom fusion | bytes 2625536 | tf_op jit(solution)/shard_map/jit(_take)/gather | solution.py:52
  84.1 2.7 copy.36
  86.8 1.2 select_bitcast_fusion.lt_ref
  87.9 487.4 %shard_map.46 = (f32[2,2560,1024]{2,1,0:T(8,128)}, f32[2,2560,512]{2,1,0:T(8,128)}) custom-call(f32[2,160,1024]{2,1,0:T(8,128)} %select_bitcast_fusion.lt_ref, f32[2,320,512]{2,1,0:T(8,128)} %rt_ref.1), custom_call_target="tpu_custom_call" | custom-call | tf_op jit(solution)/shard_map/pallas_call | solution.py:109
  575.3 12.1 %fusion.2 = f32[1024,512]{1,0:T(8,128)S(1)} fusion(f32[2,2560,1024]{2,1,0:T(8,128)} %get-tuple-element.7, f32[2,2560,512]{2,1,0:T(8,128)} %get-tuple-element.8), kind=kOutput, calls=%fused_computation.4 | convolution fusion | flops 8053063680 | bytes 17825792 | tf_op jit(solution)/shard_map/dot_general | solution.py:138
  587.4 12.6 %fusion.33 = (f32[1024,512]{1,0:T(8,128)S(1)}, f32[1024,512]{1,0:T(8,128)}) fusion(f32[1024,512]{1,0:T(8,128)S(1)} %fusion.2, f32[2,2560,512]{2,1,0:T(8,128)S(1)} %copy-done, f32[2,2560,1024]{2,1,0:T(8,128)} %get-tuple-element.7), kind=kOutput, calls=%fused_computation.66 | convolution fusion | flops 8053587968 | bytes 22020096 | tf_op jit(solution)/shard_map/dot_general | solution.py:138
  600.1 19.0 %subtract_subtract_fusion = f32[1024,512]{1,0:T(8,128)} fusion(f32[1024,512]{1,0:T(8,128)S(1)} %fusion.2, f32[1024,512]{1,0:T(8,128)} %get-tuple-element.12, f32[2,2560,512]{2,1,0:T(8,128)} %get-tuple-element.8, f32[2,2560,1024]{2,1,0:T(8,128)} %get-tuple-element.7), kind=kOutput, calls=%fused_computation.23 | convolution fusion | flops 8058044416 | bytes 37748736 | tf_op jit(solution)/shard_map/dot_general | solution.py:138
  619.1 2.1 pad_maximum_fusion
  621.2 60.7 %all_to_all.25 = f32[2,16,64,512]{3,2,0,1:T(8,128)S(1)} all-to-all(f32[2,16,64,512]{3,2,0,1:T(8,128)S(1)} %pad_maximum_fusion), channel_id=1, replica_groups=mesh['xh'=2,'z'=4,'xl'=2,'y'=4,'core'=2] {'xl','y','core'}, dimensions={1} | all-to-all | bytes 8388608 | tf_op jit(solution)/shard_map/all_to_all | solution.py:144
  681.9 4.4 copy.39
  686.3 4.9 reshape.236
  (17 shorter events, 0.3 us)
Async XLA Ops:
  3.4 7.1 %copy-start.1 = (s32[64]{0:T(128)S(1)}, s32[64]{0:T(128)}, u32[]{:S(2)}) copy-start(s32[64]{0:T(128)} %param.6) | copy-start | bytes 772
  3.4 7.3 %copy-start.2 = (s32[7]{0:T(128)S(1)}, s32[7]{0:T(128)}, u32[]{:S(2)}) copy-start(s32[7]{0:T(128)} %param.7) | copy-start | bytes 88
  3.4 33.3 %all-to-all-start = ((f32[2,8,8,16,160]{4,3,1,0,2:T(8,128)}), f32[2,8,8,16,160]{4,3,1,0,2:T(8,128)S(1)}, u32[]{:S(2)}, u32[]{:S(2)}) async-start(f32[2,8,8,16,160]{4,3,1,0,2:T(8,128)} %copy.31), calls=%async_computation | async-start | bytes 4194304 | tf_op jit(solution)/shard_map/all_to_all | solution.py:41
  42.0 31.4 %all-to-all-start.1 = ((f32[2,8,8,16,160]{4,3,2,0,1:T(8,128)}), f32[2,8,8,16,160]{4,3,2,0,1:T(8,128)S(1)}, u32[]{:S(2)}, u32[]{:S(2)}) async-start(f32[2,8,8,16,160]{4,3,2,0,1:T(8,128)} %copy_select_fusion), calls=%async_computation.1 | async-start | bytes 4194304 | tf_op jit(solution)/shard_map/all_to_all | solution.py:47
  575.3 12.1 %copy-start = (f32[2,2560,512]{2,1,0:T(8,128)S(1)}, f32[2,2560,512]{2,1,0:T(8,128)}, u32[]{:S(2)}) copy-start(f32[2,2560,512]{2,1,0:T(8,128)} %get-tuple-element.8) | copy-start | bytes 31457284

commit v3 on v1

--- a/solution.py
+++ b/solution.py
@@ -53,22 +53,27 @@
     col_count = lax.axis_size(COL)
     rows = left.shape[1]
     cols = right.shape[2]
+    chunks = 4
+    width = cols // chunks
+    rparts = [right[:, :, j * width:(j + 1) * width] for j in range(chunks)]
+    first = lax.all_gather(rparts[0], ROW, axis=1, tiled=True)
     lp = permute_left(left, prefix_owner, qubit_order, row_count)
-    lp = lax.all_gather(lp, CHIPS, axis=2, tiled=True)
-    lp = lax.all_gather(lp, CORE, axis=2, tiled=True)
-    depth = right.shape[1]
-    halves = lax.axis_size(CORE)
-    rr = right.reshape(2, halves, depth // halves, cols)
-    rr = lax.all_gather(rr, ROW, axis=2, tiled=True)
-    rr = rr.reshape(2, -1, cols)
+    lall = lax.all_gather(lp, COL, axis=2, tiled=True)
+    rest = lax.optimization_barrier((lall, rparts[1:]))[1]
+    gathered = [first] + [lax.all_gather(r, ROW, axis=1, tiled=True) for r in rest]
+    lsum = lall[0] + lall[1]
     high = lax.Precision.HIGH
     dot = lambda a, b: jnp.dot(a, b, preferred_element_type=jnp.float32, precision=high)
-    t1 = dot(lp[0], rr[0])
-    t2 = dot(lp[1], rr[1])
-    t3 = dot(lp[0] + lp[1], rr[0] + rr[1])
-    tile = jnp.stack([t1 - t2, t3 - t1 - t2], axis=0)
-    tile = tile.reshape(2, col_count, rows // col_count, cols)
-    out = lax.all_to_all(tile, COL, split_axis=1, concat_axis=3, tiled=True)
+    outs = []
+    for rall in gathered:
+        t1 = dot(lall[0], rall[0])
+        t2 = dot(lall[1], rall[1])
+        t3 = dot(lsum, rall[0] + rall[1])
+        tile = jnp.stack([t1 - t2, t3 - t1 - t2], axis=0)
+        tile = tile.reshape(2, col_count, rows // col_count, width)
+        outs.append(lax.all_to_all(tile, COL, split_axis=1, concat_axis=1, tiled=True))
+    out = jnp.stack(outs, axis=3)
+    out = jnp.transpose(out, (0, 2, 1, 3, 4))
     return out.reshape(2, rows // col_count, col_count * cols)
 
 

time: 521 us -> 549 us (1.054); the launches traced: 520 us -> 540 us
  matrix products: 40.6 us -> 144 us
  waiting for transfers between devices: 317 us -> 254 us
  blocking collectives: 54.4 us -> 21.3 us
  starting transfers between devices: 13.6 us -> 30.6 us
  other arithmetic: 50.9 us -> 43.4 us
    dot_general x3 -> x12, matrix products: 40.6 us -> 144 us  [body(): jnp.dot(a, b, preferred_element_type=jnp.float32, precision=high)]
    all_gather x3 -> x5, waiting for transfers between devices: 264 us -> 201 us  [the longest x1 111 us: body(): lall = lax.all_gather(lp, COL, axis=2, tiled=True)]
    all_to_all x1, blocking collectives: 54.4 us -> 21.3 us  [body(): lax.all_to_all(tile, COL, split_axis=1, concat_axis=1, tiled=True)]
    all_to_all x0 -> x3, starting transfers between devices: none -> 16.8 us  [body(): lax.all_to_all(tile, COL, split_axis=1, concat_axis=1, tiled=True)]
    add x2 -> x1, other arithmetic: 44 us -> 31.8 us  [body(): lsum = lall[0] + lall[1]]
  transfers between devices with their start and end apart: 5 -> 10, of which waited for: 5 -> 7; matrix products, arithmetic and copies ran while one was open for 2% -> 34% of each run, Pallas kernels for 0% -> 0%
where the time goes in v3:
time: 549 us; the launch traced here: 540 us
  waiting for transfers between devices  254 us (46%)
  matrix products  144 us (26%)
  other arithmetic  43.4 us (8%)
  local copies, waits for them, and re-layouts  32.7 us (6%)
  starting transfers between devices  30.6 us (6%)
  blocking collectives  21.3 us (4%)
  between operations  14 us (3%)
    dot_general x12, matrix products, body(): jnp.dot(a, b, preferred_element_type=jnp.float32, precision=high)  144 us
    all_gather x1, waiting for transfers between devices, body(): lall = lax.all_gather(lp, COL, axis=2, tiled=True)  111 us
    all_gather x3, waiting for transfers between devices, body(): lax.all_gather(r, ROW, axis=1, tiled=True)  62.2 us
    add x1, other arithmetic, body(): lsum = lall[0] + lall[1]  31.8 us
    all_gather x1, waiting for transfers between devices, body(): first = lax.all_gather(rparts[0], ROW, axis=1, tiled=True)  28 us
    all_to_all x1, waiting for transfers between devices, permute_left(): y = lax.all_to_all(y, ROW, split_axis=1, concat_axis=1, tiled=True)  25.9 us
    all_to_all x1, waiting for transfers between devices, permute_left(): x = lax.all_to_all(x, ROW, split_axis=2, concat_axis=2, tiled=True)  25.8 us
    all_to_all x1, blocking collectives, body(): lax.all_to_all(tile, COL, split_axis=1, concat_axis=1, tiled=True)  21.3 us
  transfers between devices with their start and end apart: 10, of which 7 were waited for; matrix products, arithmetic and copies ran while one was open for 34% of the time, Pallas kernels for 0%

profile of v3, /device:TPU:1, one launch (start us, length us, event | category | flops | bytes accessed | tf_op | source)
XLA Modules:
  0.0 539.8 jit_solution(8104803770422307146)
XLA Ops:
  9.9 8.5 %all-to-all-start = ((f32[2,8,8,16,160]{4,3,1,0,2:T(8,128)}), f32[2,8,8,16,160]{4,3,1,0,2:T(8,128)S(1)}, u32[]{:S(2)}, u32[]{:S(2)}) async-start(f32[2,8,8,16,160]{4,3,1,0,2:T(8,128)} %copy.42), calls=%async_computation | async-start | bytes 4194304 | tf_op jit(solution)/shard_map/all_to_all | solution.py:37
  18.7 25.8 %all-to-all-done = f32[2,8,8,16,160]{4,3,1,0,2:T(8,128)S(1)} async-done(((f32[2,8,8,16,160]{4,3,1,0,2:T(8,128)}), f32[2,8,8,16,160]{4,3,1,0,2:T(8,128)S(1)}, u32[]{:S(2)}, u32[]{:S(2)}) %all-to-all-start) | async-done | bytes 1310752 | tf_op jit(solution)/shard_map/all_to_all | solution.py:37
  55.3 25.9 %all-to-all-done.1 = f32[2,8,8,16,160]{4,3,2,0,1:T(8,128)S(1)} async-done(((f32[2,8,8,16,160]{4,3,2,0,1:T(8,128)}), f32[2,8,8,16,160]{4,3,2,0,1:T(8,128)S(1)}, u32[]{:S(2)}, u32[]{:S(2)}) %all-to-all-start.1) | async-done | bytes 1310752 | tf_op jit(solution)/shard_map/all_to_all | solution.py:43
  84.4 5.7 %gather_fusion.1 = f32[1024,2,160]{2,1,0:T(2,128)S(1)} fusion(f32[2,1024,160]{2,0,1:T(2,128)} %copy.46, s32[1024]{0:T(1024)S(1)} %broadcast_clamp_fusion), kind=kCustom, calls=%fused_computation.1 | custom fusion | bytes 2625536 | tf_op jit(solution)/shard_map/jit(_take)/gather | solution.py:48
  101.0 110.6 %all-gather.6.cloned.1.call-done = f32[2,1024,2560]{1,0,2:T(2,128)} async-done(((f32[2,1024,160]{1,0,2:T(2,128)}), f32[2,1024,2560]{1,0,2:T(2,128)}) %all-gather.6.cloned.1.call-update) | async-done | bytes 20971536 | tf_op jit(solution)/shard_map/all_gather | solution.py:61
  212.8 31.8 %slice_add_fusion = (f32[1,1024,2560]{1,0,2:T(1,128)}, f32[1,1024,2560]{1,0,2:T(1,128)}, f32[1,1024,2560]{1,0,2:T(1,128)}) fusion(f32[2,1024,2560]{1,0,2:T(2,128)} %all-gather.6.cloned.1.call-done), kind=kLoop, calls=%fused_computation.126 | loop fusion | flops 2621440 | bytes 52428800 | tf_op jit(solution)/shard_map/add | solution.py:64
  244.6 28.0 %all-gather.8.cloned.1.call-done = f32[2,2560,128]{2,1,0:T(8,128)} async-done(((f32[2,320,128]{2,1,0:T(8,128)}), f32[2,2560,128]{2,1,0:T(8,128)}) %all-gather.8.cloned.1.call-update) | async-done | bytes 2621456 | tf_op jit(solution)/shard_map/all_gather | solution.py:59
  272.7 12.4 %fusion.14 = f32[1024,128]{1,0:T(8,128)S(1)} fusion(f32[1,1024,2560]{1,0,2:T(1,128)} %get-tuple-element.12, f32[2,2560,128]{2,1,0:T(8,128)} %all-gather.8.cloned.1.call-done), kind=kOutput, calls=%fused_computation.16 | convolution fusion | flops 2013265920 | bytes 12320768 | tf_op jit(solution)/shard_map/dot_general | solution.py:66
  285.2 8.4 %fusion.122 = (f32[1024,128]{1,0:T(8,128)S(1)}, f32[1024,128]{1,0:T(8,128)S(1)}) fusion(f32[1024,128]{1,0:T(8,128)S(1)} %fusion.14, f32[2,2560,128]{2,1,0:T(8,128)S(1)} %copy-done.4, f32[1,1024,2560]{1,0,2:T(1,128)S(1)} %copy-done), kind=kOutput, calls=%fused_computation.131 | convolution fusion | flops 2013396992 | bytes 13369344 | tf_op jit(solution)/shard_map/dot_general | solution.py:66
  293.7 17.9 %fusion.103 = f32[1024,128]{1,0:T(8,128)S(1)} fusion(f32[1024,128]{1,0:T(8,128)S(1)} %fusion.14, f32[1024,128]{1,0:T(8,128)S(1)} %get-tuple-element.27, f32[2,2560,128]{2,1,0:T(8,128)S(1)} %copy-done.4, f32[1,1024,2560]{1,0,2:T(1,128)S(1)} %bitcast.173), kind=kOutput, calls=%fused_computation.80 | convolution fusion | flops 2013855744 | bytes 14680064 | tf_op jit(solution)/shard_map/dot_general | solution.py:66
  318.1 17.3 %all-gather.14.cloned.1.call-done = f32[2,2560,128]{2,1,0:T(8,128)} async-done(((f32[2,320,128]{2,1,0:T(8,128)}), f32[2,2560,128]{2,1,0:T(8,128)}) %all-gather.14.cloned.1.call-update) | async-done | bytes 2621456 | tf_op jit(solution)/shard_map/all_gather | solution.py:63
  335.4 12.2 %fusion.8 = f32[1024,128]{1,0:T(8,128)S(1)} fusion(f32[1,1024,2560]{1,0,2:T(1,128)} %get-tuple-element.12, f32[2,2560,128]{2,1,0:T(8,128)} %all-gather.14.cloned.1.call-done), kind=kOutput, calls=%fused_computation.10 | convolution fusion | flops 2013265920 | bytes 12320768 | tf_op jit(solution)/shard_map/dot_general | solution.py:66
  347.6 12.4 %fusion.119 = (f32[1024,128]{1,0:T(8,128)S(1)}, f32[1024,128]{1,0:T(8,128)S(1)}) fusion(f32[1024,128]{1,0:T(8,128)S(1)} %fusion.8, f32[2,2560,128]{2,1,0:T(8,128)S(1)} %copy-done.3, f32[1,1024,2560]{1,0,2:T(1,128)} %get-tuple-element.13), kind=kOutput, calls=%fused_computation.128 | convolution fusion | flops 2013396992 | bytes 13369344 | tf_op jit(solution)/shard_map/dot_general | solution.py:66
  360.0 8.4 %fusion.88 = f32[1024,128]{1,0:T(8,128)S(1)} fusion(f32[1024,128]{1,0:T(8,128)S(1)} %fusion.8, f32[1024,128]{1,0:T(8,128)S(1)} %get-tuple-element.21, f32[2,2560,128]{2,1,0:T(8,128)S(1)} %copy-done.3, f32[1,1024,2560]{1,0,2:T(1,128)S(1)} %bitcast.175), kind=kOutput, calls=%fused_computation.77 | convolution fusion | flops 2013855744 | bytes 14680064 | tf_op jit(solution)/shard_map/dot_general | solution.py:66
  369.6 24.0 %all-gather.12.cloned.1.call-done = f32[2,2560,128]{2,1,0:T(8,128)} async-done(((f32[2,320,128]{2,1,0:T(8,128)}), f32[2,2560,128]{2,1,0:T(8,128)}) %all-gather.12.cloned.1.call-update) | async-done | bytes 2621456 | tf_op jit(solution)/shard_map/all_gather | solution.py:63
  393.5 12.2 %fusion.10 = f32[1024,128]{1,0:T(8,128)S(1)} fusion(f32[1,1024,2560]{1,0,2:T(1,128)} %get-tuple-element.12, f32[2,2560,128]{2,1,0:T(8,128)} %all-gather.12.cloned.1.call-done), kind=kOutput, calls=%fused_computation.12 | convolution fusion | flops 2013265920 | bytes 12320768 | tf_op jit(solution)/shard_map/dot_general | solution.py:66
  405.8 12.0 %fusion.120 = (f32[1024,128]{1,0:T(8,128)S(1)}, f32[1024,128]{1,0:T(8,128)S(1)}) fusion(f32[1024,128]{1,0:T(8,128)S(1)} %fusion.10, f32[2,2560,128]{2,1,0:T(8,128)S(1)} %copy-done.2, f32[1,1024,2560]{1,0,2:T(1,128)} %get-tuple-element.13), kind=kOutput, calls=%fused_computation.129 | convolution fusion | flops 2013396992 | bytes 13369344 | tf_op jit(solution)/shard_map/dot_general | solution.py:66
  423.2 12.4 %fusion.93 = f32[1024,128]{1,0:T(8,128)S(1)} fusion(f32[1024,128]{1,0:T(8,128)S(1)} %fusion.10, f32[1024,128]{1,0:T(8,128)S(1)} %get-tuple-element.23, f32[2,2560,128]{2,1,0:T(8,128)} %all-gather.12.cloned.1.call-done, f32[1,1024,2560]{1,0,2:T(1,128)} %get-tuple-element.11), kind=kOutput, calls=%fused_computation.78 | convolution fusion | flops 2013855744 | bytes 14680064 | tf_op jit(solution)/shard_map/dot_general | solution.py:66
  436.7 21.0 %all-gather.10.cloned.1.call-done = f32[2,2560,128]{2,1,0:T(8,128)} async-done(((f32[2,320,128]{2,1,0:T(8,128)}), f32[2,2560,128]{2,1,0:T(8,128)}) %all-gather.10.cloned.1.call-update) | async-done | bytes 2621456 | tf_op jit(solution)/shard_map/all_gather | solution.py:63
  457.7 12.2 %fusion.12 = f32[1024,128]{1,0:T(8,128)S(1)} fusion(f32[1,1024,2560]{1,0,2:T(1,128)} %get-tuple-element.12, f32[2,2560,128]{2,1,0:T(8,128)} %all-gather.10.cloned.1.call-done), kind=kOutput, calls=%fused_computation.14 | convolution fusion | flops 2013265920 | bytes 12320768 | tf_op jit(solution)/shard_map/dot_general | solution.py:66
  469.9 6.0 %all-to-all-start.4 = ((f32[2,16,64,128]{3,2,0,1:T(8,128)}), f32[2,16,64,128]{3,2,0,1:T(8,128)}, u32[]{:S(2)}, u32[]{:S(2)}) async-start(f32[2,16,64,128]{3,2,0,1:T(8,128)} %pad_maximum_fusion.2), calls=%async_computation.4 | async-start | bytes 2097152 | tf_op jit(solution)/shard_map/all_to_all | solution.py:74
  475.9 11.8 %fusion.121 = (f32[1024,128]{1,0:T(8,128)S(1)}, f32[1024,128]{1,0:T(8,128)S(1)}) fusion(f32[1024,128]{1,0:T(8,128)S(1)} %fusion.12, f32[2,2560,128]{2,1,0:T(8,128)S(1)} %copy-done.1, f32[1,1024,2560]{1,0,2:T(1,128)} %get-tuple-element.13), kind=kOutput, calls=%fused_computation.130 | convolution fusion | flops 2013396992 | bytes 13369344 | tf_op jit(solution)/shard_map/dot_general | solution.py:66
  487.6 11.7 %fusion.98 = f32[1024,128]{1,0:T(8,128)S(1)} fusion(f32[1024,128]{1,0:T(8,128)S(1)} %fusion.12, f32[1024,128]{1,0:T(8,128)S(1)} %get-tuple-element.25, f32[2,2560,128]{2,1,0:T(8,128)S(1)} %copy-done.1, f32[1,1024,2560]{1,0,2:T(1,128)} %get-tuple-element.11), kind=kOutput, calls=%fused_computation.79 | convolution fusion | flops 2013855744 | bytes 14680064 | tf_op jit(solution)/shard_map/dot_general | solution.py:66
  499.4 21.3 %all_to_all.30 = f32[2,16,64,128]{3,2,0,1:T(8,128)S(1)} all-to-all(f32[2,16,64,128]{3,2,0,1:T(8,128)S(1)} %pad_maximum_fusion.1), channel_id=1, replica_groups=mesh['xh'=2,'z'=4,'xl'=2,'y'=4,'core'=2] {'xl','y','core'}, dimensions={1} | all-to-all | bytes 2097152 | tf_op jit(solution)/shard_map/all_to_all | solution.py:74
  (80 shorter events, 55.9 us)
Async XLA Ops:
  9.9 8.7 %copy-start.9 = (s32[7]{0:T(128)S(1)}, s32[7]{0:T(128)}, u32[]{:S(2)}) copy-start(s32[7]{0:T(128)} %param.7) | copy-start | bytes 88
  9.9 34.6 %all-to-all-start = ((f32[2,8,8,16,160]{4,3,1,0,2:T(8,128)}), f32[2,8,8,16,160]{4,3,1,0,2:T(8,128)S(1)}, u32[]{:S(2)}, u32[]{:S(2)}) async-start(f32[2,8,8,16,160]{4,3,1,0,2:T(8,128)} %copy.42), calls=%async_computation | async-start | bytes 4194304 | tf_op jit(solution)/shard_map/all_to_all | solution.py:37
  49.9 31.4 %all-to-all-start.1 = ((f32[2,8,8,16,160]{4,3,2,0,1:T(8,128)}), f32[2,8,8,16,160]{4,3,2,0,1:T(8,128)S(1)}, u32[]{:S(2)}, u32[]{:S(2)}) async-start(f32[2,8,8,16,160]{4,3,2,0,1:T(8,128)} %copy_select_fusion), calls=%async_computation.1 | async-start | bytes 4194304 | tf_op jit(solution)/shard_map/all_to_all | solution.py:43
  55.1 156.5 %all-gather.6.cloned.1.call-start = ((), (), s32[]{:S(2)}) async-start(), calls=%async_computation.6 | async-start | bytes 22282240 | tf_op jit(solution)/shard_map/all_gather | solution.py:61
  99.8 172.9 %all-gather.8.cloned.1.call-start = ((), (), s32[]{:S(2)}) async-start(), calls=%async_computation.7 | async-start | bytes 2949120 | tf_op jit(solution)/shard_map/all_gather | solution.py:59
  101.0 234.4 %all-gather.14.cloned.1.call-start = ((), (), s32[]{:S(2)}) async-start(), calls=%async_computation.10 | async-start | bytes 2949120 | tf_op jit(solution)/shard_map/all_gather | solution.py:63
  211.6 181.9 %all-gather.12.cloned.1.call-start = ((), (), s32[]{:S(2)}) async-start(), calls=%async_computation.9 | async-start | bytes 2949120 | tf_op jit(solution)/shard_map/all_gather | solution.py:63
  212.2 245.5 %all-gather.10.cloned.1.call-start = ((), (), s32[]{:S(2)}) async-start(), calls=%async_computation.8 | async-start | bytes 2949120 | tf_op jit(solution)/shard_map/all_gather | solution.py:63
  272.7 12.5 %copy-start = (f32[1,1024,2560]{1,0,2:T(1,128)S(1)}, f32[1,1024,2560]{1,0,2:T(1,128)}, u32[]{:S(2)}) copy-start(f32[1,1024,2560]{1,0,2:T(1,128)} %get-tuple-element.13) | copy-start | bytes 31457284
  272.7 12.5 %copy-start.4 = (f32[2,2560,128]{2,1,0:T(8,128)S(1)}, f32[2,2560,128]{2,1,0:T(8,128)}, u32[]{:S(2)}) copy-start(f32[2,2560,128]{2,1,0:T(8,128)} %all-gather.8.cloned.1.call-done) | copy-start | bytes 7864324
  285.1 8.5 %slice-start = ((s8[10485760]{0:T(1024)(128)(4,1)}), s8[4194304]{0:T(1024)(128)(4,1)S(1)}, s32[]{:S(2)}) async-start(s8[10485760]{0:T(1024)(128)(4,1)} %bitcast.172), calls=%async_computation.11 | async-start | bytes 8388608
  285.2 8.5 %slice-start.1 = ((s8[10485760]{0:T(1024)(128)(4,1)}), s8[4194304]{0:T(1024)(128)(4,1)S(1)}, s32[]{:S(2)}) async-start(s8[10485760]{0:T(1024)(128)(4,1)} %bitcast.172), calls=%async_computation.12 | async-start | bytes 8388608
  285.2 8.5 %slice-start.2 = ((s8[10485760]{0:T(1024)(128)(4,1)}), s8[2097152]{0:T(1024)(128)(4,1)S(1)}, s32[]{:S(2)}) async-start(s8[10485760]{0:T(1024)(128)(4,1)} %bitcast.172), calls=%async_computation.13 | async-start | bytes 4194304
  312.7 105.0 %all-to-all-start.2 = ((f32[2,16,64,128]{3,2,0,1:T(8,128)}), f32[2,16,64,128]{3,2,0,1:T(8,128)S(1)}, u32[]{:S(2)}, u32[]{:S(2)}) async-start(f32[2,16,64,128]{3,2,0,1:T(8,128)} %pad_maximum_fusion), calls=%async_computation.2 | async-start | bytes 2097152 | tf_op jit(solution)/shard_map/all_to_all | solution.py:74
  335.4 12.2 %copy-start.3 = (f32[2,2560,128]{2,1,0:T(8,128)S(1)}, f32[2,2560,128]{2,1,0:T(8,128)}, u32[]{:S(2)}) copy-start(f32[2,2560,128]{2,1,0:T(8,128)} %all-gather.14.cloned.1.call-done) | copy-start | bytes 7864324
  335.4 24.6 %slice-start.3 = ((s8[10485760]{0:T(1024)(128)(4,1)}), s8[4194304]{0:T(1024)(128)(4,1)S(1)}, s32[]{:S(2)}) async-start(s8[10485760]{0:T(1024)(128)(4,1)} %bitcast.174), calls=%async_computation.14 | async-start | bytes 8388608
  335.4 24.6 %slice-start.4 = ((s8[10485760]{0:T(1024)(128)(4,1)}), s8[4194304]{0:T(1024)(128)(4,1)S(1)}, s32[]{:S(2)}) async-start(s8[10485760]{0:T(1024)(128)(4,1)} %bitcast.174), calls=%async_computation.15 | async-start | bytes 8388608
  347.6 12.4 %slice-start.5 = ((s8[10485760]{0:T(1024)(128)(4,1)}), s8[2097152]{0:T(1024)(128)(4,1)S(1)}, s32[]{:S(2)}) async-start(s8[10485760]{0:T(1024)(128)(4,1)} %bitcast.174), calls=%async_computation.16 | async-start | bytes 4194304
  393.5 12.2 %copy-start.2 = (f32[2,2560,128]{2,1,0:T(8,128)S(1)}, f32[2,2560,128]{2,1,0:T(8,128)}, u32[]{:S(2)}) copy-start(f32[2,2560,128]{2,1,0:T(8,128)} %all-gather.12.cloned.1.call-done) | copy-start | bytes 7864324
  417.8 17.9 %copy-start.5 = (f32[2,16,64,128]{3,2,0,1:T(8,128)}, f32[2,16,64,128]{3,2,0,1:T(8,128)S(1)}, u32[]{:S(2)}) copy-start(f32[2,16,64,128]{3,2,0,1:T(8,128)S(1)} %all-to-all-done.2) | copy-start | bytes 3145732
  417.8 52.1 %all-to-all-start.5 = ((f32[2,16,64,128]{3,2,0,1:T(8,128)}), f32[2,16,64,128]{3,2,0,1:T(8,128)}, u32[]{:S(2)}, u32[]{:S(2)}) async-start(f32[2,16,64,128]{3,2,0,1:T(8,128)} %pad_maximum_fusion.3), calls=%async_computation.5 | async-start | bytes 2097152 | tf_op jit(solution)/shard_map/all_to_all | solution.py:74
  457.7 18.2 %copy-start.1 = (f32[2,2560,128]{2,1,0:T(8,128)S(1)}, f32[2,2560,128]{2,1,0:T(8,128)}, u32[]{:S(2)}) copy-start(f32[2,2560,128]{2,1,0:T(8,128)} %all-gather.10.cloned.1.call-done) | copy-start | bytes 7864324
  469.9 29.5 %all-to-all-start.4 = ((f32[2,16,64,128]{3,2,0,1:T(8,128)}), f32[2,16,64,128]{3,2,0,1:T(8,128)}, u32[]{:S(2)}, u32[]{:S(2)}) async-start(f32[2,16,64,128]{3,2,0,1:T(8,128)} %pad_maximum_fusion.2), calls=%async_computation.4 | async-start | bytes 2097152 | tf_op jit(solution)/shard_map/all_to_all | solution.py:74
  499.3 21.4 %copy-start.6 = (f32[2,16,64,128]{3,2,0,1:T(8,128)S(1)}, f32[2,16,64,128]{3,2,0,1:T(8,128)}, u32[]{:S(2)}) copy-start(f32[2,16,64,128]{3,2,0,1:T(8,128)} %copy-done.5) | copy-start | bytes 3145732
  (2 other events, 13.7 us)
Sparse Core Ops, SparseCore 0:
  99.9 111.6 all-gather.5
  213.9 58.7 all-gather.7
  275.0 60.3 all-gather.13
  337.5 55.9 all-gather.11
  395.7 61.9 all-gather.9

commit v4 on v3

--- a/solution.py
+++ b/solution.py
@@ -53,23 +53,20 @@
     col_count = lax.axis_size(COL)
     rows = left.shape[1]
     cols = right.shape[2]
-    chunks = 4
-    width = cols // chunks
-    rparts = [right[:, :, j * width:(j + 1) * width] for j in range(chunks)]
-    first = lax.all_gather(rparts[0], ROW, axis=1, tiled=True)
+    rall = lax.all_gather(right, ROW, axis=1, tiled=True)
     lp = permute_left(left, prefix_owner, qubit_order, row_count)
+    lp = lax.optimization_barrier((lp, rall))[0]
     lall = lax.all_gather(lp, COL, axis=2, tiled=True)
-    rest = lax.optimization_barrier((lall, rparts[1:]))[1]
-    gathered = [first] + [lax.all_gather(r, ROW, axis=1, tiled=True) for r in rest]
-    lsum = lall[0] + lall[1]
     high = lax.Precision.HIGH
     dot = lambda a, b: jnp.dot(a, b, preferred_element_type=jnp.float32, precision=high)
+    chunks = 2
+    width = cols // chunks
     outs = []
-    for rall in gathered:
-        t1 = dot(lall[0], rall[0])
-        t2 = dot(lall[1], rall[1])
-        t3 = dot(lsum, rall[0] + rall[1])
-        tile = jnp.stack([t1 - t2, t3 - t1 - t2], axis=0)
+    for j in range(chunks):
+        rr = rall[:, :, j * width:(j + 1) * width]
+        re = dot(lall[0], rr[0]) - dot(lall[1], rr[1])
+        im = dot(lall[0], rr[1]) + dot(lall[1], rr[0])
+        tile = jnp.stack([re, im], axis=0)
         tile = tile.reshape(2, col_count, rows // col_count, width)
         outs.append(lax.all_to_all(tile, COL, split_axis=1, concat_axis=1, tiled=True))
     out = jnp.stack(outs, axis=3)

time: 549 us -> 466 us (0.85)
  matrix products: 144 us -> 91.2 us
  other arithmetic: 43.4 us -> 9.97 us
  local copies, waits for them, and re-layouts: 32.7 us -> 55.5 us
  waiting for transfers between devices: 254 us -> 237 us
  starting transfers between devices: 30.6 us -> 17.3 us
  blocking collectives: 21.3 us -> 32.2 us
    dot_general x12 -> x8, matrix products: 144 us -> 91.2 us  [body(): jnp.dot(a, b, preferred_element_type=jnp.float32, precision=high)]
    all_gather x4 -> x1, waiting for transfers between devices: 90.2 us -> 50.6 us  [body(): rall = lax.all_gather(right, ROW, axis=1, tiled=True)]
    add x1 -> x0, other arithmetic: 31.8 us -> none  [body(): lsum = lall[0] + lall[1]]
    slice x1, local copies, waits for them, and re-layouts: 1.1 us -> 22.6 us  [body(): re = dot(lall[0], rr[0]) - dot(lall[1], rr[1])]
    all_to_all x1, waiting for transfers between devices: 25.8 us -> 39.1 us  [permute_left(): x = lax.all_to_all(x, ROW, split_axis=2, concat_axis=2, tiled=True)]
    all_to_all x3 -> x1, starting transfers between devices: 16.8 us -> 4.94 us  [body(): lax.all_to_all(tile, COL, split_axis=1, concat_axis=1, tiled=True)]
    all_to_all x1, waiting for transfers between devices: 25.9 us -> 36.9 us  [permute_left(): y = lax.all_to_all(y, ROW, split_axis=1, concat_axis=1, tiled=True)]
    all_to_all x1, blocking collectives: 21.3 us -> 32.2 us  [body(): lax.all_to_all(tile, COL, split_axis=1, concat_axis=1, tiled=True)]
  transfers between devices with their start and end apart: 10 -> 5, of which waited for: 7 -> 4; matrix products, arithmetic and copies ran while one was open for 34% -> 14% of each run, Pallas kernels for 0% -> 0%
where the time goes in v4:
time: 466 us; the launch traced here: 457 us
  waiting for transfers between devices  237 us (51%)
  matrix products  91.2 us (20%)
  local copies, waits for them, and re-layouts  55.5 us (12%)
  blocking collectives  32.2 us (7%)
  starting transfers between devices  17.3 us (4%)
  between operations  14.2 us (3%)
  other arithmetic  9.97 us (2%)
    all_gather x1, waiting for transfers between devices, body(): lall = lax.all_gather(lp, COL, axis=2, tiled=True)  110 us
    dot_general x8, matrix products, body(): jnp.dot(a, b, preferred_element_type=jnp.float32, precision=high)  91.2 us
    all_gather x1, waiting for transfers between devices, body(): rall = lax.all_gather(right, ROW, axis=1, tiled=True)  50.6 us
    all_to_all x1, waiting for transfers between devices, permute_left(): x = lax.all_to_all(x, ROW, split_axis=2, concat_axis=2, tiled=True)  39.1 us
    all_to_all x1, waiting for transfers between devices, permute_left(): y = lax.all_to_all(y, ROW, split_axis=1, concat_axis=1, tiled=True)  36.9 us
    all_to_all x1, blocking collectives, body(): lax.all_to_all(tile, COL, split_axis=1, concat_axis=1, tiled=True)  32.2 us
    slice x1, local copies, waits for them, and re-layouts, body(): re = dot(lall[0], rr[0]) - dot(lall[1], rr[1])  22.6 us
  transfers between devices with their start and end apart: 5, of which 4 were waited for; matrix products, arithmetic and copies ran while one was open for 14% of the time, Pallas kernels for 0%

profile of v4, /device:TPU:1, one launch (start us, length us, event | category | flops | bytes accessed | tf_op | source)
XLA Modules:
  0.0 457.2 jit_solution(9038100695471533994)
XLA Ops:
  10.6 8.3 %all-to-all-start = ((f32[2,8,8,16,160]{4,3,1,0,2:T(8,128)}), f32[2,8,8,16,160]{4,3,1,0,2:T(8,128)S(1)}, u32[]{:S(2)}, u32[]{:S(2)}) async-start(f32[2,8,8,16,160]{4,3,1,0,2:T(8,128)} %copy.34), calls=%async_computation | async-start | bytes 4194304 | tf_op jit(solution)/shard_map/all_to_all | solution.py:37
  19.3 39.1 %all-to-all-done = f32[2,8,8,16,160]{4,3,1,0,2:T(8,128)S(1)} async-done(((f32[2,8,8,16,160]{4,3,1,0,2:T(8,128)}), f32[2,8,8,16,160]{4,3,1,0,2:T(8,128)S(1)}, u32[]{:S(2)}, u32[]{:S(2)}) %all-to-all-start) | async-done | bytes 1310752 | tf_op jit(solution)/shard_map/all_to_all | solution.py:37
  60.0 2.3 gather_fusion
  63.8 4.0 all-to-all-start.1
  68.0 36.9 %all-to-all-done.1 = f32[2,8,8,16,160]{4,3,2,0,1:T(8,128)S(1)} async-done(((f32[2,8,8,16,160]{4,3,2,0,1:T(8,128)}), f32[2,8,8,16,160]{4,3,2,0,1:T(8,128)S(1)}, u32[]{:S(2)}, u32[]{:S(2)}) %all-to-all-start.1) | async-done | bytes 1310752 | tf_op jit(solution)/shard_map/all_to_all | solution.py:43
  105.2 2.9 copy.38
  108.1 5.8 %gather_fusion.1 = f32[1024,2,160]{2,1,0:T(2,128)S(1)} fusion(f32[2,1024,160]{2,0,1:T(2,128)} %copy.38, s32[1024]{0:T(1024)S(1)} %broadcast_clamp_fusion), kind=kCustom, calls=%fused_computation.1 | custom fusion | bytes 2625536 | tf_op jit(solution)/shard_map/jit(_take)/gather | solution.py:48
  113.9 4.5 select_bitcast_fusion
  118.4 50.6 %all-gather.3.cloned.1.call-done = f32[2,2560,512]{2,1,0:T(8,128)} async-done(((f32[2,320,512]{2,1,0:T(8,128)}), f32[2,2560,512]{2,1,0:T(8,128)}) %all-gather.3.cloned.1.call-update) | async-done | bytes 10485776 | tf_op jit(solution)/shard_map/all_gather | solution.py:56
  169.0 5.0 %copy.39 = f32[2,1024,160]{1,0,2:T(2,128)} copy(f32[2,1024,160]{2,0,1:T(2,128)} %select_bitcast_fusion) | data formatting | bytes 2621440 | tf_op jit(solution)/shard_map/optimization_barrier | solution.py:58
  174.0 109.5 %all-gather.5.cloned.1.call-done = f32[2,1024,2560]{1,0,2:T(2,128)} async-done(((f32[2,1024,160]{1,0,2:T(2,128)}), f32[2,1024,2560]{1,0,2:T(2,128)}) %all-gather.5.cloned.1.call-update) | async-done | bytes 20971536 | tf_op jit(solution)/shard_map/all_gather | solution.py:59
  283.5 22.6 %fusion.46 = (f32[1,1024,2560]{1,0,2:T(1,128)S(1)}, f32[1,1024,2560]{1,0,2:T(1,128)}) fusion(f32[2,1024,2560]{1,0,2:T(2,128)} %all-gather.5.cloned.1.call-done), kind=kLoop, calls=%fused_computation.80 | loop fusion | bytes 41943040 | tf_op jit(solution)/shard_map/slice | solution.py:67
  306.2 16.6 %fusion = f32[1024,256]{1,0:T(8,128)S(1)} fusion(f32[1,1024,2560]{1,0,2:T(1,128)} %get-tuple-element.8, f32[2,2560,512]{2,1,0:T(8,128)} %all-gather.3.cloned.1.call-done), kind=kOutput, calls=%fused_computation.2 | convolution fusion | flops 4026531840 | bytes 14155776 | tf_op jit(solution)/shard_map/dot_general | solution.py:61
  322.8 10.3 %fusion.2 = f32[1024,256]{1,0:T(8,128)S(1)} fusion(f32[1,1024,2560]{1,0,2:T(1,128)S(1)} %copy-done.1, f32[2,2560,512]{2,1,0:T(8,128)} %all-gather.3.cloned.1.call-done), kind=kOutput, calls=%fused_computation.4 | convolution fusion | flops 4026531840 | bytes 14155776 | tf_op jit(solution)/shard_map/dot_general | solution.py:61
  333.1 10.7 %fusion.33 = f32[1024,256]{1,0:T(8,128)S(1)} fusion(f32[1024,256]{1,0:T(8,128)S(1)} %fusion, f32[2,2560,512]{2,1,0:T(8,128)} %all-gather.3.cloned.1.call-done, f32[1,1024,2560]{1,0,2:T(1,128)S(1)} %get-tuple-element.7), kind=kOutput, calls=%fused_computation.38 | convolution fusion | flops 4026793984 | bytes 15204352 | tf_op jit(solution)/shard_map/dot_general | solution.py:61
  343.8 10.3 %fusion.30 = f32[1024,256]{1,0:T(8,128)S(1)} fusion(f32[1024,256]{1,0:T(8,128)S(1)} %fusion.2, f32[2,2560,512]{2,1,0:T(8,128)} %all-gather.3.cloned.1.call-done, f32[1,1024,2560]{1,0,2:T(1,128)S(1)} %get-tuple-element.7), kind=kOutput, calls=%fused_computation.37 | convolution fusion | flops 4026793984 | bytes 15204352 | tf_op jit(solution)/shard_map/dot_general | solution.py:61
  355.5 4.9 %all-to-all-start.3 = ((f32[2,16,64,256]{3,2,0,1:T(8,128)}), f32[2,16,64,256]{3,2,0,1:T(8,128)}, u32[]{:S(2)}, u32[]{:S(2)}) async-start(f32[2,16,64,256]{3,2,0,1:T(8,128)} %pad_maximum_fusion.1), calls=%async_computation.3 | async-start | bytes 4194304 | tf_op jit(solution)/shard_map/all_to_all | solution.py:71
  360.5 12.7 %fusion.4 = f32[1024,256]{1,0:T(8,128)S(1)} fusion(f32[1,1024,2560]{1,0,2:T(1,128)} %get-tuple-element.8, f32[2,2560,512]{2,1,0:T(8,128)} %all-gather.3.cloned.1.call-done), kind=kOutput, calls=%fused_computation.6 | convolution fusion | flops 4026531840 | bytes 14155776 | tf_op jit(solution)/shard_map/dot_general | solution.py:61
  373.3 13.0 %fusion.6 = f32[1024,256]{1,0:T(8,128)S(1)} fusion(f32[1,1024,2560]{1,0,2:T(1,128)} %get-tuple-element.8, f32[2,2560,512]{2,1,0:T(8,128)} %all-gather.3.cloned.1.call-done), kind=kOutput, calls=%fused_computation.8 | convolution fusion | flops 4026531840 | bytes 14155776 | tf_op jit(solution)/shard_map/dot_general | solution.py:61
  386.3 8.7 %fusion.24 = f32[1024,256]{1,0:T(8,128)S(1)} fusion(f32[1024,256]{1,0:T(8,128)S(1)} %fusion.6, f32[2,2560,512]{2,1,0:T(8,128)S(1)} %bitcast.100, f32[1,1024,2560]{1,0,2:T(1,128)S(1)} %bitcast.98), kind=kOutput, calls=%fused_computation.35 | convolution fusion | flops 4026793984 | bytes 15204352 | tf_op jit(solution)/shard_map/dot_general | solution.py:61
  395.0 9.0 %fusion.27 = f32[1024,256]{1,0:T(8,128)S(1)} fusion(f32[1024,256]{1,0:T(8,128)S(1)} %fusion.4, f32[2,2560,512]{2,1,0:T(8,128)S(1)} %bitcast.100, f32[1,1024,2560]{1,0,2:T(1,128)S(1)} %bitcast.98), kind=kOutput, calls=%fused_computation.36 | convolution fusion | flops 4026793984 | bytes 15204352 | tf_op jit(solution)/shard_map/dot_general | solution.py:61
  404.2 32.2 %all_to_all.20 = f32[2,16,64,256]{3,2,0,1:T(8,128)S(1)} all-to-all(f32[2,16,64,256]{3,2,0,1:T(8,128)S(1)} %pad_maximum_fusion), channel_id=1, replica_groups=mesh['xh'=2,'z'=4,'xl'=2,'y'=4,'core'=2] {'xl','y','core'}, dimensions={1} | all-to-all | bytes 4194304 | tf_op jit(solution)/shard_map/all_to_all | solution.py:71
  438.3 5.2 %copy.44 = f32[2,64,16,2,256]{4,3,2,1,0:T(2,128)} copy(f32[2,64,16,2,256]{4,1,0,2,3:T(8,128)S(1)} %maximum_bitcast_fusion) | data formatting | bytes 8388608 | tf_op jit(solution)/shard_map/transpose | solution.py:73
  443.5 6.4 %reshape.238 = f32[2,64,8192]{2,1,0:T(8,128)} reshape(f32[2,64,16,2,256]{4,3,2,1,0:T(2,128)} %copy.44) | data formatting | bytes 8388608 | tf_op jit(solution)/shard_map/reshape | solution.py:74
  (48 shorter events, 11.5 us)
Async XLA Ops:
  6.5 162.4 %all-gather.3.cloned.1.call-start = ((), (), s32[]{:S(2)}) async-start(), calls=%async_computation.4 | async-start | bytes 11796480 | tf_op jit(solution)/shard_map/all_gather | solution.py:56
  9.1 9.9 %copy-start.2 = (s32[64]{0:T(128)S(1)}, s32[64]{0:T(128)}, u32[]{:S(2)}) copy-start(s32[64]{0:T(128)} %param.6) | copy-start | bytes 772
  9.1 10.1 %copy-start.3 = (s32[7]{0:T(128)S(1)}, s32[7]{0:T(128)}, u32[]{:S(2)}) copy-start(s32[7]{0:T(128)} %param.7) | copy-start | bytes 88
  10.6 47.8 %all-to-all-start = ((f32[2,8,8,16,160]{4,3,1,0,2:T(8,128)}), f32[2,8,8,16,160]{4,3,1,0,2:T(8,128)S(1)}, u32[]{:S(2)}, u32[]{:S(2)}) async-start(f32[2,8,8,16,160]{4,3,1,0,2:T(8,128)} %copy.34), calls=%async_computation | async-start | bytes 4194304 | tf_op jit(solution)/shard_map/all_to_all | solution.py:37
  63.8 41.2 %all-to-all-start.1 = ((f32[2,8,8,16,160]{4,3,2,0,1:T(8,128)}), f32[2,8,8,16,160]{4,3,2,0,1:T(8,128)S(1)}, u32[]{:S(2)}, u32[]{:S(2)}) async-start(f32[2,8,8,16,160]{4,3,2,0,1:T(8,128)} %copy_select_fusion), calls=%async_computation.1 | async-start | bytes 4194304 | tf_op jit(solution)/shard_map/all_to_all | solution.py:43
  67.8 215.7 %all-gather.5.cloned.1.call-start = ((), (), s32[]{:S(2)}) async-start(), calls=%async_computation.5 | async-start | bytes 22282240 | tf_op jit(solution)/shard_map/all_gather | solution.py:59
  306.2 37.6 %copy-start = (f32[1,1024,2560]{1,0,2:T(1,128)}, f32[1,1024,2560]{1,0,2:T(1,128)S(1)}, u32[]{:S(2)}) copy-start(f32[1,1024,2560]{1,0,2:T(1,128)S(1)} %get-tuple-element.7) | copy-start | bytes 31457284
  306.2 16.6 %copy-start.1 = (f32[1,1024,2560]{1,0,2:T(1,128)S(1)}, f32[1,1024,2560]{1,0,2:T(1,128)}, u32[]{:S(2)}) copy-start(f32[1,1024,2560]{1,0,2:T(1,128)} %get-tuple-element.8) | copy-start | bytes 31457284
  355.5 48.7 %all-to-all-start.3 = ((f32[2,16,64,256]{3,2,0,1:T(8,128)}), f32[2,16,64,256]{3,2,0,1:T(8,128)}, u32[]{:S(2)}, u32[]{:S(2)}) async-start(f32[2,16,64,256]{3,2,0,1:T(8,128)} %pad_maximum_fusion.1), calls=%async_computation.3 | async-start | bytes 4194304 | tf_op jit(solution)/shard_map/all_to_all | solution.py:71
  360.5 25.8 %slice-start = ((s8[10485760]{0:T(1024)(128)(4,1)}), s8[4194304]{0:T(1024)(128)(4,1)S(1)}, s32[]{:S(2)}) async-start(s8[10485760]{0:T(1024)(128)(4,1)} %bitcast.97), calls=%async_computation.6 | async-start | bytes 8388608
  360.5 25.8 %slice-start.1 = ((s8[10485760]{0:T(1024)(128)(4,1)}), s8[4194304]{0:T(1024)(128)(4,1)S(1)}, s32[]{:S(2)}) async-start(s8[10485760]{0:T(1024)(128)(4,1)} %bitcast.97), calls=%async_computation.7 | async-start | bytes 8388608
  360.5 25.8 %slice-start.3 = ((s8[10485760]{0:T(1024)(128)(4,1)}), s8[4194304]{0:T(1024)(128)(4,1)S(1)}, s32[]{:S(2)}) async-start(s8[10485760]{0:T(1024)(128)(4,1)} %bitcast.99), calls=%async_computation.9 | async-start | bytes 8388608
  360.5 25.8 %slice-start.4 = ((s8[10485760]{0:T(1024)(128)(4,1)}), s8[4194304]{0:T(1024)(128)(4,1)S(1)}, s32[]{:S(2)}) async-start(s8[10485760]{0:T(1024)(128)(4,1)} %bitcast.99), calls=%async_computation.10 | async-start | bytes 8388608
  373.2 13.0 %slice-start.2 = ((s8[10485760]{0:T(1024)(128)(4,1)}), s8[2097152]{0:T(1024)(128)(4,1)S(1)}, s32[]{:S(2)}) async-start(s8[10485760]{0:T(1024)(128)(4,1)} %bitcast.97), calls=%async_computation.8 | async-start | bytes 4194304
  373.2 13.0 %slice-start.5 = ((s8[10485760]{0:T(1024)(128)(4,1)}), s8[2097152]{0:T(1024)(128)(4,1)S(1)}, s32[]{:S(2)}) async-start(s8[10485760]{0:T(1024)(128)(4,1)} %bitcast.99), calls=%async_computation.11 | async-start | bytes 4194304
Sparse Core Ops, SparseCore 0:
  9.7 159.2 all-gather.2
  174.1 109.3 all-gather.4

commit v5 on v3

--- a/solution.py
+++ b/solution.py
@@ -28,7 +28,7 @@
     return jnp.sum(bits * powers[None, :], axis=1)
 
 
-def permute_left(left, prefix_owner, qubit_order, row_count):
+def permute_left(left, prefix_owner, qubit_order, row_count, col_count):
     _, rows, kcols = left.shape
     span = 2**LOW_BITS
     local = rows // span
@@ -45,7 +45,12 @@
     s = inner_order(qubit_order, LOW_BITS)
     o_local = jnp.arange(local, dtype=jnp.int32)
     idx = (s[None, :] // sub) * (local * sub) + o_local[:, None] * sub + s[None, :] % sub
-    return jnp.take(y, idx.reshape(-1), axis=1)
+    idx = idx.reshape(-1)
+    q = rows // col_count // 2
+    m = jnp.arange(rows, dtype=jnp.int32)
+    h, rest = m // (rows // 2), m % (rows // 2)
+    pos = (rest // q) * (2 * q) + h * q + rest % q
+    return jnp.take(y, jnp.take(idx, pos), axis=1)
 
 
 def body(left, right, prefix_owner, qubit_order):
@@ -53,27 +58,32 @@
     col_count = lax.axis_size(COL)
     rows = left.shape[1]
     cols = right.shape[2]
-    chunks = 4
-    width = cols // chunks
-    rparts = [right[:, :, j * width:(j + 1) * width] for j in range(chunks)]
-    first = lax.all_gather(rparts[0], ROW, axis=1, tiled=True)
-    lp = permute_left(left, prefix_owner, qubit_order, row_count)
-    lall = lax.all_gather(lp, COL, axis=2, tiled=True)
-    rest = lax.optimization_barrier((lall, rparts[1:]))[1]
-    gathered = [first] + [lax.all_gather(r, ROW, axis=1, tiled=True) for r in rest]
-    lsum = lall[0] + lall[1]
+    rall = lax.all_gather(right, ROW, axis=1, tiled=True)
+    lp = permute_left(left, prefix_owner, qubit_order, row_count, col_count)
+    lt = jnp.swapaxes(lp, 1, 2)
+    halves = 2
+    part = rows // halves
+    lt = lax.optimization_barrier((lt, rall))[0]
     high = lax.Precision.HIGH
-    dot = lambda a, b: jnp.dot(a, b, preferred_element_type=jnp.float32, precision=high)
+    dims = (((0,), (0,)), ((), ()))
+    dot = lambda a, b: lax.dot_general(a, b, dims, preferred_element_type=jnp.float32, precision=high)
+    rsum = rall[0] + rall[1]
     outs = []
-    for rall in gathered:
+    prev = None
+    for h in range(halves):
+        piece = lt[:, :, h * part:(h + 1) * part]
+        if prev is not None:
+            piece = lax.optimization_barrier((piece, prev))[0]
+        lall = lax.all_gather(piece, COL, axis=1, tiled=True)
+        prev = lall
         t1 = dot(lall[0], rall[0])
         t2 = dot(lall[1], rall[1])
-        t3 = dot(lsum, rall[0] + rall[1])
+        t3 = dot(lall[0] + lall[1], rsum)
         tile = jnp.stack([t1 - t2, t3 - t1 - t2], axis=0)
-        tile = tile.reshape(2, col_count, rows // col_count, width)
+        tile = tile.reshape(2, col_count, part // col_count, cols)
         outs.append(lax.all_to_all(tile, COL, split_axis=1, concat_axis=1, tiled=True))
-    out = jnp.stack(outs, axis=3)
-    out = jnp.transpose(out, (0, 2, 1, 3, 4))
+    out = jnp.stack(outs, axis=1)
+    out = jnp.transpose(out, (0, 1, 3, 2, 4))
     return out.reshape(2, rows // col_count, col_count * cols)
 
 

time: 549 us -> 411 us (0.75)
  matrix products: 144 us -> 32.8 us
  waiting for transfers between devices: 254 us -> 234 us
  starting transfers between devices: 30.6 us -> 17.5 us
  blocking collectives: 21.3 us -> 32.4 us
    dot_general x12 -> x6, matrix products: 144 us -> 32.8 us  [body(): lax.dot_general(a, b, dims, preferred_element_type=jnp.float32, precision...]
    all_gather x5 -> x3, waiting for transfers between devices: 201 us -> 162 us  [the longest x2 111 us: body(): lall = lax.all_gather(piece, COL, axis=1, tiled=True)]
    all_to_all x1, waiting for transfers between devices: 25.8 us -> 39.1 us  [permute_left(): x = lax.all_to_all(x, ROW, split_axis=2, concat_axis=2, tiled=True)]
    all_to_all x3 -> x1, starting transfers between devices: 16.8 us -> 5.06 us  [body(): lax.all_to_all(tile, COL, split_axis=1, concat_axis=1, tiled=True)]
    all_to_all x1, blocking collectives: 21.3 us -> 32.4 us  [body(): lax.all_to_all(tile, COL, split_axis=1, concat_axis=1, tiled=True)]
    all_to_all x1, waiting for transfers between devices: 25.9 us -> 32.4 us  [permute_left(): y = lax.all_to_all(y, ROW, split_axis=1, concat_axis=1, tiled=True)]
    add x1 -> x2, other arithmetic: 31.8 us -> 27.7 us  [body(): t3 = dot(lall[0] + lall[1], rsum)]
  transfers between devices with their start and end apart: 10 -> 6, of which waited for: 7 -> 5; matrix products, arithmetic and copies ran while one was open for 34% -> 22% of each run, Pallas kernels for 0% -> 0%
where the time goes in v5:
time: 411 us; the launch traced here: 405 us
  waiting for transfers between devices  234 us (57%)
  other arithmetic  38.1 us (9%)
  local copies, waits for them, and re-layouts  36 us (9%)
  matrix products  32.8 us (8%)
  blocking collectives  32.4 us (8%)
  starting transfers between devices  17.5 us (4%)
  between operations  13.7 us (3%)
    all_gather x2, waiting for transfers between devices, body(): lall = lax.all_gather(piece, COL, axis=1, tiled=True)  111 us
    all_gather x1, waiting for transfers between devices, body(): rall = lax.all_gather(right, ROW, axis=1, tiled=True)  50.6 us
    all_to_all x1, waiting for transfers between devices, permute_left(): x = lax.all_to_all(x, ROW, split_axis=2, concat_axis=2, tiled=True)  39.1 us
    dot_general x6, matrix products, body(): lax.dot_general(a, b, dims, preferred_element_type=jnp.float32, precision...  32.8 us
    all_to_all x1, waiting for transfers between devices, permute_left(): y = lax.all_to_all(y, ROW, split_axis=1, concat_axis=1, tiled=True)  32.4 us
    all_to_all x1, blocking collectives, body(): lax.all_to_all(tile, COL, split_axis=1, concat_axis=1, tiled=True)  32.4 us
    add x2, other arithmetic, body(): t3 = dot(lall[0] + lall[1], rsum)  27.7 us
    gather x2, local copies, waits for them, and re-layouts, permute_left(): return jnp.take(y, jnp.take(idx, pos), axis=1)  10.3 us
  transfers between devices with their start and end apart: 6, of which 5 were waited for; matrix products, arithmetic and copies ran while one was open for 22% of the time, Pallas kernels for 0%

profile of v5, /device:TPU:1, one launch (start us, length us, event | category | flops | bytes accessed | tf_op | source)
XLA Modules:
  0.0 404.6 jit_solution(8222940412952827119)
XLA Ops:
  10.6 8.3 %all-to-all-start = ((f32[2,8,8,16,160]{4,3,1,0,2:T(8,128)}), f32[2,8,8,16,160]{4,3,1,0,2:T(8,128)S(1)}, u32[]{:S(2)}, u32[]{:S(2)}) async-start(f32[2,8,8,16,160]{4,3,1,0,2:T(8,128)} %copy.36), calls=%async_computation | async-start | bytes 4194304 | tf_op jit(solution)/shard_map/all_to_all | solution.py:37
  19.4 39.1 %all-to-all-done = f32[2,8,8,16,160]{4,3,1,0,2:T(8,128)S(1)} async-done(((f32[2,8,8,16,160]{4,3,1,0,2:T(8,128)}), f32[2,8,8,16,160]{4,3,1,0,2:T(8,128)S(1)}, u32[]{:S(2)}, u32[]{:S(2)}) %all-to-all-start) | async-done | bytes 1310752 | tf_op jit(solution)/shard_map/all_to_all | solution.py:37
  60.0 2.3 gather_fusion.1
  63.8 4.0 all-to-all-start.1
  67.9 4.5 %gather_fusion = s32[1024]{0:T(1024)S(1)} fusion(s32[1024]{0:T(1024)S(1)} %add_bitcast_fusion, s32[1024]{0:T(1024)S(1)} %broadcast_clamp_fusion.1), kind=kCustom, calls=%fused_computation | custom fusion | bytes 12288 | tf_op jit(solution)/shard_map/jit(_take)/gather | solution.py:53
  72.5 32.4 %all-to-all-done.1 = f32[2,8,8,16,160]{4,3,2,0,1:T(8,128)S(1)} async-done(((f32[2,8,8,16,160]{4,3,2,0,1:T(8,128)}), f32[2,8,8,16,160]{4,3,2,0,1:T(8,128)S(1)}, u32[]{:S(2)}, u32[]{:S(2)}) %all-to-all-start.1) | async-done | bytes 1310752 | tf_op jit(solution)/shard_map/all_to_all | solution.py:43
  105.1 2.9 copy.40
  108.1 5.8 %gather_fusion.2 = f32[1024,2,160]{2,1,0:T(2,128)S(1)} fusion(f32[2,1024,160]{2,0,1:T(2,128)} %copy.40, s32[1024]{0:T(1024)S(1)} %broadcast_clamp_fusion), kind=kCustom, calls=%fused_computation.2 | custom fusion | bytes 2625536 | tf_op jit(solution)/shard_map/jit(_take)/gather | solution.py:53
  113.9 4.5 %select_bitcast_fusion = f32[2,160,1024]{1,0,2:T(2,128)} fusion(f32[1024,2,160]{2,1,0:T(2,128)S(1)} %gather_fusion.2, pred[1024]{0:T(1024)(128)(4,1)S(1)} %compare_and_fusion.1), kind=kLoop, calls=%fused_computation.36 | loop fusion | flops 327680 | bytes 2622464 | tf_op jit(solution)/shard_map/jit(_take)/select_n | solution.py:53
  118.3 50.6 %all-gather.4.cloned.1.call-done = f32[2,2560,512]{2,1,0:T(8,128)} async-done(((f32[2,320,512]{2,1,0:T(8,128)}), f32[2,2560,512]{2,1,0:T(8,128)}) %all-gather.4.cloned.1.call-update) | async-done | bytes 10485776 | tf_op jit(solution)/shard_map/all_gather | solution.py:61
  173.1 60.1 %all-gather.6.cloned.1.call-done = f32[2,2560,512]{2,0,1:T(2,128)} async-done(((f32[2,160,512]{2,0,1:T(2,128)}), f32[2,2560,512]{2,0,1:T(2,128)}) %all-gather.6.cloned.1.call-update) | async-done | bytes 10485776 | tf_op jit(solution)/shard_map/all_gather | solution.py:77
  235.1 14.6 %slice_add_fusion.4 = (f32[1,2560,512]{2,0,1:T(1,128)S(1)}, f32[1,2560,512]{2,0,1:T(1,128)S(1)}, f32[1,2560,512]{2,0,1:T(1,128)S(1)}) fusion(f32[2,2560,512]{2,0,1:T(2,128)} %all-gather.6.cloned.1.call-done), kind=kLoop, calls=%fused_computation.127 | loop fusion | flops 1310720 | bytes 26214400 | tf_op jit(solution)/shard_map/add | solution.py:81
  249.7 4.3 %fusion.12 = f32[512,512]{1,0:T(8,128)S(1)} fusion(f32[1,2560,512]{2,0,1:T(1,128)S(1)} %get-tuple-element.10, f32[2,2560,512]{2,1,0:T(8,128)S(1)} %bitcast.106), kind=kOutput, calls=%fused_computation.15 | convolution fusion | flops 4026531840 | bytes 11534336 | tf_op jit(solution)/shard_map/dot_general | solution.py:69
  254.0 4.3 %fusion.81 = (f32[512,512]{1,0:T(8,128)S(1)}, f32[512,512]{1,0:T(8,128)S(1)}) fusion(f32[512,512]{1,0:T(8,128)S(1)} %fusion.12, f32[2,2560,512]{2,1,0:T(8,128)S(1)} %bitcast.106, f32[1,2560,512]{2,0,1:T(1,128)S(1)} %get-tuple-element.11), kind=kOutput, calls=%fused_computation.130 | convolution fusion | flops 4026793984 | bytes 13631488 | tf_op jit(solution)/shard_map/dot_general | solution.py:69
  258.3 4.6 %fusion.33 = f32[512,512]{1,0:T(8,128)S(1)} fusion(f32[512,512]{1,0:T(8,128)S(1)} %fusion.12, f32[512,512]{1,0:T(8,128)S(1)} %get-tuple-element.22, f32[2,2560,512]{2,1,0:T(8,128)S(1)} %bitcast.106, f32[1,2560,512]{2,0,1:T(1,128)S(1)} %get-tuple-element.9), kind=kOutput, calls=%fused_computation.38 | convolution fusion | flops 4028366848 | bytes 18874368 | tf_op jit(solution)/shard_map/dot_general | solution.py:69
  264.4 5.1 %all-to-all-start.2 = ((f32[2,16,32,512]{3,2,0,1:T(8,128)}), f32[2,16,32,512]{3,2,0,1:T(8,128)}, u32[]{:S(2)}, u32[]{:S(2)}) async-start(f32[2,16,32,512]{3,2,0,1:T(8,128)} %pad_maximum_fusion), calls=%async_computation.2 | async-start | bytes 4194304 | tf_op jit(solution)/shard_map/all_to_all | solution.py:84
  269.5 51.3 %all-gather.8.cloned.1.call-done = f32[2,2560,512]{2,0,1:T(2,128)} async-done(((f32[2,160,512]{2,0,1:T(2,128)}), f32[2,2560,512]{2,0,1:T(2,128)}) %all-gather.8.cloned.1.call-update) | async-done | bytes 10485776 | tf_op jit(solution)/shard_map/all_gather | solution.py:77
  320.7 13.1 %slice_add_fusion.3 = (f32[1,2560,512]{2,0,1:T(1,128)S(1)}, f32[1,2560,512]{2,0,1:T(1,128)S(1)}, f32[1,2560,512]{2,0,1:T(1,128)S(1)}) fusion(f32[2,2560,512]{2,0,1:T(2,128)} %all-gather.8.cloned.1.call-done), kind=kLoop, calls=%fused_computation.126 | loop fusion | flops 1310720 | bytes 26214400 | tf_op jit(solution)/shard_map/add | solution.py:81
  333.9 11.0 %fusion.3 = f32[512,512]{1,0:T(8,128)S(1)} fusion(f32[1,2560,512]{2,0,1:T(1,128)S(1)} %get-tuple-element.13, f32[2,2560,512]{2,1,0:T(8,128)} %all-gather.4.cloned.1.call-done), kind=kOutput, calls=%fused_computation.6 | convolution fusion | flops 4026531840 | bytes 11534336 | tf_op jit(solution)/shard_map/dot_general | solution.py:69
  344.9 4.3 %fusion.80 = (f32[512,512]{1,0:T(8,128)S(1)}, f32[512,512]{1,0:T(8,128)S(1)}) fusion(f32[512,512]{1,0:T(8,128)S(1)} %fusion.3, f32[2,2560,512]{2,1,0:T(8,128)S(1)} %bitcast.108, f32[1,2560,512]{2,0,1:T(1,128)S(1)} %get-tuple-element.14), kind=kOutput, calls=%fused_computation.129 | convolution fusion | flops 4026793984 | bytes 13631488 | tf_op jit(solution)/shard_map/dot_general | solution.py:69
  349.2 4.4 %fusion.43 = f32[512,512]{1,0:T(8,128)S(1)} fusion(f32[512,512]{1,0:T(8,128)S(1)} %fusion.3, f32[512,512]{1,0:T(8,128)S(1)} %get-tuple-element.20, f32[2,2560,512]{2,1,0:T(8,128)S(1)} %bitcast.108, f32[1,2560,512]{2,0,1:T(1,128)S(1)} %get-tuple-element.12), kind=kOutput, calls=%fused_computation.40 | convolution fusion | flops 4028366848 | bytes 18874368 | tf_op jit(solution)/shard_map/dot_general | solution.py:69
  353.9 32.4 %all_to_all.20 = f32[2,16,32,512]{3,2,0,1:T(8,128)S(1)} all-to-all(f32[2,16,32,512]{3,2,0,1:T(8,128)S(1)} %pad_maximum_fusion.1), channel_id=1, replica_groups=mesh['xh'=2,'z'=4,'xl'=2,'y'=4,'core'=2] {'xl','y','core'}, dimensions={1} | all-to-all | bytes 4194304 | tf_op jit(solution)/shard_map/all_to_all | solution.py:84
  388.5 4.4 %copy.47 = f32[2,2,32,16,512]{4,3,2,1,0:T(8,128)} copy(f32[2,2,32,16,512]{4,2,0,3,1:T(8,128)S(1)} %maximum_bitcast_fusion) | data formatting | bytes 8388608 | tf_op jit(solution)/shard_map/transpose | solution.py:86
  392.8 4.9 %reshape.365 = f32[2,64,8192]{2,1,0:T(8,128)} reshape(f32[2,2,32,16,512]{4,3,2,1,0:T(8,128)} %copy.47) | data formatting | bytes 8388608 | tf_op jit(solution)/shard_map/reshape | solution.py:87
  (51 shorter events, 17.8 us)
Async XLA Ops:
  6.5 162.4 %all-gather.4.cloned.1.call-start = ((), (), s32[]{:S(2)}) async-start(), calls=%async_computation.4 | async-start | bytes 11796480 | tf_op jit(solution)/shard_map/all_gather | solution.py:61
  7.3 11.7 %copy-start = (s32[64]{0:T(128)S(1)}, s32[64]{0:T(128)}, u32[]{:S(2)}) copy-start(s32[64]{0:T(128)} %param.6) | copy-start | bytes 772
  7.3 12.0 %copy-start.1 = (s32[7]{0:T(128)S(1)}, s32[7]{0:T(128)}, u32[]{:S(2)}) copy-start(s32[7]{0:T(128)} %param.7) | copy-start | bytes 88
  10.6 47.8 %all-to-all-start = ((f32[2,8,8,16,160]{4,3,1,0,2:T(8,128)}), f32[2,8,8,16,160]{4,3,1,0,2:T(8,128)S(1)}, u32[]{:S(2)}, u32[]{:S(2)}) async-start(f32[2,8,8,16,160]{4,3,1,0,2:T(8,128)} %copy.36), calls=%async_computation | async-start | bytes 4194304 | tf_op jit(solution)/shard_map/all_to_all | solution.py:37
  63.8 41.2 %all-to-all-start.1 = ((f32[2,8,8,16,160]{4,3,2,0,1:T(8,128)}), f32[2,8,8,16,160]{4,3,2,0,1:T(8,128)S(1)}, u32[]{:S(2)}, u32[]{:S(2)}) async-start(f32[2,8,8,16,160]{4,3,2,0,1:T(8,128)} %copy_select_fusion), calls=%async_computation.1 | async-start | bytes 4194304 | tf_op jit(solution)/shard_map/all_to_all | solution.py:43
  67.8 165.4 %all-gather.6.cloned.1.call-start = ((), (), s32[]{:S(2)}) async-start(), calls=%async_computation.5 | async-start | bytes 11141120 | tf_op jit(solution)/shard_map/all_gather | solution.py:77
  173.1 147.7 %all-gather.8.cloned.1.call-start = ((), (), s32[]{:S(2)}) async-start(), calls=%async_computation.6 | async-start | bytes 11141120 | tf_op jit(solution)/shard_map/all_gather | solution.py:77
  235.0 14.7 %slice-start = ((s8[10485760]{0:T(1024)(128)(4,1)}), s8[2097152]{0:T(1024)(128)(4,1)S(1)}, s32[]{:S(2)}) async-start(s8[10485760]{0:T(1024)(128)(4,1)} %bitcast.105), calls=%async_computation.7 | async-start | bytes 4194304
  235.1 14.7 %slice-start.1 = ((s8[10485760]{0:T(1024)(128)(4,1)}), s8[4194304]{0:T(1024)(128)(4,1)S(1)}, s32[]{:S(2)}) async-start(s8[10485760]{0:T(1024)(128)(4,1)} %bitcast.105), calls=%async_computation.8 | async-start | bytes 8388608
  235.1 14.7 %slice-start.2 = ((s8[10485760]{0:T(1024)(128)(4,1)}), s8[4194304]{0:T(1024)(128)(4,1)S(1)}, s32[]{:S(2)}) async-start(s8[10485760]{0:T(1024)(128)(4,1)} %bitcast.105), calls=%async_computation.9 | async-start | bytes 8388608
  264.4 89.5 %all-to-all-start.2 = ((f32[2,16,32,512]{3,2,0,1:T(8,128)}), f32[2,16,32,512]{3,2,0,1:T(8,128)}, u32[]{:S(2)}, u32[]{:S(2)}) async-start(f32[2,16,32,512]{3,2,0,1:T(8,128)} %pad_maximum_fusion), calls=%async_computation.2 | async-start | bytes 4194304 | tf_op jit(solution)/shard_map/all_to_all | solution.py:84
  320.7 24.2 %slice-start.3 = ((s8[10485760]{0:T(1024)(128)(4,1)}), s8[4194304]{0:T(1024)(128)(4,1)S(1)}, s32[]{:S(2)}) async-start(s8[10485760]{0:T(1024)(128)(4,1)} %bitcast.107), calls=%async_computation.10 | async-start | bytes 8388608
  320.7 24.2 %slice-start.4 = ((s8[10485760]{0:T(1024)(128)(4,1)}), s8[4194304]{0:T(1024)(128)(4,1)S(1)}, s32[]{:S(2)}) async-start(s8[10485760]{0:T(1024)(128)(4,1)} %bitcast.107), calls=%async_computation.11 | async-start | bytes 8388608
  333.9 11.1 %slice-start.5 = ((s8[10485760]{0:T(1024)(128)(4,1)}), s8[2097152]{0:T(1024)(128)(4,1)S(1)}, s32[]{:S(2)}) async-start(s8[10485760]{0:T(1024)(128)(4,1)} %bitcast.107), calls=%async_computation.12 | async-start | bytes 4194304
Sparse Core Ops, SparseCore 0:
  9.7 159.2 all-gather.3
  173.2 59.9 all-gather.5
  235.2 85.5 all-gather.7

commit v6 on v5

--- a/solution.py
+++ b/solution.py
@@ -67,7 +67,6 @@
     high = lax.Precision.HIGH
     dims = (((0,), (0,)), ((), ()))
     dot = lambda a, b: lax.dot_general(a, b, dims, preferred_element_type=jnp.float32, precision=high)
-    rsum = rall[0] + rall[1]
     outs = []
     prev = None
     for h in range(halves):
@@ -76,14 +75,12 @@
             piece = lax.optimization_barrier((piece, prev))[0]
         lall = lax.all_gather(piece, COL, axis=1, tiled=True)
         prev = lall
-        t1 = dot(lall[0], rall[0])
-        t2 = dot(lall[1], rall[1])
-        t3 = dot(lall[0] + lall[1], rsum)
-        tile = jnp.stack([t1 - t2, t3 - t1 - t2], axis=0)
+        re = dot(lall[0], rall[0]) - dot(lall[1], rall[1])
+        im = dot(lall[0], rall[1]) + dot(lall[1], rall[0])
+        tile = jnp.stack([re, im], axis=0)
         tile = tile.reshape(2, col_count, part // col_count, cols)
-        outs.append(lax.all_to_all(tile, COL, split_axis=1, concat_axis=1, tiled=True))
-    out = jnp.stack(outs, axis=1)
-    out = jnp.transpose(out, (0, 1, 3, 2, 4))
+        outs.append(lax.all_to_all(tile, COL, split_axis=1, concat_axis=3, tiled=True))
+    out = jnp.concatenate(outs, axis=1)
     return out.reshape(2, rows // col_count, col_count * cols)
 
 

time: 411 us -> 411 us (level)
  blocking collectives: 32.4 us -> 0 us
  other arithmetic: 38.1 us -> 9.8 us
  waiting for transfers between devices: 234 us -> 258 us
  local copies, waits for them, and re-layouts: 36 us -> 58.5 us
  matrix products: 32.8 us -> 42.1 us
  starting transfers between devices: 17.5 us -> 23.1 us
    all_to_all x1 -> x0, blocking collectives: 32.4 us -> none  [body(): lax.all_to_all(tile, COL, split_axis=1, concat_axis=1, tiled=True)]
    add x2 -> x0, other arithmetic: 27.7 us -> none  [body(): t3 = dot(lall[0] + lall[1], rsum)]
    all_to_all x1 -> x2, waiting for transfers between devices: 0.01 us -> 26.6 us  [body(): lax.all_to_all(tile, COL, split_axis=1, concat_axis=3, tiled=True)]
    slice x0 -> x2, local copies, waits for them, and re-layouts: none -> 26.3 us  [body(): re = dot(lall[0], rall[0]) - dot(lall[1], rall[1])]
    dot_general x6 -> x8, matrix products: 32.8 us -> 42.1 us  [body(): lax.dot_general(a, b, dims, preferred_element_type=jnp.float32, precision...]
    all_to_all x1 -> x2, starting transfers between devices: 5.06 us -> 10.7 us  [body(): lax.all_to_all(tile, COL, split_axis=1, concat_axis=3, tiled=True)]
    reshape x1 -> x0, local copies, waits for them, and re-layouts: 4.94 us -> none  [body(): return out.reshape(2, rows // col_count, col_count * cols)]
    transpose x1 -> x0, local copies, waits for them, and re-layouts: 4.39 us -> none  [body(): out = jnp.transpose(out, (0, 1, 3, 2, 4))]
  transfers between devices with their start and end apart: 6 -> 7, of which waited for: 5 -> 6; matrix products, arithmetic and copies ran while one was open for 22% -> 25% of each run, Pallas kernels for 0% -> 0%
where the time goes in v6:
time: 411 us; the launch traced here: 405 us
  waiting for transfers between devices  258 us (63%)
  local copies, waits for them, and re-layouts  58.5 us (14%)
  matrix products  42.1 us (10%)
  starting transfers between devices  23.1 us (6%)
  between operations  13.7 us (3%)
  other arithmetic  9.8 us (2%)
    all_gather x2, waiting for transfers between devices, body(): lall = lax.all_gather(piece, COL, axis=1, tiled=True)  108 us
    all_gather x1, waiting for transfers between devices, body(): rall = lax.all_gather(right, ROW, axis=1, tiled=True)  50.6 us
    dot_general x8, matrix products, body(): lax.dot_general(a, b, dims, preferred_element_type=jnp.float32, precision...  42.1 us
    all_to_all x1, waiting for transfers between devices, permute_left(): x = lax.all_to_all(x, ROW, split_axis=2, concat_axis=2, tiled=True)  39.1 us
    all_to_all x1, waiting for transfers between devices, permute_left(): y = lax.all_to_all(y, ROW, split_axis=1, concat_axis=1, tiled=True)  32.4 us
    all_to_all x2, waiting for transfers between devices, body(): lax.all_to_all(tile, COL, split_axis=1, concat_axis=3, tiled=True)  26.6 us
    slice x2, local copies, waits for them, and re-layouts, body(): re = dot(lall[0], rall[0]) - dot(lall[1], rall[1])  26.3 us
    all_to_all x2, starting transfers between devices, body(): lax.all_to_all(tile, COL, split_axis=1, concat_axis=3, tiled=True)  10.7 us
  transfers between devices with their start and end apart: 7, of which 6 were waited for; matrix products, arithmetic and copies ran while one was open for 25% of the time, Pallas kernels for 0%

profile of v6, /device:TPU:1, one launch (start us, length us, event | category | flops | bytes accessed | tf_op | source)
XLA Modules:
  0.0 404.8 jit_solution(9216417836134505769)
XLA Ops:
  10.6 8.3 %all-to-all-start = ((f32[2,8,8,16,160]{4,3,1,0,2:T(8,128)}), f32[2,8,8,16,160]{4,3,1,0,2:T(8,128)S(1)}, u32[]{:S(2)}, u32[]{:S(2)}) async-start(f32[2,8,8,16,160]{4,3,1,0,2:T(8,128)} %copy.36), calls=%async_computation | async-start | bytes 4194304 | tf_op jit(solution)/shard_map/all_to_all | solution.py:37
  19.4 39.1 %all-to-all-done = f32[2,8,8,16,160]{4,3,1,0,2:T(8,128)S(1)} async-done(((f32[2,8,8,16,160]{4,3,1,0,2:T(8,128)}), f32[2,8,8,16,160]{4,3,1,0,2:T(8,128)S(1)}, u32[]{:S(2)}, u32[]{:S(2)}) %all-to-all-start) | async-done | bytes 1310752 | tf_op jit(solution)/shard_map/all_to_all | solution.py:37
  63.8 4.0 all-to-all-start.1
  67.9 4.5 %gather_fusion = s32[1024]{0:T(1024)S(1)} fusion(s32[1024]{0:T(1024)S(1)} %add_bitcast_fusion, s32[1024]{0:T(1024)S(1)} %broadcast_clamp_fusion.1), kind=kCustom, calls=%fused_computation | custom fusion | bytes 12288 | tf_op jit(solution)/shard_map/jit(_take)/gather | solution.py:53
  72.5 32.4 %all-to-all-done.1 = f32[2,8,8,16,160]{4,3,2,0,1:T(8,128)S(1)} async-done(((f32[2,8,8,16,160]{4,3,2,0,1:T(8,128)}), f32[2,8,8,16,160]{4,3,2,0,1:T(8,128)S(1)}, u32[]{:S(2)}, u32[]{:S(2)}) %all-to-all-start.1) | async-done | bytes 1310752 | tf_op jit(solution)/shard_map/all_to_all | solution.py:43
  105.1 2.9 copy.40
  108.1 5.8 %gather_fusion.2 = f32[1024,2,160]{2,1,0:T(2,128)S(1)} fusion(f32[2,1024,160]{2,0,1:T(2,128)} %copy.40, s32[1024]{0:T(1024)S(1)} %broadcast_clamp_fusion), kind=kCustom, calls=%fused_computation.2 | custom fusion | bytes 2625536 | tf_op jit(solution)/shard_map/jit(_take)/gather | solution.py:53
  113.9 4.5 %select_bitcast_fusion = f32[2,160,1024]{1,0,2:T(2,128)} fusion(f32[1024,2,160]{2,1,0:T(2,128)S(1)} %gather_fusion.2, pred[1024]{0:T(1024)(128)(4,1)S(1)} %compare_and_fusion.1), kind=kLoop, calls=%fused_computation.33 | loop fusion | flops 327680 | bytes 2622464 | tf_op jit(solution)/shard_map/jit(_take)/select_n | solution.py:53
  118.3 50.6 %all-gather.4.cloned.1.call-done = f32[2,2560,512]{2,1,0:T(8,128)} async-done(((f32[2,320,512]{2,1,0:T(8,128)}), f32[2,2560,512]{2,1,0:T(8,128)}) %all-gather.4.cloned.1.call-update) | async-done | bytes 10485776 | tf_op jit(solution)/shard_map/all_gather | solution.py:61
  173.1 60.1 %all-gather.6.cloned.1.call-done = f32[2,2560,512]{2,0,1:T(2,128)} async-done(((f32[2,160,512]{2,0,1:T(2,128)}), f32[2,2560,512]{2,0,1:T(2,128)}) %all-gather.6.cloned.1.call-update) | async-done | bytes 10485776 | tf_op jit(solution)/shard_map/all_gather | solution.py:76
  235.0 13.6 %fusion.67 = (f32[1,2560,512]{2,0,1:T(1,128)S(1)}, f32[1,2560,512]{2,0,1:T(1,128)S(1)}) fusion(f32[2,2560,512]{2,0,1:T(2,128)} %all-gather.6.cloned.1.call-done), kind=kLoop, calls=%fused_computation.123 | loop fusion | bytes 20971520 | tf_op jit(solution)/shard_map/slice | solution.py:78
  248.7 4.3 %fusion.10 = f32[512,512]{1,0:T(8,128)S(1)} fusion(f32[1,2560,512]{2,0,1:T(1,128)S(1)} %get-tuple-element.10, f32[2,2560,512]{2,1,0:T(8,128)S(1)} %bitcast.102), kind=kOutput, calls=%fused_computation.15 | convolution fusion | flops 4026531840 | bytes 11534336 | tf_op jit(solution)/shard_map/dot_general | solution.py:69
  253.0 4.3 %fusion.8 = f32[512,512]{1,0:T(8,128)S(1)} fusion(f32[1,2560,512]{2,0,1:T(1,128)S(1)} %get-tuple-element.10, f32[2,2560,512]{2,1,0:T(8,128)S(1)} %bitcast.102), kind=kOutput, calls=%fused_computation.13 | convolution fusion | flops 4026531840 | bytes 11534336 | tf_op jit(solution)/shard_map/dot_general | solution.py:69
  257.3 4.5 %fusion.24 = f32[512,512]{1,0:T(8,128)S(1)} fusion(f32[512,512]{1,0:T(8,128)S(1)} %fusion.10, f32[2,2560,512]{2,1,0:T(8,128)S(1)} %bitcast.102, f32[1,2560,512]{2,0,1:T(1,128)S(1)} %get-tuple-element.9), kind=kOutput, calls=%fused_computation.34 | convolution fusion | flops 4026793984 | bytes 12582912 | tf_op jit(solution)/shard_map/dot_general | solution.py:69
  261.7 4.3 %fusion.27 = f32[512,512]{1,0:T(8,128)S(1)} fusion(f32[512,512]{1,0:T(8,128)S(1)} %fusion.8, f32[2,2560,512]{2,1,0:T(8,128)S(1)} %bitcast.102, f32[1,2560,512]{2,0,1:T(1,128)S(1)} %get-tuple-element.9), kind=kOutput, calls=%fused_computation.35 | convolution fusion | flops 4026793984 | bytes 12582912 | tf_op jit(solution)/shard_map/dot_general | solution.py:69
  267.6 5.1 %all-to-all-start.2 = ((f32[2,16,32,512]{3,2,0,1:T(8,128)}), f32[2,16,32,512]{3,2,0,1:T(8,128)S(1)}, u32[]{:S(2)}, u32[]{:S(2)}) async-start(f32[2,16,32,512]{3,2,0,1:T(8,128)} %pad_maximum_fusion.1), calls=%async_computation.2 | async-start | bytes 4194304 | tf_op jit(solution)/shard_map/all_to_all | solution.py:82
  272.6 48.1 %all-gather.8.cloned.1.call-done = f32[2,2560,512]{2,0,1:T(2,128)} async-done(((f32[2,160,512]{2,0,1:T(2,128)}), f32[2,2560,512]{2,0,1:T(2,128)}) %all-gather.8.cloned.1.call-update) | async-done | bytes 10485776 | tf_op jit(solution)/shard_map/all_gather | solution.py:76
  320.8 12.7 %fusion.68 = (f32[1,2560,512]{2,0,1:T(1,128)S(1)}, f32[1,2560,512]{2,0,1:T(1,128)S(1)}) fusion(f32[2,2560,512]{2,0,1:T(2,128)} %all-gather.8.cloned.1.call-done), kind=kLoop, calls=%fused_computation.124 | loop fusion | bytes 20971520 | tf_op jit(solution)/shard_map/slice | solution.py:78
  333.5 11.0 %fusion.2 = f32[512,512]{1,0:T(8,128)S(1)} fusion(f32[1,2560,512]{2,0,1:T(1,128)S(1)} %get-tuple-element.12, f32[2,2560,512]{2,1,0:T(8,128)} %all-gather.4.cloned.1.call-done), kind=kOutput, calls=%fused_computation.7 | convolution fusion | flops 4026531840 | bytes 11534336 | tf_op jit(solution)/shard_map/dot_general | solution.py:69
  344.5 4.5 %fusion = f32[512,512]{1,0:T(8,128)S(1)} fusion(f32[1,2560,512]{2,0,1:T(1,128)S(1)} %get-tuple-element.12, f32[2,2560,512]{2,1,0:T(8,128)S(1)} %bitcast.104), kind=kOutput, calls=%fused_computation.5 | convolution fusion | flops 4026531840 | bytes 11534336 | tf_op jit(solution)/shard_map/dot_general | solution.py:69
  349.0 4.5 %fusion.30 = f32[512,512]{1,0:T(8,128)S(1)} fusion(f32[512,512]{1,0:T(8,128)S(1)} %fusion.2, f32[2,2560,512]{2,1,0:T(8,128)S(1)} %bitcast.104, f32[1,2560,512]{2,0,1:T(1,128)S(1)} %get-tuple-element.11), kind=kOutput, calls=%fused_computation.36 | convolution fusion | flops 4026793984 | bytes 12582912 | tf_op jit(solution)/shard_map/dot_general | solution.py:69
  353.5 4.8 %fusion.33 = f32[512,512]{1,0:T(8,128)S(1)} fusion(f32[512,512]{1,0:T(8,128)S(1)} %fusion, f32[2,2560,512]{2,1,0:T(8,128)S(1)} %bitcast.104, f32[1,2560,512]{2,0,1:T(1,128)S(1)} %get-tuple-element.11), kind=kOutput, calls=%fused_computation.37 | convolution fusion | flops 4026793984 | bytes 12582912 | tf_op jit(solution)/shard_map/dot_general | solution.py:69
  359.8 5.6 %all-to-all-start.3 = ((f32[2,16,32,512]{3,2,0,1:T(8,128)}), f32[2,16,32,512]{3,2,0,1:T(8,128)}, u32[]{:S(2)}, u32[]{:S(2)}) async-start(f32[2,16,32,512]{3,2,0,1:T(8,128)} %pad_maximum_fusion.2), calls=%async_computation.3 | async-start | bytes 4194304 | tf_op jit(solution)/shard_map/all_to_all | solution.py:82
  366.9 26.6 %all-to-all-done.3 = f32[2,16,32,512]{3,2,0,1:T(8,128)} async-done(((f32[2,16,32,512]{3,2,0,1:T(8,128)}), f32[2,16,32,512]{3,2,0,1:T(8,128)}, u32[]{:S(2)}, u32[]{:S(2)}) %all-to-all-start.3) | async-done | bytes 2097184 | tf_op jit(solution)/shard_map/all_to_all | solution.py:82
  (57 shorter events, 25.2 us)
Async XLA Ops:
  6.5 162.4 %all-gather.4.cloned.1.call-start = ((), (), s32[]{:S(2)}) async-start(), calls=%async_computation.4 | async-start | bytes 11796480 | tf_op jit(solution)/shard_map/all_gather | solution.py:61
  7.3 11.7 %copy-start.1 = (s32[64]{0:T(128)S(1)}, s32[64]{0:T(128)}, u32[]{:S(2)}) copy-start(s32[64]{0:T(128)} %param.6) | copy-start | bytes 772
  7.3 12.0 %copy-start.2 = (s32[7]{0:T(128)S(1)}, s32[7]{0:T(128)}, u32[]{:S(2)}) copy-start(s32[7]{0:T(128)} %param.7) | copy-start | bytes 88
  10.6 47.8 %all-to-all-start = ((f32[2,8,8,16,160]{4,3,1,0,2:T(8,128)}), f32[2,8,8,16,160]{4,3,1,0,2:T(8,128)S(1)}, u32[]{:S(2)}, u32[]{:S(2)}) async-start(f32[2,8,8,16,160]{4,3,1,0,2:T(8,128)} %copy.36), calls=%async_computation | async-start | bytes 4194304 | tf_op jit(solution)/shard_map/all_to_all | solution.py:37
  63.8 41.2 %all-to-all-start.1 = ((f32[2,8,8,16,160]{4,3,2,0,1:T(8,128)}), f32[2,8,8,16,160]{4,3,2,0,1:T(8,128)S(1)}, u32[]{:S(2)}, u32[]{:S(2)}) async-start(f32[2,8,8,16,160]{4,3,2,0,1:T(8,128)} %copy_select_fusion), calls=%async_computation.1 | async-start | bytes 4194304 | tf_op jit(solution)/shard_map/all_to_all | solution.py:43
  67.8 165.4 %all-gather.6.cloned.1.call-start = ((), (), s32[]{:S(2)}) async-start(), calls=%async_computation.5 | async-start | bytes 11141120 | tf_op jit(solution)/shard_map/all_gather | solution.py:76
  173.1 147.7 %all-gather.8.cloned.1.call-start = ((), (), s32[]{:S(2)}) async-start(), calls=%async_computation.6 | async-start | bytes 11141120 | tf_op jit(solution)/shard_map/all_gather | solution.py:76
  235.0 13.6 %slice-start = ((s8[10485760]{0:T(1024)(128)(4,1)}), s8[2097152]{0:T(1024)(128)(4,1)S(1)}, s32[]{:S(2)}) async-start(s8[10485760]{0:T(1024)(128)(4,1)} %bitcast.101), calls=%async_computation.7 | async-start | bytes 4194304
  235.0 13.6 %slice-start.1 = ((s8[10485760]{0:T(1024)(128)(4,1)}), s8[4194304]{0:T(1024)(128)(4,1)S(1)}, s32[]{:S(2)}) async-start(s8[10485760]{0:T(1024)(128)(4,1)} %bitcast.101), calls=%async_computation.8 | async-start | bytes 8388608
  235.0 13.6 %slice-start.2 = ((s8[10485760]{0:T(1024)(128)(4,1)}), s8[4194304]{0:T(1024)(128)(4,1)S(1)}, s32[]{:S(2)}) async-start(s8[10485760]{0:T(1024)(128)(4,1)} %bitcast.101), calls=%async_computation.9 | async-start | bytes 8388608
  267.6 92.2 %all-to-all-start.2 = ((f32[2,16,32,512]{3,2,0,1:T(8,128)}), f32[2,16,32,512]{3,2,0,1:T(8,128)S(1)}, u32[]{:S(2)}, u32[]{:S(2)}) async-start(f32[2,16,32,512]{3,2,0,1:T(8,128)} %pad_maximum_fusion.1), calls=%async_computation.2 | async-start | bytes 4194304 | tf_op jit(solution)/shard_map/all_to_all | solution.py:82
  320.8 23.7 %slice-start.3 = ((s8[10485760]{0:T(1024)(128)(4,1)}), s8[4194304]{0:T(1024)(128)(4,1)S(1)}, s32[]{:S(2)}) async-start(s8[10485760]{0:T(1024)(128)(4,1)} %bitcast.103), calls=%async_computation.10 | async-start | bytes 8388608
  320.8 23.8 %slice-start.4 = ((s8[10485760]{0:T(1024)(128)(4,1)}), s8[4194304]{0:T(1024)(128)(4,1)S(1)}, s32[]{:S(2)}) async-start(s8[10485760]{0:T(1024)(128)(4,1)} %bitcast.103), calls=%async_computation.11 | async-start | bytes 8388608
  333.5 11.1 %slice-start.5 = ((s8[10485760]{0:T(1024)(128)(4,1)}), s8[2097152]{0:T(1024)(128)(4,1)S(1)}, s32[]{:S(2)}) async-start(s8[10485760]{0:T(1024)(128)(4,1)} %bitcast.103), calls=%async_computation.12 | async-start | bytes 4194304
  359.8 33.7 %all-to-all-start.3 = ((f32[2,16,32,512]{3,2,0,1:T(8,128)}), f32[2,16,32,512]{3,2,0,1:T(8,128)}, u32[]{:S(2)}, u32[]{:S(2)}) async-start(f32[2,16,32,512]{3,2,0,1:T(8,128)} %pad_maximum_fusion.2), calls=%async_computation.3 | async-start | bytes 4194304 | tf_op jit(solution)/shard_map/all_to_all | solution.py:82
  366.9 28.4 %copy-start = (f32[1,16,2,4,8,512]{5,4,1,3,2,0:T(8,128)S(1)}, f32[1,16,2,4,8,512]{5,4,1,3,2,0:T(8,128)}, u32[]{:S(2)}) copy-start(f32[1,16,2,4,8,512]{5,4,1,3,2,0:T(8,128)} %copy.54) | copy-start | bytes 6291460
Sparse Core Ops, SparseCore 0:
  9.7 159.2 all-gather.3
  173.2 59.9 all-gather.5
  235.1 85.5 all-gather.7

commit v7 on v6

--- a/solution.py
+++ b/solution.py
@@ -71,12 +71,15 @@
     prev = None
     for h in range(halves):
         piece = lt[:, :, h * part:(h + 1) * part]
+        piece = jnp.swapaxes(piece, 0, 1).reshape(piece.shape[1], 2 * part)
         if prev is not None:
             piece = lax.optimization_barrier((piece, prev))[0]
-        lall = lax.all_gather(piece, COL, axis=1, tiled=True)
+        lall = lax.all_gather(piece, COL, axis=0, tiled=True)
         prev = lall
-        re = dot(lall[0], rall[0]) - dot(lall[1], rall[1])
-        im = dot(lall[0], rall[1]) + dot(lall[1], rall[0])
+        pr = dot(lall, rall[0])
+        pi = dot(lall, rall[1])
+        re = pr[:part] - pi[part:]
+        im = pi[:part] + pr[part:]
         tile = jnp.stack([re, im], axis=0)
         tile = tile.reshape(2, col_count, part // col_count, cols)
         outs.append(lax.all_to_all(tile, COL, split_axis=1, concat_axis=3, tiled=True))

time: 411 us -> 400 us (0.973); the launches traced: 405 us -> 399 us
  local copies, waits for them, and re-layouts: 58.5 us -> 32.2 us
  matrix products: 42.1 us -> 55 us
  waiting for transfers between devices: 258 us -> 264 us
    slice x4 -> x0, local copies, waits for them, and re-layouts: 30.4 us -> none  [the longest x2 26.3 us: body(): re = dot(lall[0], rall[0]) - dot(lall[1], rall[1])]
    dot_general x8 -> x4, matrix products: 42.1 us -> 55 us  [body(): lax.dot_general(a, b, dims, preferred_element_type=jnp.float32, precision...]
    all_gather x2, waiting for transfers between devices: 108 us -> 115 us  [body(): lall = lax.all_gather(piece, COL, axis=0, tiled=True)]
  transfers between devices with their start and end apart: 7 -> 7, of which waited for: 6 -> 6; matrix products, arithmetic and copies ran while one was open for 25% -> 22% of each run, Pallas kernels for 0% -> 0%
where the time goes in v7:
time: 400 us; the launch traced here: 399 us
  waiting for transfers between devices  264 us (66%)
  matrix products  55 us (14%)
  local copies, waits for them, and re-layouts  32.2 us (8%)
  starting transfers between devices  23.5 us (6%)
  between operations  13.4 us (3%)
  other arithmetic  10.7 us (3%)
    all_gather x2, waiting for transfers between devices, body(): lall = lax.all_gather(piece, COL, axis=0, tiled=True)  115 us
    dot_general x4, matrix products, body(): lax.dot_general(a, b, dims, preferred_element_type=jnp.float32, precision...  55 us
    all_gather x1, waiting for transfers between devices, body(): rall = lax.all_gather(right, ROW, axis=1, tiled=True)  50.9 us
    all_to_all x1, waiting for transfers between devices, permute_left(): x = lax.all_to_all(x, ROW, split_axis=2, concat_axis=2, tiled=True)  39.1 us
    all_to_all x1, waiting for transfers between devices, permute_left(): y = lax.all_to_all(y, ROW, split_axis=1, concat_axis=1, tiled=True)  32.1 us
    all_to_all x2, waiting for transfers between devices, body(): lax.all_to_all(tile, COL, split_axis=1, concat_axis=3, tiled=True)  26.6 us
    all_to_all x2, starting transfers between devices, body(): lax.all_to_all(tile, COL, split_axis=1, concat_axis=3, tiled=True)  10.8 us
    gather x2, local copies, waits for them, and re-layouts, permute_left(): return jnp.take(y, jnp.take(idx, pos), axis=1)  10.3 us
  transfers between devices with their start and end apart: 7, of which 6 were waited for; matrix products, arithmetic and copies ran while one was open for 22% of the time, Pallas kernels for 0%

profile of v7, /device:TPU:1, one launch (start us, length us, event | category | flops | bytes accessed | tf_op | source)
XLA Modules:
  0.0 399.2 jit_solution(9032665061973365983)
XLA Ops:
  8.7 1.6 copy.40
  10.2 8.5 %all-to-all-start = ((f32[2,8,8,16,160]{4,3,1,0,2:T(8,128)}), f32[2,8,8,16,160]{4,3,1,0,2:T(8,128)S(1)}, u32[]{:S(2)}, u32[]{:S(2)}) async-start(f32[2,8,8,16,160]{4,3,1,0,2:T(8,128)} %copy.40), calls=%async_computation | async-start | bytes 4194304 | tf_op jit(solution)/shard_map/all_to_all | solution.py:37
  19.1 39.1 %all-to-all-done = f32[2,8,8,16,160]{4,3,1,0,2:T(8,128)S(1)} async-done(((f32[2,8,8,16,160]{4,3,1,0,2:T(8,128)}), f32[2,8,8,16,160]{4,3,1,0,2:T(8,128)S(1)}, u32[]{:S(2)}, u32[]{:S(2)}) %all-to-all-start) | async-done | bytes 1310752 | tf_op jit(solution)/shard_map/all_to_all | solution.py:37
  58.1 1.6 copy.41
  59.7 2.3 gather_fusion.1
  63.5 4.0 all-to-all-start.1
  67.6 4.5 %gather_fusion = s32[1024]{0:T(1024)S(1)} fusion(s32[1024]{0:T(1024)S(1)} %add_bitcast_fusion, s32[1024]{0:T(1024)S(1)} %broadcast_clamp_fusion.1), kind=kCustom, calls=%fused_computation | custom fusion | bytes 12288 | tf_op jit(solution)/shard_map/jit(_take)/gather | solution.py:53
  72.2 32.1 %all-to-all-done.1 = f32[2,8,8,16,160]{4,3,2,0,1:T(8,128)S(1)} async-done(((f32[2,8,8,16,160]{4,3,2,0,1:T(8,128)}), f32[2,8,8,16,160]{4,3,2,0,1:T(8,128)S(1)}, u32[]{:S(2)}, u32[]{:S(2)}) %all-to-all-start.1) | async-done | bytes 1310752 | tf_op jit(solution)/shard_map/all_to_all | solution.py:43
  104.6 2.9 copy.44
  107.5 5.8 %gather_fusion.2 = f32[1024,2,160]{2,1,0:T(2,128)S(1)} fusion(f32[2,1024,160]{2,0,1:T(2,128)} %copy.44, s32[1024]{0:T(1024)S(1)} %broadcast_clamp_fusion), kind=kCustom, calls=%fused_computation.2 | custom fusion | bytes 2625536 | tf_op jit(solution)/shard_map/jit(_take)/gather | solution.py:53
  113.3 4.5 %select_bitcast_fusion = f32[2,160,1024]{1,0,2:T(2,128)} fusion(f32[1024,2,160]{2,1,0:T(2,128)S(1)} %gather_fusion.2, pred[1024]{0:T(1024)(128)(4,1)S(1)} %compare_and_fusion.1), kind=kLoop, calls=%fused_computation.13 | loop fusion | flops 327680 | bytes 2622464 | tf_op jit(solution)/shard_map/jit(_take)/select_n | solution.py:53
  117.8 50.9 %all-gather.4.cloned.1.call-done = f32[2,2560,512]{2,1,0:T(8,128)} async-done(((f32[2,320,512]{2,1,0:T(8,128)}), f32[2,2560,512]{2,1,0:T(8,128)}) %all-gather.4.cloned.1.call-update) | async-done | bytes 10485776 | tf_op jit(solution)/shard_map/all_gather | solution.py:61
  168.7 2.3 slice_bitcast_fusion.7
  174.8 58.1 %all-gather.6.cloned.1.call-done = f32[2560,1024]{1,0:T(8,128)} async-done(((f32[160,1024]{1,0:T(8,128)}), f32[2560,1024]{1,0:T(8,128)}) %all-gather.6.cloned.1.call-update) | async-done | bytes 10485776 | tf_op jit(solution)/shard_map/all_gather | solution.py:77
  232.9 12.1 %fusion.3 = f32[1024,512]{1,0:T(8,128)S(1)} fusion(f32[2560,1024]{1,0:T(8,128)} %all-gather.6.cloned.1.call-done, f32[2,2560,512]{2,1,0:T(8,128)} %all-gather.4.cloned.1.call-done), kind=kOutput, calls=%fused_computation.8 | convolution fusion | flops 8053063680 | bytes 17825792 | tf_op jit(solution)/shard_map/dot_general | solution.py:69
  245.1 11.1 %fusion.1 = f32[1024,512]{1,0:T(8,128)S(1)} fusion(f32[2560,1024]{1,0:T(8,128)} %all-gather.6.cloned.1.call-done, f32[2,2560,512]{2,1,0:T(8,128)S(1)} %bitcast.92), kind=kOutput, calls=%fused_computation.6 | convolution fusion | flops 8053063680 | bytes 17825792 | tf_op jit(solution)/shard_map/dot_general | solution.py:69
  258.1 5.2 %all-to-all-start.2 = ((f32[2,16,32,512]{3,2,0,1:T(8,128)}), f32[2,16,32,512]{3,2,0,1:T(8,128)S(1)}, u32[]{:S(2)}, u32[]{:S(2)}) async-start(f32[2,16,32,512]{3,2,0,1:T(8,128)} %pad_maximum_fusion.1), calls=%async_computation.2 | async-start | bytes 4194304 | tf_op jit(solution)/shard_map/all_to_all | solution.py:85
  263.3 56.9 %all-gather.8.cloned.1.call-done = f32[2560,1024]{1,0:T(8,128)} async-done(((f32[160,1024]{1,0:T(8,128)}), f32[2560,1024]{1,0:T(8,128)}) %all-gather.8.cloned.1.call-update) | async-done | bytes 10485776 | tf_op jit(solution)/shard_map/all_gather | solution.py:77
  320.2 12.4 %fusion.2 = f32[1024,512]{1,0:T(8,128)S(1)} fusion(f32[2560,1024]{1,0:T(8,128)} %all-gather.8.cloned.1.call-done, f32[2,2560,512]{2,1,0:T(8,128)} %all-gather.4.cloned.1.call-done), kind=kOutput, calls=%fused_computation.7 | convolution fusion | flops 8053063680 | bytes 17825792 | tf_op jit(solution)/shard_map/dot_general | solution.py:69
  332.7 19.4 %fusion = f32[1024,512]{1,0:T(8,128)S(1)} fusion(f32[2560,1024]{1,0:T(8,128)S(1)} %copy-done.2, f32[2,2560,512]{2,1,0:T(8,128)} %all-gather.4.cloned.1.call-done), kind=kOutput, calls=%fused_computation.5 | convolution fusion | flops 8053063680 | bytes 17825792 | tf_op jit(solution)/shard_map/dot_general | solution.py:69
  354.1 5.6 %all-to-all-start.3 = ((f32[2,16,32,512]{3,2,0,1:T(8,128)}), f32[2,16,32,512]{3,2,0,1:T(8,128)}, u32[]{:S(2)}, u32[]{:S(2)}) async-start(f32[2,16,32,512]{3,2,0,1:T(8,128)} %pad_maximum_fusion.2), calls=%async_computation.3 | async-start | bytes 4194304 | tf_op jit(solution)/shard_map/all_to_all | solution.py:85
  361.2 26.6 %all-to-all-done.3 = f32[2,16,32,512]{3,2,0,1:T(8,128)} async-done(((f32[2,16,32,512]{3,2,0,1:T(8,128)}), f32[2,16,32,512]{3,2,0,1:T(8,128)}, u32[]{:S(2)}, u32[]{:S(2)}) %all-to-all-start.3) | async-done | bytes 2097184 | tf_op jit(solution)/shard_map/all_to_all | solution.py:85
  387.8 2.0 copy.55
  390.4 2.3 copy.53
  (52 shorter events, 14.4 us)
Async XLA Ops:
  6.5 1.3 copy-start.1
  6.5 162.1 %all-gather.4.cloned.1.call-start = ((), (), s32[]{:S(2)}) async-start(), calls=%async_computation.4 | async-start | bytes 11796480 | tf_op jit(solution)/shard_map/all_gather | solution.py:61
  10.2 8.5 %copy-start.3 = (s32[64]{0:T(128)S(1)}, s32[64]{0:T(128)}, u32[]{:S(2)}) copy-start(s32[64]{0:T(128)} %param.6) | copy-start | bytes 772
  10.2 8.7 %copy-start.4 = (s32[7]{0:T(128)S(1)}, s32[7]{0:T(128)}, u32[]{:S(2)}) copy-start(s32[7]{0:T(128)} %param.7) | copy-start | bytes 88
  10.2 47.9 %all-to-all-start = ((f32[2,8,8,16,160]{4,3,1,0,2:T(8,128)}), f32[2,8,8,16,160]{4,3,1,0,2:T(8,128)S(1)}, u32[]{:S(2)}, u32[]{:S(2)}) async-start(f32[2,8,8,16,160]{4,3,1,0,2:T(8,128)} %copy.40), calls=%async_computation | async-start | bytes 4194304 | tf_op jit(solution)/shard_map/all_to_all | solution.py:37
  63.5 40.9 %all-to-all-start.1 = ((f32[2,8,8,16,160]{4,3,2,0,1:T(8,128)}), f32[2,8,8,16,160]{4,3,2,0,1:T(8,128)S(1)}, u32[]{:S(2)}, u32[]{:S(2)}) async-start(f32[2,8,8,16,160]{4,3,2,0,1:T(8,128)} %copy_select_fusion), calls=%async_computation.1 | async-start | bytes 4194304 | tf_op jit(solution)/shard_map/all_to_all | solution.py:43
  67.5 165.4 %all-gather.6.cloned.1.call-start = ((), (), s32[]{:S(2)}) async-start(), calls=%async_computation.5 | async-start | bytes 11141120 | tf_op jit(solution)/shard_map/all_gather | solution.py:77
  172.8 147.4 %all-gather.8.cloned.1.call-start = ((), (), s32[]{:S(2)}) async-start(), calls=%async_computation.6 | async-start | bytes 11141120 | tf_op jit(solution)/shard_map/all_gather | solution.py:77
  232.9 12.1 %slice-start = ((s8[10485760]{0:T(1024)(128)(4,1)}), s8[2097152]{0:T(1024)(128)(4,1)S(1)}, s32[]{:S(2)}) async-start(s8[10485760]{0:T(1024)(128)(4,1)} %bitcast.91), calls=%async_computation.7 | async-start | bytes 4194304
  232.9 12.1 %slice-start.1 = ((s8[10485760]{0:T(1024)(128)(4,1)}), s8[4194304]{0:T(1024)(128)(4,1)S(1)}, s32[]{:S(2)}) async-start(s8[10485760]{0:T(1024)(128)(4,1)} %bitcast.91), calls=%async_computation.8 | async-start | bytes 8388608
  232.9 12.1 %slice-start.2 = ((s8[10485760]{0:T(1024)(128)(4,1)}), s8[4194304]{0:T(1024)(128)(4,1)S(1)}, s32[]{:S(2)}) async-start(s8[10485760]{0:T(1024)(128)(4,1)} %bitcast.91), calls=%async_computation.9 | async-start | bytes 8388608
  258.1 95.9 %all-to-all-start.2 = ((f32[2,16,32,512]{3,2,0,1:T(8,128)}), f32[2,16,32,512]{3,2,0,1:T(8,128)S(1)}, u32[]{:S(2)}, u32[]{:S(2)}) async-start(f32[2,16,32,512]{3,2,0,1:T(8,128)} %pad_maximum_fusion.1), calls=%async_computation.2 | async-start | bytes 4194304 | tf_op jit(solution)/shard_map/all_to_all | solution.py:85
  320.2 12.5 %copy-start.2 = (f32[2560,1024]{1,0:T(8,128)S(1)}, f32[2560,1024]{1,0:T(8,128)}, u32[]{:S(2)}) copy-start(f32[2560,1024]{1,0:T(8,128)} %all-gather.8.cloned.1.call-done) | copy-start | bytes 31457284
  354.1 33.7 %all-to-all-start.3 = ((f32[2,16,32,512]{3,2,0,1:T(8,128)}), f32[2,16,32,512]{3,2,0,1:T(8,128)}, u32[]{:S(2)}, u32[]{:S(2)}) async-start(f32[2,16,32,512]{3,2,0,1:T(8,128)} %pad_maximum_fusion.2), calls=%async_computation.3 | async-start | bytes 4194304 | tf_op jit(solution)/shard_map/all_to_all | solution.py:85
  387.8 2.2 copy-start
Sparse Core Ops, SparseCore 0:
  9.7 158.9 all-gather.3
  172.9 59.9 all-gather.5
  234.6 85.5 all-gather.7

commit v8 on v7

--- a/solution.py
+++ b/solution.py
@@ -46,11 +46,22 @@
     o_local = jnp.arange(local, dtype=jnp.int32)
     idx = (s[None, :] // sub) * (local * sub) + o_local[:, None] * sub + s[None, :] % sub
     idx = idx.reshape(-1)
-    q = rows // col_count // 2
-    m = jnp.arange(rows, dtype=jnp.int32)
-    h, rest = m // (rows // 2), m % (rows // 2)
-    pos = (rest // q) * (2 * q) + h * q + rest % q
-    return jnp.take(y, jnp.take(idx, pos), axis=1)
+    return jnp.take(y, jnp.take(idx, part_order(rows, col_count)), axis=1)
+
+
+def part_sizes(q_total):
+    return [q_total // 2, q_total // 4, q_total - q_total // 2 - q_total // 4]
+
+
+def part_order(rows, col_count):
+    q_total = rows // col_count
+    pos = []
+    off = 0
+    for qp in part_sizes(q_total):
+        for c in range(col_count):
+            pos.extend(c * q_total + off + i for i in range(qp))
+        off += qp
+    return np.asarray(pos, np.int32)
 
 
 def body(left, right, prefix_owner, qubit_order):
@@ -61,16 +72,17 @@
     rall = lax.all_gather(right, ROW, axis=1, tiled=True)
     lp = permute_left(left, prefix_owner, qubit_order, row_count, col_count)
     lt = jnp.swapaxes(lp, 1, 2)
-    halves = 2
-    part = rows // halves
     lt = lax.optimization_barrier((lt, rall))[0]
     high = lax.Precision.HIGH
     dims = (((0,), (0,)), ((), ()))
     dot = lambda a, b: lax.dot_general(a, b, dims, preferred_element_type=jnp.float32, precision=high)
     outs = []
     prev = None
-    for h in range(halves):
-        piece = lt[:, :, h * part:(h + 1) * part]
+    start = 0
+    for qp in part_sizes(rows // col_count):
+        part = qp * col_count
+        piece = lt[:, :, start:start + part]
+        start += part
         piece = jnp.swapaxes(piece, 0, 1).reshape(piece.shape[1], 2 * part)
         if prev is not None:
             piece = lax.optimization_barrier((piece, prev))[0]
@@ -81,9 +93,9 @@
         re = pr[:part] - pi[part:]
         im = pi[:part] + pr[part:]
         tile = jnp.stack([re, im], axis=0)
-        tile = tile.reshape(2, col_count, part // col_count, cols)
+        tile = tile.reshape(2, col_count, qp, cols)
         outs.append(lax.all_to_all(tile, COL, split_axis=1, concat_axis=3, tiled=True))
-    out = jnp.concatenate(outs, axis=1)
+    out = jnp.concatenate(outs, axis=2)
     return out.reshape(2, rows // col_count, col_count * cols)
 
 

time: 400 us -> 408 us (1.020); the launches traced: 399 us -> 402 us
  waiting for transfers between devices: 264 us -> 238 us
  matrix products: 55 us -> 70.9 us
  starting transfers between devices: 23.5 us -> 33.3 us
    dot_general x4 -> x6, matrix products: 55 us -> 70.9 us  [body(): lax.dot_general(a, b, dims, preferred_element_type=jnp.float32, precision...]
    all_gather x2 -> x3, waiting for transfers between devices: 115 us -> 99.5 us  [body(): lall = lax.all_gather(piece, COL, axis=0, tiled=True)]
    all_to_all x2 -> x3, waiting for transfers between devices: 26.6 us -> 15.4 us  [body(): lax.all_to_all(tile, COL, split_axis=1, concat_axis=3, tiled=True)]
    all_to_all x2 -> x3, starting transfers between devices: 10.8 us -> 20.7 us  [body(): lax.all_to_all(tile, COL, split_axis=1, concat_axis=3, tiled=True)]
  transfers between devices with their start and end apart: 7 -> 9, of which waited for: 6 -> 8; matrix products, arithmetic and copies ran while one was open for 22% -> 27% of each run, Pallas kernels for 0% -> 0%
where the time goes in v8:
time: 408 us; the launch traced here: 402 us
  waiting for transfers between devices  238 us (58%)
  matrix products  70.9 us (17%)
  starting transfers between devices  33.3 us (8%)
  local copies, waits for them, and re-layouts  33.2 us (8%)
  between operations  13.7 us (3%)
  other arithmetic  13.2 us (3%)
    all_gather x3, waiting for transfers between devices, body(): lall = lax.all_gather(piece, COL, axis=0, tiled=True)  99.5 us
    dot_general x6, matrix products, body(): lax.dot_general(a, b, dims, preferred_element_type=jnp.float32, precision...  70.9 us
    all_gather x1, waiting for transfers between devices, body(): rall = lax.all_gather(right, ROW, axis=1, tiled=True)  50.6 us
    all_to_all x1, waiting for transfers between devices, permute_left(): x = lax.all_to_all(x, ROW, split_axis=2, concat_axis=2, tiled=True)  39.1 us
    all_to_all x1, waiting for transfers between devices, permute_left(): y = lax.all_to_all(y, ROW, split_axis=1, concat_axis=1, tiled=True)  32.5 us
    all_to_all x3, starting transfers between devices, body(): lax.all_to_all(tile, COL, split_axis=1, concat_axis=3, tiled=True)  20.7 us
    all_to_all x3, waiting for transfers between devices, body(): lax.all_to_all(tile, COL, split_axis=1, concat_axis=3, tiled=True)  15.4 us
    gather x2, local copies, waits for them, and re-layouts, permute_left(): return jnp.take(y, jnp.take(idx, part_order(rows, col_count)), axis=1)  10.3 us
  transfers between devices with their start and end apart: 9, of which 8 were waited for; matrix products, arithmetic and copies ran while one was open for 27% of the time, Pallas kernels for 0%

profile of v8, /device:TPU:1, one launch (start us, length us, event | category | flops | bytes accessed | tf_op | source)
XLA Modules:
  0.0 402.2 jit_solution(1230985753976109778)
XLA Ops:
  10.6 8.3 %all-to-all-start = ((f32[2,8,8,16,160]{4,3,1,0,2:T(8,128)}), f32[2,8,8,16,160]{4,3,1,0,2:T(8,128)S(1)}, u32[]{:S(2)}, u32[]{:S(2)}) async-start(f32[2,8,8,16,160]{4,3,1,0,2:T(8,128)} %copy.52), calls=%async_computation | async-start | bytes 4194304 | tf_op jit(solution)/shard_map/all_to_all | solution.py:37
  19.3 39.1 %all-to-all-done = f32[2,8,8,16,160]{4,3,1,0,2:T(8,128)S(1)} async-done(((f32[2,8,8,16,160]{4,3,1,0,2:T(8,128)}), f32[2,8,8,16,160]{4,3,1,0,2:T(8,128)S(1)}, u32[]{:S(2)}, u32[]{:S(2)}) %all-to-all-start) | async-done | bytes 1310752 | tf_op jit(solution)/shard_map/all_to_all | solution.py:37
  60.0 2.3 gather_fusion.1
  63.8 4.0 all-to-all-start.1
  67.9 4.5 %gather_fusion = s32[1024]{0:T(1024)S(1)} fusion(s32[1024]{0:T(1024)S(1)} %add_bitcast_fusion, s32[1024]{0:T(1024)S(1)} %broadcast_clamp_fusion), kind=kCustom, calls=%fused_computation | custom fusion | bytes 12288 | tf_op jit(solution)/shard_map/jit(_take)/gather | solution.py:49
  72.5 32.5 %all-to-all-done.1 = f32[2,8,8,16,160]{4,3,2,0,1:T(8,128)S(1)} async-done(((f32[2,8,8,16,160]{4,3,2,0,1:T(8,128)}), f32[2,8,8,16,160]{4,3,2,0,1:T(8,128)S(1)}, u32[]{:S(2)}, u32[]{:S(2)}) %all-to-all-start.1) | async-done | bytes 1310752 | tf_op jit(solution)/shard_map/all_to_all | solution.py:43
  105.2 2.9 copy.56
  108.1 5.8 %gather_fusion.2 = f32[1024,2,160]{2,1,0:T(2,128)S(1)} fusion(f32[2,1024,160]{2,0,1:T(2,128)} %copy.56, s32[1024]{0:T(1024)S(1)} %fusion.12), kind=kCustom, calls=%fused_computation.2 | custom fusion | bytes 2625536 | tf_op jit(solution)/shard_map/jit(_take)/gather | solution.py:49
  113.9 4.5 %select_bitcast_fusion = f32[2,160,1024]{1,0,2:T(2,128)} fusion(f32[1024,2,160]{2,1,0:T(2,128)S(1)} %gather_fusion.2, pred[1024]{0:T(1024)(128)(4,1)S(1)} %compare_and_fusion.1), kind=kLoop, calls=%fused_computation.14 | loop fusion | flops 327680 | bytes 2622464 | tf_op jit(solution)/shard_map/jit(_take)/select_n | solution.py:49
  118.3 50.6 %all-gather.5.cloned.1.call-done = f32[2,2560,512]{2,1,0:T(8,128)} async-done(((f32[2,320,512]{2,1,0:T(8,128)}), f32[2,2560,512]{2,1,0:T(8,128)}) %all-gather.5.cloned.1.call-update) | async-done | bytes 10485776 | tf_op jit(solution)/shard_map/all_gather | solution.py:72
  176.1 58.5 %all-gather.7.cloned.1.call-done = f32[2560,1024]{1,0:T(8,128)} async-done(((f32[160,1024]{1,0:T(8,128)}), f32[2560,1024]{1,0:T(8,128)}) %all-gather.7.cloned.1.call-update) | async-done | bytes 10485776 | tf_op jit(solution)/shard_map/all_gather | solution.py:89
  236.1 40.6 %all-gather.9.cloned.1.call-done = f32[2560,512]{1,0:T(8,128)} async-done(((f32[160,512]{1,0:T(8,128)}), f32[2560,512]{1,0:T(8,128)}) %all-gather.9.cloned.1.call-update) | async-done | bytes 5242896 | tf_op jit(solution)/shard_map/all_gather | solution.py:89
  276.7 12.1 %fusion.2 = f32[1024,512]{1,0:T(8,128)S(1)} fusion(f32[2560,1024]{1,0:T(8,128)} %all-gather.7.cloned.1.call-done, f32[2,2560,512]{2,1,0:T(8,128)} %all-gather.5.cloned.1.call-done), kind=kOutput, calls=%fused_computation.7 | convolution fusion | flops 8053063680 | bytes 17825792 | tf_op jit(solution)/shard_map/dot_general | solution.py:78
  288.9 11.1 %fusion.5 = f32[1024,512]{1,0:T(8,128)S(1)} fusion(f32[2560,1024]{1,0:T(8,128)} %all-gather.7.cloned.1.call-done, f32[2,2560,512]{2,1,0:T(8,128)S(1)} %bitcast.93), kind=kOutput, calls=%fused_computation.10 | convolution fusion | flops 8053063680 | bytes 17825792 | tf_op jit(solution)/shard_map/dot_general | solution.py:78
  302.0 4.5 %all-to-all-start.2 = ((f32[2,16,32,512]{3,2,0,1:T(8,128)}), f32[2,16,32,512]{3,2,0,1:T(8,128)S(1)}, u32[]{:S(2)}, u32[]{:S(2)}) async-start(f32[2,16,32,512]{3,2,0,1:T(8,128)} %pad_maximum_fusion), calls=%async_computation.2 | async-start | bytes 4194304 | tf_op jit(solution)/shard_map/all_to_all | solution.py:97
  306.5 12.5 %fusion.1 = f32[512,512]{1,0:T(8,128)S(1)} fusion(f32[2560,512]{1,0:T(8,128)} %all-gather.9.cloned.1.call-done, f32[2,2560,512]{2,1,0:T(8,128)} %all-gather.5.cloned.1.call-done), kind=kOutput, calls=%fused_computation.6 | convolution fusion | flops 4026531840 | bytes 11534336 | tf_op jit(solution)/shard_map/dot_general | solution.py:78
  319.1 10.6 %fusion.4 = f32[512,512]{1,0:T(8,128)S(1)} fusion(f32[2560,512]{1,0:T(8,128)S(1)} %bitcast.91, f32[2,2560,512]{2,1,0:T(8,128)} %all-gather.5.cloned.1.call-done), kind=kOutput, calls=%fused_computation.9 | convolution fusion | flops 4026531840 | bytes 11534336 | tf_op jit(solution)/shard_map/dot_general | solution.py:78
  331.4 12.4 %fusion = f32[512,512]{1,0:T(8,128)S(1)} fusion(f32[2560,512]{1,0:T(8,128)} %all-gather.11.cloned.1.call-done, f32[2,2560,512]{2,1,0:T(8,128)} %all-gather.5.cloned.1.call-done), kind=kOutput, calls=%fused_computation.5 | convolution fusion | flops 4026531840 | bytes 11534336 | tf_op jit(solution)/shard_map/dot_general | solution.py:78
  343.8 11.2 %all-to-all-start.3 = ((f32[2,16,16,512]{3,2,0,1:T(8,128)}), f32[2,16,16,512]{3,2,0,1:T(8,128)}, u32[]{:S(2)}, u32[]{:S(2)}) async-start(f32[2,16,16,512]{3,2,0,1:T(8,128)} %pad_maximum_fusion.1), calls=%async_computation.3 | async-start | bytes 2097152 | tf_op jit(solution)/shard_map/all_to_all | solution.py:97
  355.0 12.2 %fusion.3 = f32[512,512]{1,0:T(8,128)S(1)} fusion(f32[2560,512]{1,0:T(8,128)} %all-gather.11.cloned.1.call-done, f32[2,2560,512]{2,1,0:T(8,128)} %all-gather.5.cloned.1.call-done), kind=kOutput, calls=%fused_computation.8 | convolution fusion | flops 4026531840 | bytes 11534336 | tf_op jit(solution)/shard_map/dot_general | solution.py:78
  368.5 2.4 all-to-all-done.3
  370.9 4.9 %all-to-all-start.4 = ((f32[2,16,16,512]{3,2,0,1:T(8,128)}), f32[2,16,16,512]{3,2,0,1:T(8,128)}, u32[]{:S(2)}, u32[]{:S(2)}) async-start(f32[2,16,16,512]{3,2,0,1:T(8,128)} %pad_maximum_fusion.2), calls=%async_computation.4 | async-start | bytes 2097152 | tf_op jit(solution)/shard_map/all_to_all | solution.py:97
  378.8 13.0 %all-to-all-done.4 = f32[2,16,16,512]{3,2,0,1:T(8,128)} async-done(((f32[2,16,16,512]{3,2,0,1:T(8,128)}), f32[2,16,16,512]{3,2,0,1:T(8,128)}, u32[]{:S(2)}, u32[]{:S(2)}) %all-to-all-start.4) | async-done | bytes 1048608 | tf_op jit(solution)/shard_map/all_to_all | solution.py:97
  393.2 2.3 maximum_bitcast_fusion
  (67 shorter events, 25.6 us)
Async XLA Ops:
  6.5 162.4 %all-gather.5.cloned.1.call-start = ((), (), s32[]{:S(2)}) async-start(), calls=%async_computation.5 | async-start | bytes 11796480 | tf_op jit(solution)/shard_map/all_gather | solution.py:72
  9.1 9.9 %copy-start.3 = (s32[64]{0:T(128)S(1)}, s32[64]{0:T(128)}, u32[]{:S(2)}) copy-start(s32[64]{0:T(128)} %param.7) | copy-start | bytes 772
  9.1 10.1 %copy-start.4 = (s32[7]{0:T(128)S(1)}, s32[7]{0:T(128)}, u32[]{:S(2)}) copy-start(s32[7]{0:T(128)} %param.8) | copy-start | bytes 88
  10.6 47.8 %all-to-all-start = ((f32[2,8,8,16,160]{4,3,1,0,2:T(8,128)}), f32[2,8,8,16,160]{4,3,1,0,2:T(8,128)S(1)}, u32[]{:S(2)}, u32[]{:S(2)}) async-start(f32[2,8,8,16,160]{4,3,1,0,2:T(8,128)} %copy.52), calls=%async_computation | async-start | bytes 4194304 | tf_op jit(solution)/shard_map/all_to_all | solution.py:37
  62.3 5.7 %copy-start.2 = (s32[1024]{0:T(1024)S(1)}, s32[1024]{0:T(1024)}, u32[]{:S(2)}) copy-start(s32[1024]{0:T(1024)} %constant.116) | copy-start | bytes 12292
  63.8 41.2 %all-to-all-start.1 = ((f32[2,8,8,16,160]{4,3,2,0,1:T(8,128)}), f32[2,8,8,16,160]{4,3,2,0,1:T(8,128)S(1)}, u32[]{:S(2)}, u32[]{:S(2)}) async-start(f32[2,8,8,16,160]{4,3,2,0,1:T(8,128)} %copy_select_fusion), calls=%async_computation.1 | async-start | bytes 4194304 | tf_op jit(solution)/shard_map/all_to_all | solution.py:43
  67.8 166.8 %all-gather.7.cloned.1.call-start = ((), (), s32[]{:S(2)}) async-start(), calls=%async_computation.6 | async-start | bytes 11141120 | tf_op jit(solution)/shard_map/all_gather | solution.py:89
  118.3 56.2 %copy-start = (f32[2,160,1024]{1,0,2:T(2,128)S(1)}, f32[2,160,1024]{1,0,2:T(2,128)}, u32[]{:S(2)}) copy-start(f32[2,160,1024]{1,0,2:T(2,128)} %select_bitcast_fusion) | copy-start | bytes 3932164
  174.5 102.2 %all-gather.9.cloned.1.call-start = ((), (), s32[]{:S(2)}) async-start(), calls=%async_computation.7 | async-start | bytes 5570560 | tf_op jit(solution)/shard_map/all_gather | solution.py:89
  234.6 96.8 %all-gather.11.cloned.1.call-start = ((), (), s32[]{:S(2)}) async-start(), calls=%async_computation.8 | async-start | bytes 5570560 | tf_op jit(solution)/shard_map/all_gather | solution.py:89
  276.7 12.1 %slice-start.2 = ((s8[10485760]{0:T(1024)(128)(4,1)}), s8[2097152]{0:T(1024)(128)(4,1)S(1)}, s32[]{:S(2)}) async-start(s8[10485760]{0:T(1024)(128)(4,1)} %bitcast.92), calls=%async_computation.11 | async-start | bytes 4194304
  276.7 12.1 %slice-start.3 = ((s8[10485760]{0:T(1024)(128)(4,1)}), s8[4194304]{0:T(1024)(128)(4,1)S(1)}, s32[]{:S(2)}) async-start(s8[10485760]{0:T(1024)(128)(4,1)} %bitcast.92), calls=%async_computation.12 | async-start | bytes 8388608
  276.7 12.1 %slice-start.4 = ((s8[10485760]{0:T(1024)(128)(4,1)}), s8[4194304]{0:T(1024)(128)(4,1)S(1)}, s32[]{:S(2)}) async-start(s8[10485760]{0:T(1024)(128)(4,1)} %bitcast.92), calls=%async_computation.13 | async-start | bytes 8388608
  302.0 17.1 %slice-start = ((s8[5242880]{0:T(1024)(128)(4,1)}), s8[1048576]{0:T(1024)(128)(4,1)S(1)}, s32[]{:S(2)}) async-start(s8[5242880]{0:T(1024)(128)(4,1)} %bitcast.90), calls=%async_computation.9 | async-start | bytes 2097152
  302.0 41.8 %all-to-all-start.2 = ((f32[2,16,32,512]{3,2,0,1:T(8,128)}), f32[2,16,32,512]{3,2,0,1:T(8,128)S(1)}, u32[]{:S(2)}, u32[]{:S(2)}) async-start(f32[2,16,32,512]{3,2,0,1:T(8,128)} %pad_maximum_fusion), calls=%async_computation.2 | async-start | bytes 4194304 | tf_op jit(solution)/shard_map/all_to_all | solution.py:97
  306.5 12.6 %slice-start.1 = ((s8[5242880]{0:T(1024)(128)(4,1)}), s8[4194304]{0:T(1024)(128)(4,1)S(1)}, s32[]{:S(2)}) async-start(s8[5242880]{0:T(1024)(128)(4,1)} %bitcast.90), calls=%async_computation.10 | async-start | bytes 8388608
  343.8 27.1 %all-to-all-start.3 = ((f32[2,16,16,512]{3,2,0,1:T(8,128)}), f32[2,16,16,512]{3,2,0,1:T(8,128)}, u32[]{:S(2)}, u32[]{:S(2)}) async-start(f32[2,16,16,512]{3,2,0,1:T(8,128)} %pad_maximum_fusion.1), calls=%async_computation.3 | async-start | bytes 2097152 | tf_op jit(solution)/shard_map/all_to_all | solution.py:97
  370.9 20.9 %all-to-all-start.4 = ((f32[2,16,16,512]{3,2,0,1:T(8,128)}), f32[2,16,16,512]{3,2,0,1:T(8,128)}, u32[]{:S(2)}, u32[]{:S(2)}) async-start(f32[2,16,16,512]{3,2,0,1:T(8,128)} %pad_maximum_fusion.2), calls=%async_computation.4 | async-start | bytes 2097152 | tf_op jit(solution)/shard_map/all_to_all | solution.py:97
  377.4 15.8 %copy-start.1 = (f32[1,16,2,4,8,512]{5,4,1,3,2,0:T(8,128)S(1)}, f32[1,16,2,4,8,512]{5,4,1,3,2,0:T(8,128)}, u32[]{:S(2)}) copy-start(f32[1,16,2,4,8,512]{5,4,1,3,2,0:T(8,128)} %copy.69) | copy-start | bytes 6291460
Sparse Core Ops, SparseCore 0:
  9.7 159.2 all-gather.4
  174.6 59.9 all-gather.6
  236.3 40.3 all-gather.8
  278.3 53.0 all-gather.10

commit v9 on v8

--- a/solution.py
+++ b/solution.py
@@ -50,7 +50,7 @@
 
 
 def part_sizes(q_total):
-    return [q_total // 2, q_total // 4, q_total - q_total // 2 - q_total // 4]
+    return [q_total * 3 // 4, q_total - q_total * 3 // 4]
 
 
 def part_order(rows, col_count):

time: 408 us -> 379 us (0.929); the launches traced: 402 us -> 379 us
  matrix products: 70.9 us -> 56.8 us
  starting transfers between devices: 33.3 us -> 28 us
    all_gather x3 -> x2, waiting for transfers between devices: 99.5 us -> 83 us  [body(): lall = lax.all_gather(piece, COL, axis=0, tiled=True)]
    dot_general x6 -> x4, matrix products: 70.9 us -> 56.8 us  [body(): lax.dot_general(a, b, dims, preferred_element_type=jnp.float32, precision...]
    all_to_all x3 -> x2, waiting for transfers between devices: 15.4 us -> 28.5 us  [body(): lax.all_to_all(tile, COL, split_axis=1, concat_axis=3, tiled=True)]
    all_to_all x3 -> x2, starting transfers between devices: 20.7 us -> 15.1 us  [body(): lax.all_to_all(tile, COL, split_axis=1, concat_axis=3, tiled=True)]
  transfers between devices with their start and end apart: 9 -> 7, of which waited for: 8 -> 7; matrix products, arithmetic and copies ran while one was open for 27% -> 24% of each run, Pallas kernels for 0% -> 0%
where the time goes in v9:
time: 379 us
  waiting for transfers between devices  234 us (62%)
  matrix products  56.8 us (15%)
  local copies, waits for them, and re-layouts  31.2 us (8%)
  starting transfers between devices  28 us (7%)
  other arithmetic  14.8 us (4%)
  between operations  13.4 us (4%)
    all_gather x2, waiting for transfers between devices, body(): lall = lax.all_gather(piece, COL, axis=0, tiled=True)  83 us
    dot_general x4, matrix products, body(): lax.dot_general(a, b, dims, preferred_element_type=jnp.float32, precision...  56.8 us
    all_gather x1, waiting for transfers between devices, body(): rall = lax.all_gather(right, ROW, axis=1, tiled=True)  50.4 us
    all_to_all x1, waiting for transfers between devices, permute_left(): x = lax.all_to_all(x, ROW, split_axis=2, concat_axis=2, tiled=True)  39.1 us
    all_to_all x1, waiting for transfers between devices, permute_left(): y = lax.all_to_all(y, ROW, split_axis=1, concat_axis=1, tiled=True)  32.7 us
    all_to_all x2, waiting for transfers between devices, body(): lax.all_to_all(tile, COL, split_axis=1, concat_axis=3, tiled=True)  28.5 us
    all_to_all x2, starting transfers between devices, body(): lax.all_to_all(tile, COL, split_axis=1, concat_axis=3, tiled=True)  15.1 us
    gather x2, local copies, waits for them, and re-layouts, permute_left(): return jnp.take(y, jnp.take(idx, part_order(rows, col_count)), axis=1)  10.3 us
  transfers between devices with their start and end apart: 7, of which 7 were waited for; matrix products, arithmetic and copies ran while one was open for 24% of the time, Pallas kernels for 0%

profile of v9, /device:TPU:1, one launch (start us, length us, event | category | flops | bytes accessed | tf_op | source)
XLA Modules:
  0.0 378.5 jit_solution(14990816908982897863)
XLA Ops:
  7.3 1.8 copy.41
  10.6 8.5 %all-to-all-start = ((f32[2,8,8,16,160]{4,3,1,0,2:T(8,128)}), f32[2,8,8,16,160]{4,3,1,0,2:T(8,128)S(1)}, u32[]{:S(2)}, u32[]{:S(2)}) async-start(f32[2,8,8,16,160]{4,3,1,0,2:T(8,128)} %copy.42), calls=%async_computation | async-start | bytes 4194304 | tf_op jit(solution)/shard_map/all_to_all | solution.py:37
  19.4 39.1 %all-to-all-done = f32[2,8,8,16,160]{4,3,1,0,2:T(8,128)S(1)} async-done(((f32[2,8,8,16,160]{4,3,1,0,2:T(8,128)}), f32[2,8,8,16,160]{4,3,1,0,2:T(8,128)S(1)}, u32[]{:S(2)}, u32[]{:S(2)}) %all-to-all-start) | async-done | bytes 1310752 | tf_op jit(solution)/shard_map/all_to_all | solution.py:37
  60.1 2.3 gather_fusion.1
  63.9 4.1 %all-to-all-start.1 = ((f32[2,8,8,16,160]{4,3,2,0,1:T(8,128)}), f32[2,8,8,16,160]{4,3,2,0,1:T(8,128)S(1)}, u32[]{:S(2)}, u32[]{:S(2)}) async-start(f32[2,8,8,16,160]{4,3,2,0,1:T(8,128)} %copy_select_fusion), calls=%async_computation.1 | async-start | bytes 4194304 | tf_op jit(solution)/shard_map/all_to_all | solution.py:43
  68.2 4.5 %gather_fusion = s32[1024]{0:T(1024)S(1)} fusion(s32[1024]{0:T(1024)S(1)} %add_bitcast_fusion, s32[1024]{0:T(1024)S(1)} %broadcast_clamp_fusion), kind=kCustom, calls=%fused_computation | custom fusion | bytes 12288 | tf_op jit(solution)/shard_map/jit(_take)/gather | solution.py:49
  72.7 32.7 %all-to-all-done.1 = f32[2,8,8,16,160]{4,3,2,0,1:T(8,128)S(1)} async-done(((f32[2,8,8,16,160]{4,3,2,0,1:T(8,128)}), f32[2,8,8,16,160]{4,3,2,0,1:T(8,128)S(1)}, u32[]{:S(2)}, u32[]{:S(2)}) %all-to-all-start.1) | async-done | bytes 1310752 | tf_op jit(solution)/shard_map/all_to_all | solution.py:43
  105.7 2.9 copy.46
  108.6 5.8 %gather_fusion.2 = f32[1024,2,160]{2,1,0:T(2,128)S(1)} fusion(f32[2,1024,160]{2,0,1:T(2,128)} %copy.46, s32[1024]{0:T(1024)S(1)} %fusion.10), kind=kCustom, calls=%fused_computation.2 | custom fusion | bytes 2625536 | tf_op jit(solution)/shard_map/jit(_take)/gather | solution.py:49
  114.4 4.5 %select_bitcast_fusion = f32[2,160,1024]{1,0,2:T(2,128)} fusion(f32[1024,2,160]{2,1,0:T(2,128)S(1)} %gather_fusion.2, pred[1024]{0:T(1024)(128)(4,1)S(1)} %compare_and_fusion.1), kind=kLoop, calls=%fused_computation.12 | loop fusion | flops 327680 | bytes 2622464 | tf_op jit(solution)/shard_map/jit(_take)/select_n | solution.py:49
  118.8 50.4 %all-gather.4.cloned.1.call-done = f32[2,2560,512]{2,1,0:T(8,128)} async-done(((f32[2,320,512]{2,1,0:T(8,128)}), f32[2,2560,512]{2,1,0:T(8,128)}) %all-gather.4.cloned.1.call-update) | async-done | bytes 10485776 | tf_op jit(solution)/shard_map/all_gather | solution.py:72
  169.2 1.9 slice_bitcast_fusion.6
  176.6 82.2 %all-gather.6.cloned.1.call-done = f32[2560,1536]{1,0:T(8,128)} async-done(((f32[160,1536]{1,0:T(8,128)}), f32[2560,1536]{1,0:T(8,128)}) %all-gather.6.cloned.1.call-update) | async-done | bytes 15728656 | tf_op jit(solution)/shard_map/all_gather | solution.py:89
  258.9 17.6 %fusion.3 = f32[1536,512]{1,0:T(8,128)S(1)} fusion(f32[2560,1536]{1,0:T(8,128)} %all-gather.6.cloned.1.call-done, f32[2,2560,512]{2,1,0:T(8,128)} %all-gather.4.cloned.1.call-done), kind=kOutput, calls=%fused_computation.8 | convolution fusion | flops 12079595520 | bytes 24117248 | tf_op jit(solution)/shard_map/dot_general | solution.py:78
  276.5 15.6 %fusion.1 = f32[1536,512]{1,0:T(8,128)S(1)} fusion(f32[2560,1536]{1,0:T(8,128)} %all-gather.6.cloned.1.call-done, f32[2,2560,512]{2,1,0:T(8,128)S(1)} %bitcast.74), kind=kOutput, calls=%fused_computation.6 | convolution fusion | flops 12079595520 | bytes 24117248 | tf_op jit(solution)/shard_map/dot_general | solution.py:78
  292.9 2.2 pad_maximum_fusion
  295.1 5.0 %all-to-all-start.2 = ((f32[2,16,48,512]{3,2,0,1:T(8,128)}), f32[2,16,48,512]{3,2,0,1:T(8,128)S(1)}, u32[]{:S(2)}, u32[]{:S(2)}) async-start(f32[2,16,48,512]{3,2,0,1:T(8,128)} %pad_maximum_fusion), calls=%async_computation.2 | async-start | bytes 6291456 | tf_op jit(solution)/shard_map/all_to_all | solution.py:97
  300.9 12.8 %fusion.2 = f32[512,512]{1,0:T(8,128)S(1)} fusion(f32[2560,512]{1,0:T(8,128)} %all-gather.8.cloned.1.call-done, f32[2,2560,512]{2,1,0:T(8,128)} %all-gather.4.cloned.1.call-done), kind=kOutput, calls=%fused_computation.7 | convolution fusion | flops 4026531840 | bytes 11534336 | tf_op jit(solution)/shard_map/dot_general | solution.py:78
  313.7 10.8 %fusion = f32[512,512]{1,0:T(8,128)S(1)} fusion(f32[2560,512]{1,0:T(8,128)S(1)} %copy-done, f32[2,2560,512]{2,1,0:T(8,128)} %all-gather.4.cloned.1.call-done), kind=kOutput, calls=%fused_computation.5 | convolution fusion | flops 4026531840 | bytes 11534336 | tf_op jit(solution)/shard_map/dot_general | solution.py:78
  325.8 14.7 %all-to-all-done.2 = f32[2,16,48,512]{3,2,0,1:T(8,128)S(1)} async-done(((f32[2,16,48,512]{3,2,0,1:T(8,128)}), f32[2,16,48,512]{3,2,0,1:T(8,128)S(1)}, u32[]{:S(2)}, u32[]{:S(2)}) %all-to-all-start.2) | async-done | bytes 3145760 | tf_op jit(solution)/shard_map/all_to_all | solution.py:97
  340.5 10.1 %all-to-all-start.3 = ((f32[2,16,16,512]{3,2,0,1:T(8,128)}), f32[2,16,16,512]{3,2,0,1:T(8,128)}, u32[]{:S(2)}, u32[]{:S(2)}) async-start(f32[2,16,16,512]{3,2,0,1:T(8,128)} %pad_maximum_fusion.1), calls=%async_computation.3 | async-start | bytes 2097152 | tf_op jit(solution)/shard_map/all_to_all | solution.py:97
  350.5 2.1 copy.55
  352.6 13.9 %all-to-all-done.3 = f32[2,16,16,512]{3,2,0,1:T(8,128)} async-done(((f32[2,16,16,512]{3,2,0,1:T(8,128)}), f32[2,16,16,512]{3,2,0,1:T(8,128)}, u32[]{:S(2)}, u32[]{:S(2)}) %all-to-all-start.3) | async-done | bytes 1048608 | tf_op jit(solution)/shard_map/all_to_all | solution.py:97
  367.8 4.2 %maximum_bitcast_fusion = f32[2,64,8192]{2,1,0:T(8,128)} fusion(f32[2,1,16,8192]{3,2,0,1:T(8,128)S(1)} %bitcast.81, f32[2,1,48,8192]{3,2,0,1:T(8,128)} %bitcast.72), kind=kLoop, calls=%fused_computation.9 | loop fusion | flops 1048576 | bytes 8388608 | tf_op jit(solution)/shard_map/reshape | solution.py:99
  (48 shorter events, 15.6 us)
Async XLA Ops:
  6.5 162.7 %all-gather.4.cloned.1.call-start = ((), (), s32[]{:S(2)}) async-start(), calls=%async_computation.4 | async-start | bytes 11796480 | tf_op jit(solution)/shard_map/all_gather | solution.py:72
  9.1 10.0 %copy-start.2 = (s32[64]{0:T(128)S(1)}, s32[64]{0:T(128)}, u32[]{:S(2)}) copy-start(s32[64]{0:T(128)} %param.7) | copy-start | bytes 772
  10.6 8.7 %copy-start.3 = (s32[7]{0:T(128)S(1)}, s32[7]{0:T(128)}, u32[]{:S(2)}) copy-start(s32[7]{0:T(128)} %param.8) | copy-start | bytes 88
  10.6 47.9 %all-to-all-start = ((f32[2,8,8,16,160]{4,3,1,0,2:T(8,128)}), f32[2,8,8,16,160]{4,3,1,0,2:T(8,128)S(1)}, u32[]{:S(2)}, u32[]{:S(2)}) async-start(f32[2,8,8,16,160]{4,3,1,0,2:T(8,128)} %copy.42), calls=%async_computation | async-start | bytes 4194304 | tf_op jit(solution)/shard_map/all_to_all | solution.py:37
  63.9 4.3 %copy-start.1 = (s32[1024]{0:T(1024)S(1)}, s32[1024]{0:T(1024)}, u32[]{:S(2)}) copy-start(s32[1024]{0:T(1024)} %constant.116) | copy-start | bytes 12292
  63.9 41.6 %all-to-all-start.1 = ((f32[2,8,8,16,160]{4,3,2,0,1:T(8,128)}), f32[2,8,8,16,160]{4,3,2,0,1:T(8,128)S(1)}, u32[]{:S(2)}, u32[]{:S(2)}) async-start(f32[2,8,8,16,160]{4,3,2,0,1:T(8,128)} %copy_select_fusion), calls=%async_computation.1 | async-start | bytes 4194304 | tf_op jit(solution)/shard_map/all_to_all | solution.py:43
  68.0 190.8 %all-gather.6.cloned.1.call-start = ((), (), s32[]{:S(2)}) async-start(), calls=%async_computation.5 | async-start | bytes 16711680 | tf_op jit(solution)/shard_map/all_gather | solution.py:89
  174.0 126.9 %all-gather.8.cloned.1.call-start = ((), (), s32[]{:S(2)}) async-start(), calls=%async_computation.6 | async-start | bytes 5570560 | tf_op jit(solution)/shard_map/all_gather | solution.py:89
  175.9 100.6 %slice-start = ((s8[10485760]{0:T(1024)(128)(4,1)}), s8[2097152]{0:T(1024)(128)(4,1)S(1)}, s32[]{:S(2)}) async-start(s8[10485760]{0:T(1024)(128)(4,1)} %bitcast.73), calls=%async_computation.7 | async-start | bytes 4194304
  258.8 17.7 %slice-start.1 = ((s8[10485760]{0:T(1024)(128)(4,1)}), s8[4194304]{0:T(1024)(128)(4,1)S(1)}, s32[]{:S(2)}) async-start(s8[10485760]{0:T(1024)(128)(4,1)} %bitcast.73), calls=%async_computation.8 | async-start | bytes 8388608
  258.9 17.7 %slice-start.2 = ((s8[10485760]{0:T(1024)(128)(4,1)}), s8[4194304]{0:T(1024)(128)(4,1)S(1)}, s32[]{:S(2)}) async-start(s8[10485760]{0:T(1024)(128)(4,1)} %bitcast.73), calls=%async_computation.9 | async-start | bytes 8388608
  295.1 45.4 %all-to-all-start.2 = ((f32[2,16,48,512]{3,2,0,1:T(8,128)}), f32[2,16,48,512]{3,2,0,1:T(8,128)S(1)}, u32[]{:S(2)}, u32[]{:S(2)}) async-start(f32[2,16,48,512]{3,2,0,1:T(8,128)} %pad_maximum_fusion), calls=%async_computation.2 | async-start | bytes 6291456 | tf_op jit(solution)/shard_map/all_to_all | solution.py:97
  300.9 12.8 %copy-start = (f32[2560,512]{1,0:T(8,128)S(1)}, f32[2560,512]{1,0:T(8,128)}, u32[]{:S(2)}) copy-start(f32[2560,512]{1,0:T(8,128)} %all-gather.8.cloned.1.call-done) | copy-start | bytes 15728644
  340.5 26.0 %all-to-all-start.3 = ((f32[2,16,16,512]{3,2,0,1:T(8,128)}), f32[2,16,16,512]{3,2,0,1:T(8,128)}, u32[]{:S(2)}, u32[]{:S(2)}) async-start(f32[2,16,16,512]{3,2,0,1:T(8,128)} %pad_maximum_fusion.1), calls=%async_computation.3 | async-start | bytes 2097152 | tf_op jit(solution)/shard_map/all_to_all | solution.py:97
Sparse Core Ops, SparseCore 0:
  9.7 159.5 all-gather.3
  174.1 84.6 all-gather.5
  260.5 40.3 all-gather.7

commit v10 on v9

--- a/solution.py
+++ b/solution.py
@@ -73,9 +73,15 @@
     lp = permute_left(left, prefix_owner, qubit_order, row_count, col_count)
     lt = jnp.swapaxes(lp, 1, 2)
     lt = lax.optimization_barrier((lt, rall))[0]
-    high = lax.Precision.HIGH
     dims = (((0,), (0,)), ((), ()))
-    dot = lambda a, b: lax.dot_general(a, b, dims, preferred_element_type=jnp.float32, precision=high)
+    dot = lambda a, b: lax.dot_general(a, b, dims, preferred_element_type=jnp.float32)
+
+    def split(a):
+        hi = lax.reduce_precision(a, exponent_bits=8, mantissa_bits=7)
+        return hi.astype(jnp.bfloat16), (a - hi).astype(jnp.bfloat16)
+
+    rcat = jnp.concatenate([rall[0], rall[1]], axis=1)
+    r_hi, r_lo = split(rcat)
     outs = []
     prev = None
     start = 0
@@ -88,10 +94,10 @@
             piece = lax.optimization_barrier((piece, prev))[0]
         lall = lax.all_gather(piece, COL, axis=0, tiled=True)
         prev = lall
-        pr = dot(lall, rall[0])
-        pi = dot(lall, rall[1])
-        re = pr[:part] - pi[part:]
-        im = pi[:part] + pr[part:]
+        l_hi, l_lo = split(lall)
+        q = dot(l_hi, r_hi) + dot(l_hi, r_lo) + dot(l_lo, r_hi)
+        re = q[:part, :cols] - q[part:, cols:]
+        im = q[:part, cols:] + q[part:, :cols]
         tile = jnp.stack([re, im], axis=0)
         tile = tile.reshape(2, col_count, qp, cols)
         outs.append(lax.all_to_all(tile, COL, split_axis=1, concat_axis=3, tiled=True))

time: 379 us -> 410 us (1.082)
  local copies, waits for them, and re-layouts: 31.2 us -> 40.6 us
  matrix products: 56.8 us -> 64.2 us
  other arithmetic: 14.8 us -> 22.1 us
  waiting for transfers between devices: 234 us -> 241 us
    squeeze x0 -> x1, local copies, waits for them, and re-layouts: none -> 9.28 us  [body(): rcat = jnp.concatenate([rall[0], rall[1]], axis=1)]
    all_to_all x2, waiting for transfers between devices: 28.5 us -> 36.3 us  [body(): lax.all_to_all(tile, COL, split_axis=1, concat_axis=3, tiled=True)]
    dot_general x4 -> x6, matrix products: 56.8 us -> 64.2 us  [body(): lax.dot_general(a, b, dims, preferred_element_type=jnp.float32)]
    convert_element_type x0 -> x1, other arithmetic: none -> 7.34 us  [split(): return (hi.astype(jnp.bfloat16), (a - hi).astype(jnp.bfloat16))]
  transfers between devices with their start and end apart: 7 -> 7, of which waited for: 7 -> 6; matrix products, arithmetic and copies ran while one was open for 24% -> 28% of each run, Pallas kernels for 0% -> 0%
where the time goes in v10:
time: 410 us; the launch traced here: 409 us
  waiting for transfers between devices  241 us (59%)
  matrix products  64.2 us (16%)
  local copies, waits for them, and re-layouts  40.6 us (10%)
  starting transfers between devices  27.7 us (7%)
  other arithmetic  22.1 us (5%)
  between operations  13.4 us (3%)
    all_gather x2, waiting for transfers between devices, body(): lall = lax.all_gather(piece, COL, axis=0, tiled=True)  82.1 us
    dot_general x6, matrix products, body(): lax.dot_general(a, b, dims, preferred_element_type=jnp.float32)  64.2 us
    all_gather x1, waiting for transfers between devices, body(): rall = lax.all_gather(right, ROW, axis=1, tiled=True)  50.6 us
    all_to_all x1, waiting for transfers between devices, permute_left(): x = lax.all_to_all(x, ROW, split_axis=2, concat_axis=2, tiled=True)  39.1 us
    all_to_all x2, waiting for transfers between devices, body(): lax.all_to_all(tile, COL, split_axis=1, concat_axis=3, tiled=True)  36.3 us
    all_to_all x1, waiting for transfers between devices, permute_left(): y = lax.all_to_all(y, ROW, split_axis=1, concat_axis=1, tiled=True)  32.5 us
    all_to_all x2, starting transfers between devices, body(): lax.all_to_all(tile, COL, split_axis=1, concat_axis=3, tiled=True)  15.1 us
    gather x2, local copies, waits for them, and re-layouts, permute_left(): return jnp.take(y, jnp.take(idx, part_order(rows, col_count)), axis=1)  10.3 us
  transfers between devices with their start and end apart: 7, of which 6 were waited for; matrix products, arithmetic and copies ran while one was open for 28% of the time, Pallas kernels for 0%

profile of v10, /device:TPU:1, one launch (start us, length us, event | category | flops | bytes accessed | tf_op | source)
XLA Modules:
  0.0 409.3 jit_solution(9201010922679683400)
XLA Ops:
  10.6 8.3 %all-to-all-start = ((f32[2,8,8,16,160]{4,3,1,0,2:T(8,128)}), f32[2,8,8,16,160]{4,3,1,0,2:T(8,128)S(1)}, u32[]{:S(2)}, u32[]{:S(2)}) async-start(f32[2,8,8,16,160]{4,3,1,0,2:T(8,128)} %copy.42), calls=%async_computation | async-start | bytes 4194304 | tf_op jit(solution)/shard_map/all_to_all | solution.py:37
  19.3 39.1 %all-to-all-done = f32[2,8,8,16,160]{4,3,1,0,2:T(8,128)S(1)} async-done(((f32[2,8,8,16,160]{4,3,1,0,2:T(8,128)}), f32[2,8,8,16,160]{4,3,1,0,2:T(8,128)S(1)}, u32[]{:S(2)}, u32[]{:S(2)}) %all-to-all-start) | async-done | bytes 1310752 | tf_op jit(solution)/shard_map/all_to_all | solution.py:37
  60.0 2.3 gather_fusion.1
  63.8 4.0 all-to-all-start.1
  67.9 4.5 %gather_fusion = s32[1024]{0:T(1024)S(1)} fusion(s32[1024]{0:T(1024)S(1)} %add_bitcast_fusion, s32[1024]{0:T(1024)S(1)} %broadcast_clamp_fusion), kind=kCustom, calls=%fused_computation | custom fusion | bytes 12288 | tf_op jit(solution)/shard_map/jit(_take)/gather | solution.py:49
  72.5 32.5 %all-to-all-done.1 = f32[2,8,8,16,160]{4,3,2,0,1:T(8,128)S(1)} async-done(((f32[2,8,8,16,160]{4,3,2,0,1:T(8,128)}), f32[2,8,8,16,160]{4,3,2,0,1:T(8,128)S(1)}, u32[]{:S(2)}, u32[]{:S(2)}) %all-to-all-start.1) | async-done | bytes 1310752 | tf_op jit(solution)/shard_map/all_to_all | solution.py:43
  105.2 2.9 copy.46
  108.1 5.8 %gather_fusion.2 = f32[1024,2,160]{2,1,0:T(2,128)S(1)} fusion(f32[2,1024,160]{2,0,1:T(2,128)} %copy.46, s32[1024]{0:T(1024)S(1)} %fusion.21), kind=kCustom, calls=%fused_computation.2 | custom fusion | bytes 2625536 | tf_op jit(solution)/shard_map/jit(_take)/gather | solution.py:49
  113.9 4.5 %select_bitcast_fusion = f32[2,160,1024]{1,0,2:T(2,128)} fusion(f32[1024,2,160]{2,1,0:T(2,128)S(1)} %gather_fusion.2, pred[1024]{0:T(1024)(128)(4,1)S(1)} %compare_and_fusion.1), kind=kLoop, calls=%fused_computation.23 | loop fusion | flops 327680 | bytes 2622464 | tf_op jit(solution)/shard_map/jit(_take)/select_n | solution.py:49
  118.4 50.6 %all-gather.4.cloned.1.call-done = f32[2,2560,512]{2,1,0:T(8,128)} async-done(((f32[2,320,512]{2,1,0:T(8,128)}), f32[2,2560,512]{2,1,0:T(8,128)}) %all-gather.4.cloned.1.call-update) | async-done | bytes 10485776 | tf_op jit(solution)/shard_map/all_gather | solution.py:72
  176.5 82.1 %all-gather.6.cloned.1.call-done = f32[2560,1536]{1,0:T(8,128)} async-done(((f32[160,1536]{1,0:T(8,128)}), f32[2560,1536]{1,0:T(8,128)}) %all-gather.6.cloned.1.call-update) | async-done | bytes 15728656 | tf_op jit(solution)/shard_map/all_gather | solution.py:95
  258.6 9.3 %slice_bitcast_fusion.1 = (f32[2560,512]{1,0:T(8,128)}, f32[2560,512]{1,0:T(8,128)}) fusion(f32[2,2560,512]{2,1,0:T(8,128)} %all-gather.4.cloned.1.call-done), kind=kLoop, calls=%fused_computation.16 | loop fusion | bytes 20971520 | tf_op jit(solution)/shard_map/squeeze | solution.py:83
  267.9 7.3 %reduce-precision_convert_fusion.1 = bf16[2560,1024]{1,0:T(8,128)(2,1)} fusion(f32[2560,512]{1,0:T(8,128)} %get-tuple-element.10, f32[2560,512]{1,0:T(8,128)} %get-tuple-element.9), kind=kLoop, calls=%fused_computation.7 | loop fusion | flops 7864320 | bytes 15728640 | tf_op jit(solution)/shard_map/convert_element_type | solution.py:81
  275.2 17.0 %fusion.7 = f32[1536,1024]{1,0:T(8,128)} fusion(f32[2560,1536]{1,0:T(8,128)} %all-gather.6.cloned.1.call-done, f32[2560,512]{1,0:T(8,128)} %get-tuple-element.10, f32[2560,512]{1,0:T(8,128)} %get-tuple-element.9), kind=kOutput, calls=%fused_computation.19 | convolution fusion | flops 8071413760 | bytes 32505856 | tf_op jit(solution)/shard_map/dot_general | solution.py:77
  292.2 14.0 %fusion.8 = f32[1536,1024]{1,0:T(8,128)} fusion(bf16[2560,1024]{1,0:T(8,128)(2,1)S(1)} %copy-done, f32[2560,1536]{1,0:T(8,128)} %all-gather.6.cloned.1.call-done), kind=kOutput, calls=%fused_computation.20 | convolution fusion | flops 8060928000 | bytes 27262976 | tf_op jit(solution)/shard_map/dot_general | solution.py:77
  306.2 16.7 %add_add_fusion = f32[1536,1024]{1,0:T(8,128)S(1)} fusion(f32[1536,1024]{1,0:T(8,128)} %fusion.8, f32[1536,1024]{1,0:T(8,128)} %fusion.7, bf16[2560,1024]{1,0:T(8,128)(2,1)} %reduce-precision_convert_fusion.1, f32[2560,1536]{1,0:T(8,128)} %all-gather.6.cloned.1.call-done), kind=kOutput, calls=%fused_computation.13 | convolution fusion | flops 8068005888 | bytes 39845888 | tf_op jit(solution)/shard_map/dot_general | solution.py:77
  325.9 5.0 %all-to-all-start.2 = ((f32[2,16,48,512]{3,2,0,1:T(8,128)}), f32[2,16,48,512]{3,2,0,1:T(8,128)S(1)}, u32[]{:S(2)}, u32[]{:S(2)}) async-start(f32[2,16,48,512]{3,2,0,1:T(8,128)} %pad_maximum_fusion.1), calls=%async_computation.2 | async-start | bytes 6291456 | tf_op jit(solution)/shard_map/all_to_all | solution.py:103
  330.9 6.6 %fusion.14 = f32[512,1024]{1,0:T(8,128)S(1)} fusion(bf16[2560,1024]{1,0:T(8,128)(2,1)} %reduce-precision_convert_fusion.1, f32[2560,512]{1,0:T(8,128)} %all-gather.8.cloned.1.call-done), kind=kOutput, calls=%fused_computation.30 | convolution fusion | flops 2686976000 | bytes 12582912 | tf_op jit(solution)/shard_map/dot_general | solution.py:77
  337.5 7.0 %fusion.13 = f32[512,1024]{1,0:T(8,128)S(1)} fusion(f32[2560,512]{1,0:T(8,128)S(1)} %copy-done.2, f32[2560,512]{1,0:T(8,128)} %get-tuple-element.10, f32[2560,512]{1,0:T(8,128)} %get-tuple-element.9), kind=kOutput, calls=%fused_computation.29 | convolution fusion | flops 2697461760 | bytes 17825792 | tf_op jit(solution)/shard_map/dot_general | solution.py:77
  344.6 2.9 add_add_fusion.1
  348.8 22.4 %all-to-all-done.2 = f32[2,16,48,512]{3,2,0,1:T(8,128)S(1)} async-done(((f32[2,16,48,512]{3,2,0,1:T(8,128)}), f32[2,16,48,512]{3,2,0,1:T(8,128)S(1)}, u32[]{:S(2)}, u32[]{:S(2)}) %all-to-all-start.2) | async-done | bytes 3145760 | tf_op jit(solution)/shard_map/all_to_all | solution.py:103
  371.2 10.1 %all-to-all-start.3 = ((f32[2,16,16,512]{3,2,0,1:T(8,128)}), f32[2,16,16,512]{3,2,0,1:T(8,128)}, u32[]{:S(2)}, u32[]{:S(2)}) async-start(f32[2,16,16,512]{3,2,0,1:T(8,128)} %pad_maximum_fusion.2), calls=%async_computation.3 | async-start | bytes 2097152 | tf_op jit(solution)/shard_map/all_to_all | solution.py:103
  383.4 13.9 %all-to-all-done.3 = f32[2,16,16,512]{3,2,0,1:T(8,128)} async-done(((f32[2,16,16,512]{3,2,0,1:T(8,128)}), f32[2,16,16,512]{3,2,0,1:T(8,128)}, u32[]{:S(2)}, u32[]{:S(2)}) %all-to-all-start.3) | async-done | bytes 1048608 | tf_op jit(solution)/shard_map/all_to_all | solution.py:103
  398.5 4.2 %maximum_bitcast_fusion = f32[2,64,8192]{2,1,0:T(8,128)} fusion(f32[2,1,16,8192]{3,2,0,1:T(8,128)S(1)} %bitcast.77, f32[2,1,48,8192]{3,2,0,1:T(8,128)} %bitcast.68), kind=kLoop, calls=%fused_computation.17 | loop fusion | flops 1048576 | bytes 8388608 | tf_op jit(solution)/shard_map/reshape | solution.py:105
  (52 shorter events, 22.9 us)
Async XLA Ops:
  6.5 162.4 %all-gather.4.cloned.1.call-start = ((), (), s32[]{:S(2)}) async-start(), calls=%async_computation.4 | async-start | bytes 11796480 | tf_op jit(solution)/shard_map/all_gather | solution.py:72
  7.3 11.7 %copy-start.3 = (s32[64]{0:T(128)S(1)}, s32[64]{0:T(128)}, u32[]{:S(2)}) copy-start(s32[64]{0:T(128)} %param.7) | copy-start | bytes 772
  7.3 11.9 %copy-start.4 = (s32[7]{0:T(128)S(1)}, s32[7]{0:T(128)}, u32[]{:S(2)}) copy-start(s32[7]{0:T(128)} %param.8) | copy-start | bytes 88
  10.6 47.8 %all-to-all-start = ((f32[2,8,8,16,160]{4,3,1,0,2:T(8,128)}), f32[2,8,8,16,160]{4,3,1,0,2:T(8,128)S(1)}, u32[]{:S(2)}, u32[]{:S(2)}) async-start(f32[2,8,8,16,160]{4,3,1,0,2:T(8,128)} %copy.42), calls=%async_computation | async-start | bytes 4194304 | tf_op jit(solution)/shard_map/all_to_all | solution.py:37
  62.3 5.7 %copy-start.1 = (s32[1024]{0:T(1024)S(1)}, s32[1024]{0:T(1024)}, u32[]{:S(2)}) copy-start(s32[1024]{0:T(1024)} %constant.116) | copy-start | bytes 12292
  63.8 41.2 %all-to-all-start.1 = ((f32[2,8,8,16,160]{4,3,2,0,1:T(8,128)}), f32[2,8,8,16,160]{4,3,2,0,1:T(8,128)S(1)}, u32[]{:S(2)}, u32[]{:S(2)}) async-start(f32[2,8,8,16,160]{4,3,2,0,1:T(8,128)} %copy_select_fusion), calls=%async_computation.1 | async-start | bytes 4194304 | tf_op jit(solution)/shard_map/all_to_all | solution.py:43
  67.8 190.8 %all-gather.6.cloned.1.call-start = ((), (), s32[]{:S(2)}) async-start(), calls=%async_computation.5 | async-start | bytes 16711680 | tf_op jit(solution)/shard_map/all_gather | solution.py:95
  173.8 157.1 %all-gather.8.cloned.1.call-start = ((), (), s32[]{:S(2)}) async-start(), calls=%async_computation.6 | async-start | bytes 5570560 | tf_op jit(solution)/shard_map/all_gather | solution.py:95
  275.2 17.0 %copy-start = (bf16[2560,1024]{1,0:T(8,128)(2,1)S(1)}, bf16[2560,1024]{1,0:T(8,128)(2,1)}, u32[]{:S(2)}) copy-start(bf16[2560,1024]{1,0:T(8,128)(2,1)} %reduce-precision_convert_fusion.1) | copy-start | bytes 15728644
  325.9 45.4 %all-to-all-start.2 = ((f32[2,16,48,512]{3,2,0,1:T(8,128)}), f32[2,16,48,512]{3,2,0,1:T(8,128)S(1)}, u32[]{:S(2)}, u32[]{:S(2)}) async-start(f32[2,16,48,512]{3,2,0,1:T(8,128)} %pad_maximum_fusion.1), calls=%async_computation.2 | async-start | bytes 6291456 | tf_op jit(solution)/shard_map/all_to_all | solution.py:103
  330.9 6.6 %copy-start.2 = (f32[2560,512]{1,0:T(8,128)S(1)}, f32[2560,512]{1,0:T(8,128)}, u32[]{:S(2)}) copy-start(f32[2560,512]{1,0:T(8,128)} %all-gather.8.cloned.1.call-done) | copy-start | bytes 15728644
  330.9 13.6 %slice-start = ((s8[5242880]{0:T(1024)(128)(4,1)}), s8[4194304]{0:T(1024)(128)(4,1)S(1)}, s32[]{:S(2)}) async-start(s8[5242880]{0:T(1024)(128)(4,1)} %bitcast.75), calls=%async_computation.7 | async-start | bytes 8388608
  337.5 7.1 %slice-start.1 = ((s8[5242880]{0:T(1024)(128)(4,1)}), s8[1048576]{0:T(1024)(128)(4,1)S(1)}, s32[]{:S(2)}) async-start(s8[5242880]{0:T(1024)(128)(4,1)} %bitcast.75), calls=%async_computation.8 | async-start | bytes 2097152
  371.2 26.0 %all-to-all-start.3 = ((f32[2,16,16,512]{3,2,0,1:T(8,128)}), f32[2,16,16,512]{3,2,0,1:T(8,128)}, u32[]{:S(2)}, u32[]{:S(2)}) async-start(f32[2,16,16,512]{3,2,0,1:T(8,128)} %pad_maximum_fusion.2), calls=%async_computation.3 | async-start | bytes 2097152 | tf_op jit(solution)/shard_map/all_to_all | solution.py:103
Sparse Core Ops, SparseCore 0:
  9.7 159.2 all-gather.3
  173.9 84.6 all-gather.5
  260.3 40.5 all-gather.7

commit v11 on v9

--- a/solution.py
+++ b/solution.py
@@ -69,7 +69,8 @@
     col_count = lax.axis_size(COL)
     rows = left.shape[1]
     cols = right.shape[2]
-    rall = lax.all_gather(right, ROW, axis=1, tiled=True)
+    rpiece = jnp.swapaxes(right, 0, 1).reshape(right.shape[1], 2 * cols)
+    rall = lax.all_gather(rpiece, ROW, axis=0, tiled=True)
     lp = permute_left(left, prefix_owner, qubit_order, row_count, col_count)
     lt = jnp.swapaxes(lp, 1, 2)
     lt = lax.optimization_barrier((lt, rall))[0]
@@ -88,10 +89,9 @@
             piece = lax.optimization_barrier((piece, prev))[0]
         lall = lax.all_gather(piece, COL, axis=0, tiled=True)
         prev = lall
-        pr = dot(lall, rall[0])
-        pi = dot(lall, rall[1])
-        re = pr[:part] - pi[part:]
-        im = pi[:part] + pr[part:]
+        q = dot(lall, rall)
+        re = q[:part, :cols] - q[part:, cols:]
+        im = q[:part, cols:] + q[part:, :cols]
         tile = jnp.stack([re, im], axis=0)
         tile = tile.reshape(2, col_count, qp, cols)
         outs.append(lax.all_to_all(tile, COL, split_axis=1, concat_axis=3, tiled=True))

time: 379 us -> 378 us (level)
  matrix products: 56.8 us -> 43.7 us
  waiting for transfers between devices: 234 us -> 245 us
    dot_general x4 -> x2, matrix products: 56.8 us -> 43.7 us  [body(): lax.dot_general(a, b, dims, preferred_element_type=jnp.float32, precision...]
    all_to_all x2, waiting for transfers between devices: 28.5 us -> 38.3 us  [body(): lax.all_to_all(tile, COL, split_axis=1, concat_axis=3, tiled=True)]
  transfers between devices with their start and end apart: 7 -> 7, of which waited for: 7 -> 7; matrix products, arithmetic and copies ran while one was open for 24% -> 21% of each run, Pallas kernels for 0% -> 0%
where the time goes in v11:
time: 378 us
  waiting for transfers between devices  245 us (65%)
  matrix products  43.7 us (12%)
  local copies, waits for them, and re-layouts  32.8 us (9%)
  starting transfers between devices  27.9 us (7%)
  other arithmetic  14.7 us (4%)
  between operations  13.3 us (4%)
    all_gather x2, waiting for transfers between devices, body(): lall = lax.all_gather(piece, COL, axis=0, tiled=True)  84.7 us
    all_gather x1, waiting for transfers between devices, body(): rall = lax.all_gather(rpiece, ROW, axis=0, tiled=True)  49.8 us
    dot_general x2, matrix products, body(): lax.dot_general(a, b, dims, preferred_element_type=jnp.float32, precision...  43.7 us
    all_to_all x1, waiting for transfers between devices, permute_left(): x = lax.all_to_all(x, ROW, split_axis=2, concat_axis=2, tiled=True)  39.1 us
    all_to_all x2, waiting for transfers between devices, body(): lax.all_to_all(tile, COL, split_axis=1, concat_axis=3, tiled=True)  38.3 us
    all_to_all x1, waiting for transfers between devices, permute_left(): y = lax.all_to_all(y, ROW, split_axis=1, concat_axis=1, tiled=True)  33.3 us
    all_to_all x2, starting transfers between devices, body(): lax.all_to_all(tile, COL, split_axis=1, concat_axis=3, tiled=True)  15.1 us
    gather x2, local copies, waits for them, and re-layouts, permute_left(): return jnp.take(y, jnp.take(idx, part_order(rows, col_count)), axis=1)  10.3 us
  transfers between devices with their start and end apart: 7, of which 7 were waited for; matrix products, arithmetic and copies ran while one was open for 21% of the time, Pallas kernels for 0%

profile of v11, /device:TPU:1, one launch (start us, length us, event | category | flops | bytes accessed | tf_op | source)
XLA Modules:
  0.0 377.7 jit_solution(4709633685626059220)
XLA Ops:
  6.5 2.6 copy.59
  11.6 8.5 %all-to-all-start = ((f32[2,8,8,16,160]{4,3,1,0,2:T(8,128)}), f32[2,8,8,16,160]{4,3,1,0,2:T(8,128)S(1)}, u32[]{:S(2)}, u32[]{:S(2)}) async-start(f32[2,8,8,16,160]{4,3,1,0,2:T(8,128)} %copy.45), calls=%async_computation | async-start | bytes 4194304 | tf_op jit(solution)/shard_map/all_to_all | solution.py:37
  20.4 39.1 %all-to-all-done = f32[2,8,8,16,160]{4,3,1,0,2:T(8,128)S(1)} async-done(((f32[2,8,8,16,160]{4,3,1,0,2:T(8,128)}), f32[2,8,8,16,160]{4,3,1,0,2:T(8,128)S(1)}, u32[]{:S(2)}, u32[]{:S(2)}) %all-to-all-start) | async-done | bytes 1310752 | tf_op jit(solution)/shard_map/all_to_all | solution.py:37
  61.1 2.3 gather_fusion.1
  64.9 4.1 %all-to-all-start.1 = ((f32[2,8,8,16,160]{4,3,2,0,1:T(8,128)}), f32[2,8,8,16,160]{4,3,2,0,1:T(8,128)S(1)}, u32[]{:S(2)}, u32[]{:S(2)}) async-start(f32[2,8,8,16,160]{4,3,2,0,1:T(8,128)} %copy_select_fusion), calls=%async_computation.1 | async-start | bytes 4194304 | tf_op jit(solution)/shard_map/all_to_all | solution.py:43
  69.2 4.5 %gather_fusion = s32[1024]{0:T(1024)S(1)} fusion(s32[1024]{0:T(1024)S(1)} %add_bitcast_fusion, s32[1024]{0:T(1024)S(1)} %broadcast_clamp_fusion), kind=kCustom, calls=%fused_computation | custom fusion | bytes 12288 | tf_op jit(solution)/shard_map/jit(_take)/gather | solution.py:49
  73.7 33.3 %all-to-all-done.1 = f32[2,8,8,16,160]{4,3,2,0,1:T(8,128)S(1)} async-done(((f32[2,8,8,16,160]{4,3,2,0,1:T(8,128)}), f32[2,8,8,16,160]{4,3,2,0,1:T(8,128)S(1)}, u32[]{:S(2)}, u32[]{:S(2)}) %all-to-all-start.1) | async-done | bytes 1310752 | tf_op jit(solution)/shard_map/all_to_all | solution.py:43
  107.2 2.9 copy.49
  110.1 5.7 %gather_fusion.2 = f32[1024,2,160]{2,1,0:T(2,128)S(1)} fusion(f32[2,1024,160]{2,0,1:T(2,128)} %copy.49, s32[1024]{0:T(1024)S(1)} %fusion.6), kind=kCustom, calls=%fused_computation.2 | custom fusion | bytes 2625536 | tf_op jit(solution)/shard_map/jit(_take)/gather | solution.py:49
  115.9 4.5 %select_bitcast_fusion = f32[2,160,1024]{1,0,2:T(2,128)} fusion(f32[1024,2,160]{2,1,0:T(2,128)S(1)} %gather_fusion.2, pred[1024]{0:T(1024)(128)(4,1)S(1)} %compare_and_fusion.1), kind=kLoop, calls=%fused_computation.6 | loop fusion | flops 327680 | bytes 2622464 | tf_op jit(solution)/shard_map/jit(_take)/select_n | solution.py:49
  120.4 49.8 %all-gather.4.cloned.1.call-done = f32[2560,1024]{1,0:T(8,128)} async-done(((f32[320,1024]{1,0:T(8,128)}), f32[2560,1024]{1,0:T(8,128)}) %all-gather.4.cloned.1.call-update) | async-done | bytes 10485776 | tf_op jit(solution)/shard_map/all_gather | solution.py:73
  170.2 1.9 slice_bitcast_fusion
  172.1 1.8 copy.51
  177.6 82.2 %all-gather.6.cloned.1.call-done = f32[2560,1536]{1,0:T(8,128)} async-done(((f32[160,1536]{1,0:T(8,128)}), f32[2560,1536]{1,0:T(8,128)}) %all-gather.6.cloned.1.call-update) | async-done | bytes 15728656 | tf_op jit(solution)/shard_map/all_gather | solution.py:90
  259.8 31.6 %fusion.11 = f32[1536,1024]{1,0:T(8,128)S(1)} fusion(f32[2560,1536]{1,0:T(8,128)} %all-gather.6.cloned.1.call-done, f32[2560,1024]{1,0:T(8,128)} %all-gather.4.cloned.1.call-done), kind=kOutput, calls=%fused_computation.55 | convolution fusion | flops 24159191040 | bytes 32505856 | tf_op jit(solution)/shard_map/dot_general | solution.py:79
  292.1 2.2 pad_maximum_fusion
  294.3 5.0 %all-to-all-start.2 = ((f32[2,16,48,512]{3,2,0,1:T(8,128)}), f32[2,16,48,512]{3,2,0,1:T(8,128)S(1)}, u32[]{:S(2)}, u32[]{:S(2)}) async-start(f32[2,16,48,512]{3,2,0,1:T(8,128)} %pad_maximum_fusion), calls=%async_computation.2 | async-start | bytes 6291456 | tf_op jit(solution)/shard_map/all_to_all | solution.py:97
  299.3 2.5 all-gather.8.cloned.1.call-done
  301.9 12.1 %fusion.12 = f32[512,1024]{1,0:T(8,128)S(1)} fusion(f32[2560,512]{1,0:T(8,128)} %all-gather.8.cloned.1.call-done, f32[2560,1024]{1,0:T(8,128)} %all-gather.4.cloned.1.call-done), kind=kOutput, calls=%fused_computation.56 | convolution fusion | flops 8053063680 | bytes 17825792 | tf_op jit(solution)/shard_map/dot_general | solution.py:79
  315.2 24.4 %all-to-all-done.2 = f32[2,16,48,512]{3,2,0,1:T(8,128)S(1)} async-done(((f32[2,16,48,512]{3,2,0,1:T(8,128)}), f32[2,16,48,512]{3,2,0,1:T(8,128)S(1)}, u32[]{:S(2)}, u32[]{:S(2)}) %all-to-all-start.2) | async-done | bytes 3145760 | tf_op jit(solution)/shard_map/all_to_all | solution.py:97
  339.7 10.1 %all-to-all-start.3 = ((f32[2,16,16,512]{3,2,0,1:T(8,128)}), f32[2,16,16,512]{3,2,0,1:T(8,128)}, u32[]{:S(2)}, u32[]{:S(2)}) async-start(f32[2,16,16,512]{3,2,0,1:T(8,128)} %pad_maximum_fusion.1), calls=%async_computation.3 | async-start | bytes 2097152 | tf_op jit(solution)/shard_map/all_to_all | solution.py:97
  349.7 2.1 copy.60
  351.8 13.8 %all-to-all-done.3 = f32[2,16,16,512]{3,2,0,1:T(8,128)} async-done(((f32[2,16,16,512]{3,2,0,1:T(8,128)}), f32[2,16,16,512]{3,2,0,1:T(8,128)}, u32[]{:S(2)}, u32[]{:S(2)}) %all-to-all-start.3) | async-done | bytes 1048608 | tf_op jit(solution)/shard_map/all_to_all | solution.py:97
  367.0 4.2 %maximum_bitcast_fusion = f32[2,64,8192]{2,1,0:T(8,128)} fusion(f32[2,1,16,8192]{3,2,0,1:T(8,128)S(1)} %bitcast.75, f32[2,1,48,8192]{3,2,0,1:T(8,128)} %bitcast.67), kind=kLoop, calls=%fused_computation.3 | loop fusion | flops 1048576 | bytes 8388608 | tf_op jit(solution)/shard_map/reshape | solution.py:99
  (40 shorter events, 13.1 us)
Async XLA Ops:
  6.5 2.7 copy-start
  6.5 163.6 %all-gather.4.cloned.1.call-start = ((), (), s32[]{:S(2)}) async-start(), calls=%async_computation.4 | async-start | bytes 11796480 | tf_op jit(solution)/shard_map/all_gather | solution.py:73
  11.6 8.5 %copy-start.2 = (s32[64]{0:T(128)S(1)}, s32[64]{0:T(128)}, u32[]{:S(2)}) copy-start(s32[64]{0:T(128)} %param.7) | copy-start | bytes 772
  11.6 8.7 %copy-start.3 = (s32[7]{0:T(128)S(1)}, s32[7]{0:T(128)}, u32[]{:S(2)}) copy-start(s32[7]{0:T(128)} %param.8) | copy-start | bytes 88
  11.6 47.9 %all-to-all-start = ((f32[2,8,8,16,160]{4,3,1,0,2:T(8,128)}), f32[2,8,8,16,160]{4,3,1,0,2:T(8,128)S(1)}, u32[]{:S(2)}, u32[]{:S(2)}) async-start(f32[2,8,8,16,160]{4,3,1,0,2:T(8,128)} %copy.45), calls=%async_computation | async-start | bytes 4194304 | tf_op jit(solution)/shard_map/all_to_all | solution.py:37
  64.9 4.3 %copy-start.1 = (s32[1024]{0:T(1024)S(1)}, s32[1024]{0:T(1024)}, u32[]{:S(2)}) copy-start(s32[1024]{0:T(1024)} %constant.116) | copy-start | bytes 12292
  64.9 42.1 %all-to-all-start.1 = ((f32[2,8,8,16,160]{4,3,2,0,1:T(8,128)}), f32[2,8,8,16,160]{4,3,2,0,1:T(8,128)S(1)}, u32[]{:S(2)}, u32[]{:S(2)}) async-start(f32[2,8,8,16,160]{4,3,2,0,1:T(8,128)} %copy_select_fusion), calls=%async_computation.1 | async-start | bytes 4194304 | tf_op jit(solution)/shard_map/all_to_all | solution.py:43
  69.0 190.8 %all-gather.6.cloned.1.call-start = ((), (), s32[]{:S(2)}) async-start(), calls=%async_computation.5 | async-start | bytes 16711680 | tf_op jit(solution)/shard_map/all_gather | solution.py:90
  174.9 126.9 %all-gather.8.cloned.1.call-start = ((), (), s32[]{:S(2)}) async-start(), calls=%async_computation.6 | async-start | bytes 5570560 | tf_op jit(solution)/shard_map/all_gather | solution.py:90
  294.3 45.3 %all-to-all-start.2 = ((f32[2,16,48,512]{3,2,0,1:T(8,128)}), f32[2,16,48,512]{3,2,0,1:T(8,128)S(1)}, u32[]{:S(2)}, u32[]{:S(2)}) async-start(f32[2,16,48,512]{3,2,0,1:T(8,128)} %pad_maximum_fusion), calls=%async_computation.2 | async-start | bytes 6291456 | tf_op jit(solution)/shard_map/all_to_all | solution.py:97
  339.7 26.0 %all-to-all-start.3 = ((f32[2,16,16,512]{3,2,0,1:T(8,128)}), f32[2,16,16,512]{3,2,0,1:T(8,128)}, u32[]{:S(2)}, u32[]{:S(2)}) async-start(f32[2,16,16,512]{3,2,0,1:T(8,128)} %pad_maximum_fusion.1), calls=%async_computation.3 | async-start | bytes 2097152 | tf_op jit(solution)/shard_map/all_to_all | solution.py:97
Sparse Core Ops, SparseCore 0:
  9.7 160.4 all-gather.3
  175.1 84.6 all-gather.5
  261.5 40.3 all-gather.7

commit v12 on v11

--- a/solution.py
+++ b/solution.py
@@ -69,7 +69,10 @@
     col_count = lax.axis_size(COL)
     rows = left.shape[1]
     cols = right.shape[2]
-    rpiece = jnp.swapaxes(right, 0, 1).reshape(right.shape[1], 2 * cols)
+    splits = 2
+    sub = cols // splits
+    rpiece = jnp.transpose(right.reshape(2, right.shape[1], splits, sub), (1, 2, 0, 3))
+    rpiece = rpiece.reshape(right.shape[1], 2 * cols)
     rall = lax.all_gather(rpiece, ROW, axis=0, tiled=True)
     lp = permute_left(left, prefix_owner, qubit_order, row_count, col_count)
     lt = jnp.swapaxes(lp, 1, 2)
@@ -80,7 +83,7 @@
     outs = []
     prev = None
     start = 0
-    for qp in part_sizes(rows // col_count):
+    for p, qp in enumerate(part_sizes(rows // col_count)):
         part = qp * col_count
         piece = lt[:, :, start:start + part]
         start += part
@@ -89,12 +92,20 @@
             piece = lax.optimization_barrier((piece, prev))[0]
         lall = lax.all_gather(piece, COL, axis=0, tiled=True)
         prev = lall
-        q = dot(lall, rall)
-        re = q[:part, :cols] - q[part:, cols:]
-        im = q[:part, cols:] + q[part:, :cols]
-        tile = jnp.stack([re, im], axis=0)
-        tile = tile.reshape(2, col_count, qp, cols)
-        outs.append(lax.all_to_all(tile, COL, split_axis=1, concat_axis=3, tiled=True))
+        pieces = []
+        nsplit = splits if p == 0 else 1
+        step = splits // nsplit
+        for j in range(nsplit):
+            q = dot(lall, rall[:, j * step * 2 * sub:(j + 1) * step * 2 * sub])
+            q = q.reshape(2 * part, step, 2, sub)
+            re = q[:part, :, 0] - q[part:, :, 1]
+            im = q[:part, :, 1] + q[part:, :, 0]
+            tile = jnp.stack([re, im], axis=0)
+            tile = tile.reshape(2, col_count, qp, step * sub)
+            got = lax.all_to_all(tile, COL, split_axis=1, concat_axis=3, tiled=True)
+            pieces.append(got.reshape(2, qp, col_count, step, sub))
+        got = jnp.concatenate(pieces, axis=3) if nsplit > 1 else pieces[0]
+        outs.append(got.reshape(2, 1, qp, col_count * cols))
     out = jnp.concatenate(outs, axis=2)
     return out.reshape(2, rows // col_count, col_count * cols)
 

time: 378 us -> 392 us (1.037); the launches traced: 378 us -> 384 us
  waiting for transfers between devices: 245 us -> 212 us
  local copies, waits for them, and re-layouts: 32.8 us -> 59.4 us
  matrix products: 43.7 us -> 49.3 us
  other arithmetic: 14.7 us -> 19 us
    all_to_all x2 -> x3, waiting for transfers between devices: 38.3 us -> 7.96 us  [body(): got = lax.all_to_all(tile, COL, split_axis=1, concat_axis=3, tiled=True)]
    unnamed x11 -> x33, local copies, waits for them, and re-layouts: 2.58 us -> 14.4 us
    reshape x1 -> x5, local copies, waits for them, and re-layouts: 2.64 us -> 11.9 us  [the longest x1 3.68 us: body(): outs.append(got.reshape(2, 1, qp, col_count * cols))]
    dot_general x2 -> x3, matrix products: 43.7 us -> 49.3 us  [body(): lax.dot_general(a, b, dims, preferred_element_type=jnp.float32, precision...]
    sub x2 -> x3, other arithmetic: 0.96 us -> 5.33 us  [body(): re = q[:part, :, 0] - q[part:, :, 1]]
    all_to_all x2 -> x3, starting transfers between devices: 15.1 us -> 17.7 us  [body(): got = lax.all_to_all(tile, COL, split_axis=1, concat_axis=3, tiled=True)]
  transfers between devices with their start and end apart: 7 -> 8, of which waited for: 7 -> 5; matrix products, arithmetic and copies ran while one was open for 21% -> 29% of each run, Pallas kernels for 0% -> 0%
where the time goes in v12:
time: 392 us; the launch traced here: 384 us
  waiting for transfers between devices  212 us (54%)
  local copies, waits for them, and re-layouts  59.4 us (15%)
  matrix products  49.3 us (13%)
  starting transfers between devices  30.7 us (8%)
  other arithmetic  19 us (5%)
  between operations  13.7 us (3%)
    all_gather x2, waiting for transfers between devices, body(): lall = lax.all_gather(piece, COL, axis=0, tiled=True)  82.1 us
    all_gather x1, waiting for transfers between devices, body(): rall = lax.all_gather(rpiece, ROW, axis=0, tiled=True)  49.8 us
    dot_general x3, matrix products, body(): lax.dot_general(a, b, dims, preferred_element_type=jnp.float32, precision...  49.3 us
    all_to_all x1, waiting for transfers between devices, permute_left(): x = lax.all_to_all(x, ROW, split_axis=2, concat_axis=2, tiled=True)  39.1 us
    all_to_all x1, waiting for transfers between devices, permute_left(): y = lax.all_to_all(y, ROW, split_axis=1, concat_axis=1, tiled=True)  33.3 us
    all_to_all x3, starting transfers between devices, body(): got = lax.all_to_all(tile, COL, split_axis=1, concat_axis=3, tiled=True)  17.7 us
    unnamed x33, local copies, waits for them, and re-layouts  14.4 us
    gather x2, local copies, waits for them, and re-layouts, permute_left(): return jnp.take(y, jnp.take(idx, part_order(rows, col_count)), axis=1)  10.3 us
  transfers between devices with their start and end apart: 8, of which 5 were waited for; matrix products, arithmetic and copies ran while one was open for 29% of the time, Pallas kernels for 0%

profile of v12, /device:TPU:1, one launch (start us, length us, event | category | flops | bytes accessed | tf_op | source)
XLA Modules:
  0.0 384.3 jit_solution(10737170278134178299)
XLA Ops:
  14.2 8.5 %all-to-all-start = ((f32[2,8,8,16,160]{4,3,1,0,2:T(8,128)}), f32[2,8,8,16,160]{4,3,1,0,2:T(8,128)S(1)}, u32[]{:S(2)}, u32[]{:S(2)}) async-start(f32[2,8,8,16,160]{4,3,1,0,2:T(8,128)} %copy.67), calls=%async_computation | async-start | bytes 4194304 | tf_op jit(solution)/shard_map/all_to_all | solution.py:37
  23.0 39.1 %all-to-all-done = f32[2,8,8,16,160]{4,3,1,0,2:T(8,128)S(1)} async-done(((f32[2,8,8,16,160]{4,3,1,0,2:T(8,128)}), f32[2,8,8,16,160]{4,3,1,0,2:T(8,128)S(1)}, u32[]{:S(2)}, u32[]{:S(2)}) %all-to-all-start) | async-done | bytes 1310752 | tf_op jit(solution)/shard_map/all_to_all | solution.py:37
  67.5 4.1 %all-to-all-start.1 = ((f32[2,8,8,16,160]{4,3,2,0,1:T(8,128)}), f32[2,8,8,16,160]{4,3,2,0,1:T(8,128)S(1)}, u32[]{:S(2)}, u32[]{:S(2)}) async-start(f32[2,8,8,16,160]{4,3,2,0,1:T(8,128)} %copy_select_fusion), calls=%async_computation.1 | async-start | bytes 4194304 | tf_op jit(solution)/shard_map/all_to_all | solution.py:43
  71.8 4.5 %gather_fusion = s32[1024]{0:T(1024)S(1)} fusion(s32[1024]{0:T(1024)S(1)} %add_bitcast_fusion, s32[1024]{0:T(1024)S(1)} %broadcast_clamp_fusion), kind=kCustom, calls=%fused_computation | custom fusion | bytes 12288 | tf_op jit(solution)/shard_map/jit(_take)/gather | solution.py:49
  76.3 33.3 %all-to-all-done.1 = f32[2,8,8,16,160]{4,3,2,0,1:T(8,128)S(1)} async-done(((f32[2,8,8,16,160]{4,3,2,0,1:T(8,128)}), f32[2,8,8,16,160]{4,3,2,0,1:T(8,128)S(1)}, u32[]{:S(2)}, u32[]{:S(2)}) %all-to-all-start.1) | async-done | bytes 1310752 | tf_op jit(solution)/shard_map/all_to_all | solution.py:43
  109.8 2.9 copy.71
  112.8 5.7 %gather_fusion.2 = f32[1024,2,160]{2,1,0:T(2,128)S(1)} fusion(f32[2,1024,160]{2,0,1:T(2,128)} %copy.71, s32[1024]{0:T(1024)S(1)} %fusion.12), kind=kCustom, calls=%fused_computation.2 | custom fusion | bytes 2625536 | tf_op jit(solution)/shard_map/jit(_take)/gather | solution.py:49
  118.5 4.5 %select_bitcast_fusion = f32[2,160,1024]{1,0,2:T(2,128)} fusion(f32[1024,2,160]{2,1,0:T(2,128)S(1)} %gather_fusion.2, pred[1024]{0:T(1024)(128)(4,1)S(1)} %compare_and_fusion.1), kind=kLoop, calls=%fused_computation.10 | loop fusion | flops 327680 | bytes 2622464 | tf_op jit(solution)/shard_map/jit(_take)/select_n | solution.py:49
  123.0 49.8 %all-gather.4.cloned.1.call-done = f32[2560,1024]{1,0:T(8,128)} async-done(((f32[320,1024]{1,0:T(8,128)}), f32[2560,1024]{1,0:T(8,128)}) %all-gather.4.cloned.1.call-update) | async-done | bytes 10485776 | tf_op jit(solution)/shard_map/all_gather | solution.py:76
  180.3 82.0 %all-gather.6.cloned.1.call-done = f32[2560,1536]{1,0:T(8,128)} async-done(((f32[160,1536]{1,0:T(8,128)}), f32[2560,1536]{1,0:T(8,128)}) %all-gather.6.cloned.1.call-update) | async-done | bytes 15728656 | tf_op jit(solution)/shard_map/all_gather | solution.py:93
  262.4 17.9 %fusion.2 = f32[1536,512]{0,1:T(8,128)S(1)} fusion(f32[2560,1536]{1,0:T(8,128)} %all-gather.6.cloned.1.call-done, f32[2560,1024]{1,0:T(8,128)} %all-gather.4.cloned.1.call-done), kind=kOutput, calls=%fused_computation.5 | convolution fusion | flops 12079595520 | bytes 24117248 | tf_op jit(solution)/shard_map/dot_general | solution.py:82
  287.0 5.6 %all-to-all-start.2 = ((f32[2,16,48,256]{3,2,0,1:T(8,128)}), f32[2,16,48,256]{3,2,0,1:T(8,128)S(1)}, u32[]{:S(2)}, u32[]{:S(2)}) async-start(f32[2,16,48,256]{3,2,0,1:T(8,128)} %copy.78), calls=%async_computation.2 | async-start | bytes 3145728 | tf_op jit(solution)/shard_map/all_to_all | solution.py:105
  292.6 18.1 %fusion = f32[1536,512]{0,1:T(8,128)S(1)} fusion(f32[2560,1536]{1,0:T(8,128)} %all-gather.6.cloned.1.call-done, f32[2560,1024]{1,0:T(8,128)} %all-gather.4.cloned.1.call-done), kind=kOutput, calls=%fused_computation.3 | convolution fusion | flops 12079595520 | bytes 24117248 | tf_op jit(solution)/shard_map/dot_general | solution.py:82
  312.1 2.3 copy.92
  314.4 2.3 copy.93
  322.1 6.0 %all-to-all-start.3 = ((f32[2,16,48,256]{3,2,0,1:T(8,128)}), f32[2,16,48,256]{3,2,0,1:T(8,128)}, u32[]{:S(2)}, u32[]{:S(2)}) async-start(f32[2,16,48,256]{3,2,0,1:T(8,128)} %copy.83), calls=%async_computation.3 | async-start | bytes 3145728 | tf_op jit(solution)/shard_map/all_to_all | solution.py:105
  328.2 13.4 %fusion.19 = f32[512,1024]{1,0:T(8,128)} fusion(f32[2560,512]{1,0:T(8,128)} %all-gather.8.cloned.1.call-done, f32[2560,1024]{1,0:T(8,128)} %all-gather.4.cloned.1.call-done), kind=kOutput, calls=%fused_computation.64 | convolution fusion | flops 8053063680 | bytes 17825792 | tf_op jit(solution)/shard_map/dot_general | solution.py:82
  341.6 3.0 reshape.384
  344.6 3.7 fusion.5
  350.2 6.1 %all-to-all-start.4 = ((f32[2,16,16,512]{3,2,0,1:T(8,128)}), f32[2,16,16,512]{3,2,0,1:T(8,128)}, u32[]{:S(2)}, u32[]{:S(2)}) async-start(f32[2,16,16,512]{3,2,0,1:T(8,128)} %pad_maximum_fusion.3), calls=%async_computation.4 | async-start | bytes 2097152 | tf_op jit(solution)/shard_map/all_to_all | solution.py:105
  358.0 2.4 copy.84
  360.4 3.7 reshape.382
  364.1 8.0 %all-to-all-done.4 = f32[2,16,16,512]{3,2,0,1:T(8,128)} async-done(((f32[2,16,16,512]{3,2,0,1:T(8,128)}), f32[2,16,16,512]{3,2,0,1:T(8,128)}, u32[]{:S(2)}, u32[]{:S(2)}) %all-to-all-start.4) | async-done | bytes 1048608 | tf_op jit(solution)/shard_map/all_to_all | solution.py:105
  373.4 4.2 %maximum_bitcast_fusion = f32[2,64,8192]{2,1,0:T(8,128)} fusion(f32[2,1,16,8192]{3,2,0,1:T(8,128)S(1)} %bitcast.71, f32[2,1,48,8192]{3,2,0,1:T(8,128)} %reshape.382), kind=kLoop, calls=%fused_computation.7 | loop fusion | flops 1048576 | bytes 8388608 | tf_op jit(solution)/shard_map/reshape | solution.py:110
  (80 shorter events, 39.6 us)
Async XLA Ops:
  6.5 166.3 %all-gather.4.cloned.1.call-start = ((), (), s32[]{:S(2)}) async-start(), calls=%async_computation.5 | async-start | bytes 11796480 | tf_op jit(solution)/shard_map/all_gather | solution.py:76
  9.7 2.2 copy-start.7
  14.2 8.5 %copy-start.9 = (s32[64]{0:T(128)S(1)}, s32[64]{0:T(128)}, u32[]{:S(2)}) copy-start(s32[64]{0:T(128)} %param.7) | copy-start | bytes 772
  14.2 8.7 %copy-start.10 = (s32[7]{0:T(128)S(1)}, s32[7]{0:T(128)}, u32[]{:S(2)}) copy-start(s32[7]{0:T(128)} %param.8) | copy-start | bytes 88
  14.2 47.9 %all-to-all-start = ((f32[2,8,8,16,160]{4,3,1,0,2:T(8,128)}), f32[2,8,8,16,160]{4,3,1,0,2:T(8,128)S(1)}, u32[]{:S(2)}, u32[]{:S(2)}) async-start(f32[2,8,8,16,160]{4,3,1,0,2:T(8,128)} %copy.67), calls=%async_computation | async-start | bytes 4194304 | tf_op jit(solution)/shard_map/all_to_all | solution.py:37
  67.5 4.3 %copy-start.8 = (s32[1024]{0:T(1024)S(1)}, s32[1024]{0:T(1024)}, u32[]{:S(2)}) copy-start(s32[1024]{0:T(1024)} %constant.116) | copy-start | bytes 12292
  67.5 42.1 %all-to-all-start.1 = ((f32[2,8,8,16,160]{4,3,2,0,1:T(8,128)}), f32[2,8,8,16,160]{4,3,2,0,1:T(8,128)S(1)}, u32[]{:S(2)}, u32[]{:S(2)}) async-start(f32[2,8,8,16,160]{4,3,2,0,1:T(8,128)} %copy_select_fusion), calls=%async_computation.1 | async-start | bytes 4194304 | tf_op jit(solution)/shard_map/all_to_all | solution.py:43
  71.6 190.8 %all-gather.6.cloned.1.call-start = ((), (), s32[]{:S(2)}) async-start(), calls=%async_computation.6 | async-start | bytes 16711680 | tf_op jit(solution)/shard_map/all_gather | solution.py:93
  177.6 150.6 %all-gather.8.cloned.1.call-start = ((), (), s32[]{:S(2)}) async-start(), calls=%async_computation.7 | async-start | bytes 5570560 | tf_op jit(solution)/shard_map/all_gather | solution.py:93
  282.0 2.3 copy-start.3
  283.2 1.2 copy-start.4
  284.3 1.2 copy-start.5
  287.0 35.1 %all-to-all-start.2 = ((f32[2,16,48,256]{3,2,0,1:T(8,128)}), f32[2,16,48,256]{3,2,0,1:T(8,128)S(1)}, u32[]{:S(2)}, u32[]{:S(2)}) async-start(f32[2,16,48,256]{3,2,0,1:T(8,128)} %copy.78), calls=%async_computation.2 | async-start | bytes 3145728 | tf_op jit(solution)/shard_map/all_to_all | solution.py:105
  317.8 2.7 copy-start.2
  319.0 1.6 copy-start.6
  322.1 6.1 %copy-start = (f32[2,16,48,256]{3,2,0,1:T(8,128)}, f32[2,16,48,256]{3,2,0,1:T(8,128)S(1)}, u32[]{:S(2)}) copy-start(f32[2,16,48,256]{3,2,0,1:T(8,128)S(1)} %all-to-all-done.2) | copy-start | bytes 4718596
  322.1 28.1 %all-to-all-start.3 = ((f32[2,16,48,256]{3,2,0,1:T(8,128)}), f32[2,16,48,256]{3,2,0,1:T(8,128)}, u32[]{:S(2)}, u32[]{:S(2)}) async-start(f32[2,16,48,256]{3,2,0,1:T(8,128)} %copy.83), calls=%async_computation.3 | async-start | bytes 3145728 | tf_op jit(solution)/shard_map/all_to_all | solution.py:105
  349.1 7.2 %copy-start.1 = (f32[2,16,48,256]{3,2,0,1:T(8,128)S(1)}, f32[2,16,48,256]{3,2,0,1:T(8,128)}, u32[]{:S(2)}) copy-start(f32[2,16,48,256]{3,2,0,1:T(8,128)} %copy-done) | copy-start | bytes 4718596
  350.2 21.9 %all-to-all-start.4 = ((f32[2,16,16,512]{3,2,0,1:T(8,128)}), f32[2,16,16,512]{3,2,0,1:T(8,128)}, u32[]{:S(2)}, u32[]{:S(2)}) async-start(f32[2,16,16,512]{3,2,0,1:T(8,128)} %pad_maximum_fusion.3), calls=%async_computation.4 | async-start | bytes 2097152 | tf_op jit(solution)/shard_map/all_to_all | solution.py:105
Sparse Core Ops, SparseCore 0:
  11.9 160.8 all-gather.3
  177.7 84.6 all-gather.5
  264.1 55.6 all-gather.7

commit v13 on v11

--- a/solution.py
+++ b/solution.py
@@ -1,7 +1,11 @@
+import functools
+
 import jax
 import jax.numpy as jnp
 import numpy as np
 from jax import lax
+from jax.experimental import pallas as pl
+from jax.experimental.pallas import tpu as pltpu
 from jax.sharding import Mesh
 from jax.sharding import PartitionSpec as P
 
@@ -64,6 +68,56 @@
     return np.asarray(pos, np.int32)
 
 
+MESH_ID = pl.DeviceIdType.MESH
+
+
+def scatter_kernel(ncol, tile_ref, out_ref, send, recv, own):
+    xh, z = lax.axis_index("xh"), lax.axis_index("z")
+    xl, y, core = lax.axis_index("xl"), lax.axis_index("y"), lax.axis_index("core")
+    ys = ncol // 4
+    me = (xl * ys + y) * 2 + core
+    w = tile_ref.shape[-1]
+
+    def col_dev(j):
+        return (xh, z, j // (ys * 2), (j // 2) % ys, j % 2)
+
+    barrier = pltpu.get_barrier_semaphore()
+    for off in range(1, ncol):
+        pl.semaphore_signal(barrier, 1, device_id=col_dev((me + off) % ncol), device_id_type=MESH_ID)
+    pl.semaphore_wait(barrier, ncol - 1)
+
+    dst = out_ref.at[:, :, pl.ds(pl.multiple_of(me * w, w), w)]
+    local = pltpu.make_async_copy(tile_ref.at[me], dst, own.at[0])
+    local.start()
+    copies = []
+    for off in range(1, ncol):
+        j = (me + off) % ncol
+        c = pltpu.make_async_remote_copy(
+            tile_ref.at[j], dst, send.at[off], recv.at[off],
+            device_id=col_dev(j), device_id_type=MESH_ID)
+        c.start()
+        copies.append(c)
+    local.wait()
+    for c in copies:
+        c.wait()
+
+
+def scatter_cols(tile, ncol):
+    _, b, q, w = tile.shape
+    return pl.pallas_call(
+        functools.partial(scatter_kernel, ncol),
+        out_shape=jax.ShapeDtypeStruct((b, q, ncol * w), tile.dtype),
+        in_specs=[pl.BlockSpec(memory_space=pl.ANY)],
+        out_specs=pl.BlockSpec(memory_space=pl.ANY),
+        scratch_shapes=[
+            pltpu.SemaphoreType.DMA((ncol,)),
+            pltpu.SemaphoreType.DMA((ncol,)),
+            pltpu.SemaphoreType.DMA((1,)),
+        ],
+        compiler_params=pltpu.CompilerParams(collective_id=0, has_side_effects=True),
+    )(tile)
+
+
 def body(left, right, prefix_owner, qubit_order):
     row_count = lax.axis_size(ROW)
     col_count = lax.axis_size(COL)
@@ -92,9 +146,13 @@
         q = dot(lall, rall)
         re = q[:part, :cols] - q[part:, cols:]
         im = q[:part, cols:] + q[part:, :cols]
-        tile = jnp.stack([re, im], axis=0)
-        tile = tile.reshape(2, col_count, qp, cols)
-        outs.append(lax.all_to_all(tile, COL, split_axis=1, concat_axis=3, tiled=True))
+        if start == rows:
+            tile = jnp.stack([re.reshape(col_count, qp, cols), im.reshape(col_count, qp, cols)], axis=1)
+            outs.append(scatter_cols(tile, col_count).reshape(2, 1, qp, col_count * cols))
+        else:
+            tile = jnp.stack([re, im], axis=0)
+            tile = tile.reshape(2, col_count, qp, cols)
+            outs.append(lax.all_to_all(tile, COL, split_axis=1, concat_axis=3, tiled=True))
     out = jnp.concatenate(outs, axis=2)
     return out.reshape(2, rows // col_count, col_count * cols)
 

time: 378 us -> 377 us (level)
  blocking collectives: 0 us -> 42.7 us
  waiting for transfers between devices: 245 us -> 204 us
  Pallas kernels: 0 us -> 16.6 us
  starting transfers between devices: 27.9 us -> 12.8 us
    all_to_all x0 -> x1, blocking collectives: none -> 42.7 us  [body(): lax.all_to_all(tile, COL, split_axis=1, concat_axis=3, tiled=True)]
    all_to_all x2 -> x0, waiting for transfers between devices: 38.3 us -> none  [body(): lax.all_to_all(tile, COL, split_axis=1, concat_axis=3, tiled=True)]
    pallas_call x0 -> x1, Pallas kernels: none -> 16.6 us  [scatter_cols(): pl.pallas_call(functools.partial(scatter_kernel, ncol), out_shape=jax.Sha...]
    all_to_all x2 -> x0, starting transfers between devices: 15.1 us -> none  [body(): lax.all_to_all(tile, COL, split_axis=1, concat_axis=3, tiled=True)]
  transfers between devices with their start and end apart: 7 -> 5, of which waited for: 7 -> 4; matrix products, arithmetic and copies ran while one was open for 21% -> 16% of each run, Pallas kernels for 0% -> 0%
where the time goes in v13:
time: 377 us; the launch traced here: 376 us
  waiting for transfers between devices  204 us (54%)
  matrix products  43.7 us (12%)
  blocking collectives  42.7 us (11%)
  local copies, waits for them, and re-layouts  29.8 us (8%)
  Pallas kernels  16.6 us (4%)
  between operations  13.3 us (4%)
  starting transfers between devices  12.8 us (3%)
  other arithmetic  12.2 us (3%)
    all_gather x2, waiting for transfers between devices, body(): lall = lax.all_gather(piece, COL, axis=0, tiled=True)  82.2 us
    all_gather x1, waiting for transfers between devices, body(): rall = lax.all_gather(rpiece, ROW, axis=0, tiled=True)  49.8 us
    dot_general x2, matrix products, body(): lax.dot_general(a, b, dims, preferred_element_type=jnp.float32, precision...  43.7 us
    all_to_all x1, blocking collectives, body(): lax.all_to_all(tile, COL, split_axis=1, concat_axis=3, tiled=True)  42.7 us
    all_to_all x1, waiting for transfers between devices, permute_left(): x = lax.all_to_all(x, ROW, split_axis=2, concat_axis=2, tiled=True)  39.1 us
    all_to_all x1, waiting for transfers between devices, permute_left(): y = lax.all_to_all(y, ROW, split_axis=1, concat_axis=1, tiled=True)  33.3 us
    pallas_call x1, Pallas kernels, scatter_cols(): pl.pallas_call(functools.partial(scatter_kernel, ncol), out_shape=jax.Sha...  16.6 us
    gather x2, local copies, waits for them, and re-layouts, permute_left(): return jnp.take(y, jnp.take(idx, part_order(rows, col_count)), axis=1)  10.3 us
  transfers between devices with their start and end apart: 5, of which 4 were waited for; matrix products, arithmetic and copies ran while one was open for 16% of the time, Pallas kernels for 0%

profile of v13, /device:TPU:1, one launch (start us, length us, event | category | flops | bytes accessed | tf_op | source)
XLA Modules:
  0.0 375.5 jit_solution(16068413456578264312)
XLA Ops:
  6.5 2.6 copy.49
  10.0 1.6 copy.38
  11.6 8.5 %all-to-all-start = ((f32[2,8,8,16,160]{4,3,1,0,2:T(8,128)}), f32[2,8,8,16,160]{4,3,1,0,2:T(8,128)S(1)}, u32[]{:S(2)}, u32[]{:S(2)}) async-start(f32[2,8,8,16,160]{4,3,1,0,2:T(8,128)} %copy.38), calls=%async_computation | async-start | bytes 4194304 | tf_op jit(solution)/shard_map/all_to_all | solution.py:41
  20.4 39.1 %all-to-all-done = f32[2,8,8,16,160]{4,3,1,0,2:T(8,128)S(1)} async-done(((f32[2,8,8,16,160]{4,3,1,0,2:T(8,128)}), f32[2,8,8,16,160]{4,3,1,0,2:T(8,128)S(1)}, u32[]{:S(2)}, u32[]{:S(2)}) %all-to-all-start) | async-done | bytes 1310752 | tf_op jit(solution)/shard_map/all_to_all | solution.py:41
  59.5 1.6 copy.39
  61.1 2.3 gather_fusion.1
  63.3 1.5 copy_select_fusion
  64.9 4.1 %all-to-all-start.1 = ((f32[2,8,8,16,160]{4,3,2,0,1:T(8,128)}), f32[2,8,8,16,160]{4,3,2,0,1:T(8,128)S(1)}, u32[]{:S(2)}, u32[]{:S(2)}) async-start(f32[2,8,8,16,160]{4,3,2,0,1:T(8,128)} %copy_select_fusion), calls=%async_computation.1 | async-start | bytes 4194304 | tf_op jit(solution)/shard_map/all_to_all | solution.py:47
  69.1 4.5 %gather_fusion = s32[1024]{0:T(1024)S(1)} fusion(s32[1024]{0:T(1024)S(1)} %add_bitcast_fusion, s32[1024]{0:T(1024)S(1)} %broadcast_clamp_fusion), kind=kCustom, calls=%fused_computation | custom fusion | bytes 12288 | tf_op jit(solution)/shard_map/jit(_take)/gather | solution.py:53
  73.7 33.3 %all-to-all-done.1 = f32[2,8,8,16,160]{4,3,2,0,1:T(8,128)S(1)} async-done(((f32[2,8,8,16,160]{4,3,2,0,1:T(8,128)}), f32[2,8,8,16,160]{4,3,2,0,1:T(8,128)S(1)}, u32[]{:S(2)}, u32[]{:S(2)}) %all-to-all-start.1) | async-done | bytes 1310752 | tf_op jit(solution)/shard_map/all_to_all | solution.py:47
  107.2 2.9 copy.42
  110.2 5.8 %gather_fusion.2 = f32[1024,2,160]{2,1,0:T(2,128)S(1)} fusion(f32[2,1024,160]{2,0,1:T(2,128)} %copy.42, s32[1024]{0:T(1024)S(1)} %fusion.6), kind=kCustom, calls=%fused_computation.2 | custom fusion | bytes 2625536 | tf_op jit(solution)/shard_map/jit(_take)/gather | solution.py:53
  115.9 4.5 %select_bitcast_fusion = f32[2,160,1024]{1,0,2:T(2,128)} fusion(f32[1024,2,160]{2,1,0:T(2,128)S(1)} %gather_fusion.2, pred[1024]{0:T(1024)(128)(4,1)S(1)} %compare_and_fusion.1), kind=kLoop, calls=%fused_computation.6 | loop fusion | flops 327680 | bytes 2622464 | tf_op jit(solution)/shard_map/jit(_take)/select_n | solution.py:53
  120.4 49.8 %all-gather.4.cloned.1.call-done = f32[2560,1024]{1,0:T(8,128)} async-done(((f32[320,1024]{1,0:T(8,128)}), f32[2560,1024]{1,0:T(8,128)}) %all-gather.4.cloned.1.call-update) | async-done | bytes 10485776 | tf_op jit(solution)/shard_map/all_gather | solution.py:127
  170.2 1.9 slice_bitcast_fusion
  172.1 1.8 copy.44
  175.1 1.2 slice_bitcast_fusion.1
  177.6 82.2 %all-gather.6.cloned.1.call-done = f32[2560,1536]{1,0:T(8,128)} async-done(((f32[160,1536]{1,0:T(8,128)}), f32[2560,1536]{1,0:T(8,128)}) %all-gather.6.cloned.1.call-update) | async-done | bytes 15728656 | tf_op jit(solution)/shard_map/all_gather | solution.py:144
  259.8 31.6 %fusion.11 = f32[1536,1024]{1,0:T(8,128)S(1)} fusion(f32[2560,1536]{1,0:T(8,128)} %all-gather.6.cloned.1.call-done, f32[2560,1024]{1,0:T(8,128)} %all-gather.4.cloned.1.call-done), kind=kOutput, calls=%fused_computation.55 | convolution fusion | flops 24159191040 | bytes 32505856 | tf_op jit(solution)/shard_map/dot_general | solution.py:133
  292.4 42.7 %all_to_all.28 = f32[2,16,48,512]{3,2,0,1:T(8,128)S(1)} all-to-all(f32[2,16,48,512]{3,2,0,1:T(8,128)S(1)} %pad_maximum_fusion), channel_id=1, replica_groups=mesh['xh'=2,'z'=4,'xl'=2,'y'=4,'core'=2] {'xl','y','core'}, dimensions={1} | all-to-all | bytes 6291456 | tf_op jit(solution)/shard_map/all_to_all | solution.py:155
  335.5 12.1 %fusion.12 = f32[512,1024]{1,0:T(8,128)S(1)} fusion(f32[2560,512]{1,0:T(8,128)} %all-gather.8.cloned.1.call-done, f32[2560,1024]{1,0:T(8,128)} %all-gather.4.cloned.1.call-done), kind=kOutput, calls=%fused_computation.56 | convolution fusion | flops 8053063680 | bytes 17825792 | tf_op jit(solution)/shard_map/dot_general | solution.py:133
  347.8 1.0 pad_maximum_fusion.1.tile_ref
  348.9 16.6 %shard_map.55 = f32[2,16,8192]{2,1,0:T(8,128)} custom-call(f32[16,2,16,512]{3,2,1,0:T(8,128)} %pad_maximum_fusion.1.tile_ref), custom_call_target="tpu_custom_call" | custom-call | tf_op jit(solution)/shard_map/pallas_call | solution.py:107
  365.4 3.5 maximum_bitcast_fusion
  (37 shorter events, 5.6 us)
Async XLA Ops:
  6.5 2.7 copy-start
  6.5 163.6 %all-gather.4.cloned.1.call-start = ((), (), s32[]{:S(2)}) async-start(), calls=%async_computation.3 | async-start | bytes 11796480 | tf_op jit(solution)/shard_map/all_gather | solution.py:127
  11.6 8.5 %copy-start.2 = (s32[64]{0:T(128)S(1)}, s32[64]{0:T(128)}, u32[]{:S(2)}) copy-start(s32[64]{0:T(128)} %param.7) | copy-start | bytes 772
  11.6 8.7 %copy-start.3 = (s32[7]{0:T(128)S(1)}, s32[7]{0:T(128)}, u32[]{:S(2)}) copy-start(s32[7]{0:T(128)} %param.8) | copy-start | bytes 88
  11.6 47.9 %all-to-all-start = ((f32[2,8,8,16,160]{4,3,1,0,2:T(8,128)}), f32[2,8,8,16,160]{4,3,1,0,2:T(8,128)S(1)}, u32[]{:S(2)}, u32[]{:S(2)}) async-start(f32[2,8,8,16,160]{4,3,1,0,2:T(8,128)} %copy.38), calls=%async_computation | async-start | bytes 4194304 | tf_op jit(solution)/shard_map/all_to_all | solution.py:41
  64.9 4.3 %copy-start.1 = (s32[1024]{0:T(1024)S(1)}, s32[1024]{0:T(1024)}, u32[]{:S(2)}) copy-start(s32[1024]{0:T(1024)} %constant.116) | copy-start | bytes 12292
  64.9 42.1 %all-to-all-start.1 = ((f32[2,8,8,16,160]{4,3,2,0,1:T(8,128)}), f32[2,8,8,16,160]{4,3,2,0,1:T(8,128)S(1)}, u32[]{:S(2)}, u32[]{:S(2)}) async-start(f32[2,8,8,16,160]{4,3,2,0,1:T(8,128)} %copy_select_fusion), calls=%async_computation.1 | async-start | bytes 4194304 | tf_op jit(solution)/shard_map/all_to_all | solution.py:47
  69.0 190.8 %all-gather.6.cloned.1.call-start = ((), (), s32[]{:S(2)}) async-start(), calls=%async_computation.4 | async-start | bytes 16711680 | tf_op jit(solution)/shard_map/all_gather | solution.py:144
  174.9 160.5 %all-gather.8.cloned.1.call-start = ((), (), s32[]{:S(2)}) async-start(), calls=%async_computation.5 | async-start | bytes 5570560 | tf_op jit(solution)/shard_map/all_gather | solution.py:144
Sparse Core Ops, SparseCore 0:
  9.7 160.4 all-gather.3
  175.0 84.6 all-gather.5
  261.4 40.5 all-gather.7

commit v14 on v13

--- a/solution.py
+++ b/solution.py
@@ -102,7 +102,7 @@
         c.wait()
 
 
-def scatter_cols(tile, ncol):
+def scatter_cols(tile, ncol, cid):
     _, b, q, w = tile.shape
     return pl.pallas_call(
         functools.partial(scatter_kernel, ncol),
@@ -114,7 +114,7 @@
             pltpu.SemaphoreType.DMA((ncol,)),
             pltpu.SemaphoreType.DMA((1,)),
         ],
-        compiler_params=pltpu.CompilerParams(collective_id=0, has_side_effects=True),
+        compiler_params=pltpu.CompilerParams(collective_id=cid, has_side_effects=True),
     )(tile)
 
 
@@ -146,13 +146,8 @@
         q = dot(lall, rall)
         re = q[:part, :cols] - q[part:, cols:]
         im = q[:part, cols:] + q[part:, :cols]
-        if start == rows:
-            tile = jnp.stack([re.reshape(col_count, qp, cols), im.reshape(col_count, qp, cols)], axis=1)
-            outs.append(scatter_cols(tile, col_count).reshape(2, 1, qp, col_count * cols))
-        else:
-            tile = jnp.stack([re, im], axis=0)
-            tile = tile.reshape(2, col_count, qp, cols)
-            outs.append(lax.all_to_all(tile, COL, split_axis=1, concat_axis=3, tiled=True))
+        tile = jnp.stack([re.reshape(col_count, qp, cols), im.reshape(col_count, qp, cols)], axis=1)
+        outs.append(scatter_cols(tile, col_count, len(outs)).reshape(2, 1, qp, col_count * cols))
     out = jnp.concatenate(outs, axis=2)
     return out.reshape(2, rows // col_count, col_count * cols)
 

time: 377 us -> 390 us (1.034)
  Pallas kernels: 16.6 us -> 69.5 us
  blocking collectives: 42.7 us -> 0 us
    pallas_call x1 -> x2, Pallas kernels: 16.6 us -> 69.5 us  [scatter_cols(): pl.pallas_call(functools.partial(scatter_kernel, ncol), out_shape=jax.Sha...]
    all_to_all x1 -> x0, blocking collectives: 42.7 us -> none  [body(): lax.all_to_all(tile, COL, split_axis=1, concat_axis=3, tiled=True)]
  transfers between devices with their start and end apart: 5 -> 5, of which waited for: 4 -> 4; matrix products, arithmetic and copies ran while one was open for 16% -> 16% of each run, Pallas kernels for 0% -> 13%
where the time goes in v14:
time: 390 us; the launch traced here: 387 us
  waiting for transfers between devices  204 us (52%)
  Pallas kernels  69.5 us (18%)
  matrix products  43.7 us (11%)
  local copies, waits for them, and re-layouts  29.5 us (8%)
  other arithmetic  14 us (4%)
  between operations  13.3 us (3%)
  starting transfers between devices  12.8 us (3%)
    all_gather x2, waiting for transfers between devices, body(): lall = lax.all_gather(piece, COL, axis=0, tiled=True)  82.2 us
    pallas_call x2, Pallas kernels, scatter_cols(): pl.pallas_call(functools.partial(scatter_kernel, ncol), out_shape=jax.Sha...  69.5 us
    all_gather x1, waiting for transfers between devices, body(): rall = lax.all_gather(rpiece, ROW, axis=0, tiled=True)  49.8 us
    dot_general x2, matrix products, body(): lax.dot_general(a, b, dims, preferred_element_type=jnp.float32, precision...  43.7 us
    all_to_all x1, waiting for transfers between devices, permute_left(): x = lax.all_to_all(x, ROW, split_axis=2, concat_axis=2, tiled=True)  39.1 us
    all_to_all x1, waiting for transfers between devices, permute_left(): y = lax.all_to_all(y, ROW, split_axis=1, concat_axis=1, tiled=True)  33.3 us
    gather x2, local copies, waits for them, and re-layouts, permute_left(): return jnp.take(y, jnp.take(idx, part_order(rows, col_count)), axis=1)  10.3 us
    all_to_all x1, starting transfers between devices, permute_left(): x = lax.all_to_all(x, ROW, split_axis=2, concat_axis=2, tiled=True)  8.45 us
  transfers between devices with their start and end apart: 5, of which 4 were waited for; matrix products, arithmetic and copies ran while one was open for 16% of the time, Pallas kernels for 13%

profile of v14, /device:TPU:1, one launch (start us, length us, event | category | flops | bytes accessed | tf_op | source)
XLA Modules:
  0.0 387.3 jit_solution(4404112657643898178)
XLA Ops:
  6.5 2.6 copy.30
  10.0 1.6 copy.22
  11.6 8.5 %all-to-all-start = ((f32[2,8,8,16,160]{4,3,1,0,2:T(8,128)}), f32[2,8,8,16,160]{4,3,1,0,2:T(8,128)S(1)}, u32[]{:S(2)}, u32[]{:S(2)}) async-start(f32[2,8,8,16,160]{4,3,1,0,2:T(8,128)} %copy.22), calls=%async_computation | async-start | bytes 4194304 | tf_op jit(solution)/shard_map/all_to_all | solution.py:41
  20.4 39.1 %all-to-all-done = f32[2,8,8,16,160]{4,3,1,0,2:T(8,128)S(1)} async-done(((f32[2,8,8,16,160]{4,3,1,0,2:T(8,128)}), f32[2,8,8,16,160]{4,3,1,0,2:T(8,128)S(1)}, u32[]{:S(2)}, u32[]{:S(2)}) %all-to-all-start) | async-done | bytes 1310752 | tf_op jit(solution)/shard_map/all_to_all | solution.py:41
  59.5 1.6 copy.23
  61.1 2.3 gather_fusion.1
  63.3 1.5 copy_select_fusion
  64.9 4.1 %all-to-all-start.1 = ((f32[2,8,8,16,160]{4,3,2,0,1:T(8,128)}), f32[2,8,8,16,160]{4,3,2,0,1:T(8,128)S(1)}, u32[]{:S(2)}, u32[]{:S(2)}) async-start(f32[2,8,8,16,160]{4,3,2,0,1:T(8,128)} %copy_select_fusion), calls=%async_computation.1 | async-start | bytes 4194304 | tf_op jit(solution)/shard_map/all_to_all | solution.py:47
  69.1 4.5 %gather_fusion = s32[1024]{0:T(1024)S(1)} fusion(s32[1024]{0:T(1024)S(1)} %add_bitcast_fusion, s32[1024]{0:T(1024)S(1)} %broadcast_clamp_fusion), kind=kCustom, calls=%fused_computation | custom fusion | bytes 12288 | tf_op jit(solution)/shard_map/jit(_take)/gather | solution.py:53
  73.7 33.3 %all-to-all-done.1 = f32[2,8,8,16,160]{4,3,2,0,1:T(8,128)S(1)} async-done(((f32[2,8,8,16,160]{4,3,2,0,1:T(8,128)}), f32[2,8,8,16,160]{4,3,2,0,1:T(8,128)S(1)}, u32[]{:S(2)}, u32[]{:S(2)}) %all-to-all-start.1) | async-done | bytes 1310752 | tf_op jit(solution)/shard_map/all_to_all | solution.py:47
  107.2 2.9 copy.26
  110.2 5.7 %gather_fusion.2 = f32[1024,2,160]{2,1,0:T(2,128)S(1)} fusion(f32[2,1024,160]{2,0,1:T(2,128)} %copy.26, s32[1024]{0:T(1024)S(1)} %fusion.6), kind=kCustom, calls=%fused_computation.2 | custom fusion | bytes 2625536 | tf_op jit(solution)/shard_map/jit(_take)/gather | solution.py:53
  115.9 4.5 %select_bitcast_fusion = f32[2,160,1024]{1,0,2:T(2,128)} fusion(f32[1024,2,160]{2,1,0:T(2,128)S(1)} %gather_fusion.2, pred[1024]{0:T(1024)(128)(4,1)S(1)} %compare_and_fusion.1), kind=kLoop, calls=%fused_computation.6 | loop fusion | flops 327680 | bytes 2622464 | tf_op jit(solution)/shard_map/jit(_take)/select_n | solution.py:53
  120.4 49.8 %all-gather.4.cloned.1.call-done = f32[2560,1024]{1,0:T(8,128)} async-done(((f32[320,1024]{1,0:T(8,128)}), f32[2560,1024]{1,0:T(8,128)}) %all-gather.4.cloned.1.call-update) | async-done | bytes 10485776 | tf_op jit(solution)/shard_map/all_gather | solution.py:127
  170.2 1.9 slice_bitcast_fusion
  172.1 1.8 copy.28
  175.1 1.2 slice_bitcast_fusion.1
  177.6 82.2 %all-gather.6.cloned.1.call-done = f32[2560,1536]{1,0:T(8,128)} async-done(((f32[160,1536]{1,0:T(8,128)}), f32[2560,1536]{1,0:T(8,128)}) %all-gather.6.cloned.1.call-update) | async-done | bytes 15728656 | tf_op jit(solution)/shard_map/all_gather | solution.py:144
  259.7 31.6 %fusion.11 = f32[1536,1024]{1,0:T(8,128)S(1)} fusion(f32[2560,1536]{1,0:T(8,128)} %all-gather.6.cloned.1.call-done, f32[2560,1024]{1,0:T(8,128)} %all-gather.4.cloned.1.call-done), kind=kOutput, calls=%fused_computation.55 | convolution fusion | flops 24159191040 | bytes 32505856 | tf_op jit(solution)/shard_map/dot_general | solution.py:133
  292.1 2.2 pad_maximum_fusion.tile_ref
  294.3 48.5 %shard_map.55 = f32[2,48,8192]{2,1,0:T(8,128)} custom-call(f32[16,2,48,512]{3,2,1,0:T(8,128)} %pad_maximum_fusion.tile_ref), custom_call_target="tpu_custom_call" | custom-call | tf_op jit(solution)/shard_map/pallas_call | solution.py:107
  342.8 12.1 %fusion.12 = f32[512,1024]{1,0:T(8,128)S(1)} fusion(f32[2560,512]{1,0:T(8,128)} %all-gather.8.cloned.1.call-done, f32[2560,1024]{1,0:T(8,128)} %all-gather.4.cloned.1.call-done), kind=kOutput, calls=%fused_computation.56 | convolution fusion | flops 8053063680 | bytes 17825792 | tf_op jit(solution)/shard_map/dot_general | solution.py:133
  356.2 21.0 %shard_map.56 = f32[2,16,8192]{2,1,0:T(8,128)} custom-call(f32[16,2,16,512]{3,2,1,0:T(8,128)} %pad_maximum_fusion.1.tile_ref), custom_call_target="tpu_custom_call" | custom-call | tf_op jit(solution)/shard_map/pallas_call | solution.py:107
  377.2 3.5 maximum_bitcast_fusion
  (38 shorter events, 6.0 us)
Async XLA Ops:
  6.5 2.7 copy-start.1
  6.5 163.6 %all-gather.4.cloned.1.call-start = ((), (), s32[]{:S(2)}) async-start(), calls=%async_computation.2 | async-start | bytes 11796480 | tf_op jit(solution)/shard_map/all_gather | solution.py:127
  11.6 8.5 %copy-start.3 = (s32[64]{0:T(128)S(1)}, s32[64]{0:T(128)}, u32[]{:S(2)}) copy-start(s32[64]{0:T(128)} %param.7) | copy-start | bytes 772
  11.6 8.7 %copy-start.4 = (s32[7]{0:T(128)S(1)}, s32[7]{0:T(128)}, u32[]{:S(2)}) copy-start(s32[7]{0:T(128)} %param.8) | copy-start | bytes 88
  11.6 47.9 %all-to-all-start = ((f32[2,8,8,16,160]{4,3,1,0,2:T(8,128)}), f32[2,8,8,16,160]{4,3,1,0,2:T(8,128)S(1)}, u32[]{:S(2)}, u32[]{:S(2)}) async-start(f32[2,8,8,16,160]{4,3,1,0,2:T(8,128)} %copy.22), calls=%async_computation | async-start | bytes 4194304 | tf_op jit(solution)/shard_map/all_to_all | solution.py:41
  64.9 4.3 %copy-start.2 = (s32[1024]{0:T(1024)S(1)}, s32[1024]{0:T(1024)}, u32[]{:S(2)}) copy-start(s32[1024]{0:T(1024)} %constant.116) | copy-start | bytes 12292
  64.9 42.1 %all-to-all-start.1 = ((f32[2,8,8,16,160]{4,3,2,0,1:T(8,128)}), f32[2,8,8,16,160]{4,3,2,0,1:T(8,128)S(1)}, u32[]{:S(2)}, u32[]{:S(2)}) async-start(f32[2,8,8,16,160]{4,3,2,0,1:T(8,128)} %copy_select_fusion), calls=%async_computation.1 | async-start | bytes 4194304 | tf_op jit(solution)/shard_map/all_to_all | solution.py:47
  69.0 190.7 %all-gather.6.cloned.1.call-start = ((), (), s32[]{:S(2)}) async-start(), calls=%async_computation.3 | async-start | bytes 16711680 | tf_op jit(solution)/shard_map/all_gather | solution.py:144
  174.9 167.9 %all-gather.8.cloned.1.call-start = ((), (), s32[]{:S(2)}) async-start(), calls=%async_computation.4 | async-start | bytes 5570560 | tf_op jit(solution)/shard_map/all_gather | solution.py:144
  355.1 22.1 %copy-start = (f32[2,48,8192]{2,1,0:T(8,128)S(1)}, f32[2,48,8192]{2,1,0:T(8,128)}, u32[]{:S(2)}) copy-start(f32[2,48,8192]{2,1,0:T(8,128)} %shard_map.55) | copy-start | bytes 9437188
Sparse Core Ops, SparseCore 0:
  9.7 160.4 all-gather.3
  175.0 84.6 all-gather.5
  261.4 49.0 all-gather.7

commit v15 on v13

--- a/solution.py
+++ b/solution.py
@@ -54,7 +54,7 @@
 
 
 def part_sizes(q_total):
-    return [q_total * 3 // 4, q_total - q_total * 3 // 4]
+    return [q_total * 5 // 8, q_total - q_total * 5 // 8]
 
 
 def part_order(rows, col_count):

time: 377 us -> 383 us (1.016)
  waiting for transfers between devices: 204 us -> 191 us
  blocking collectives: 42.7 us -> 52.9 us
  Pallas kernels: 16.6 us -> 24.5 us
    all_gather x2, waiting for transfers between devices: 82.2 us -> 69.1 us  [body(): lall = lax.all_gather(piece, COL, axis=0, tiled=True)]
    all_to_all x1, blocking collectives: 42.7 us -> 52.9 us  [body(): lax.all_to_all(tile, COL, split_axis=1, concat_axis=3, tiled=True)]
    pallas_call x1, Pallas kernels: 16.6 us -> 24.5 us  [scatter_cols(): pl.pallas_call(functools.partial(scatter_kernel, ncol), out_shape=jax.Sha...]
  transfers between devices with their start and end apart: 5 -> 5, of which waited for: 4 -> 4; matrix products, arithmetic and copies ran while one was open for 16% -> 15% of each run, Pallas kernels for 0% -> 0%
where the time goes in v15:
time: 383 us; the launch traced here: 381 us
  waiting for transfers between devices  191 us (50%)
  blocking collectives  52.9 us (14%)
  matrix products  43.5 us (11%)
  local copies, waits for them, and re-layouts  30.3 us (8%)
  Pallas kernels  24.5 us (6%)
  between operations  13.3 us (3%)
  starting transfers between devices  12.8 us (3%)
  other arithmetic  12.7 us (3%)
    all_gather x2, waiting for transfers between devices, body(): lall = lax.all_gather(piece, COL, axis=0, tiled=True)  69.1 us
    all_to_all x1, blocking collectives, body(): lax.all_to_all(tile, COL, split_axis=1, concat_axis=3, tiled=True)  52.9 us
    all_gather x1, waiting for transfers between devices, body(): rall = lax.all_gather(rpiece, ROW, axis=0, tiled=True)  49.8 us
    dot_general x2, matrix products, body(): lax.dot_general(a, b, dims, preferred_element_type=jnp.float32, precision...  43.5 us
    all_to_all x1, waiting for transfers between devices, permute_left(): x = lax.all_to_all(x, ROW, split_axis=2, concat_axis=2, tiled=True)  39.1 us
    all_to_all x1, waiting for transfers between devices, permute_left(): y = lax.all_to_all(y, ROW, split_axis=1, concat_axis=1, tiled=True)  33.3 us
    pallas_call x1, Pallas kernels, scatter_cols(): pl.pallas_call(functools.partial(scatter_kernel, ncol), out_shape=jax.Sha...  24.5 us
    gather x2, local copies, waits for them, and re-layouts, permute_left(): return jnp.take(y, jnp.take(idx, part_order(rows, col_count)), axis=1)  10.3 us
  transfers between devices with their start and end apart: 5, of which 4 were waited for; matrix products, arithmetic and copies ran while one was open for 15% of the time, Pallas kernels for 0%

profile of v15, /device:TPU:1, one launch (start us, length us, event | category | flops | bytes accessed | tf_op | source)
XLA Modules:
  0.0 381.4 jit_solution(18307543682696922557)
XLA Ops:
  6.5 2.6 copy.49
  10.0 1.6 copy.38
  11.6 8.5 %all-to-all-start = ((f32[2,8,8,16,160]{4,3,1,0,2:T(8,128)}), f32[2,8,8,16,160]{4,3,1,0,2:T(8,128)S(1)}, u32[]{:S(2)}, u32[]{:S(2)}) async-start(f32[2,8,8,16,160]{4,3,1,0,2:T(8,128)} %copy.38), calls=%async_computation | async-start | bytes 4194304 | tf_op jit(solution)/shard_map/all_to_all | solution.py:41
  20.4 39.1 %all-to-all-done = f32[2,8,8,16,160]{4,3,1,0,2:T(8,128)S(1)} async-done(((f32[2,8,8,16,160]{4,3,1,0,2:T(8,128)}), f32[2,8,8,16,160]{4,3,1,0,2:T(8,128)S(1)}, u32[]{:S(2)}, u32[]{:S(2)}) %all-to-all-start) | async-done | bytes 1310752 | tf_op jit(solution)/shard_map/all_to_all | solution.py:41
  59.5 1.6 copy.39
  61.1 2.3 gather_fusion.1
  63.3 1.5 copy_select_fusion
  64.9 4.1 %all-to-all-start.1 = ((f32[2,8,8,16,160]{4,3,2,0,1:T(8,128)}), f32[2,8,8,16,160]{4,3,2,0,1:T(8,128)S(1)}, u32[]{:S(2)}, u32[]{:S(2)}) async-start(f32[2,8,8,16,160]{4,3,2,0,1:T(8,128)} %copy_select_fusion), calls=%async_computation.1 | async-start | bytes 4194304 | tf_op jit(solution)/shard_map/all_to_all | solution.py:47
  69.1 4.5 %gather_fusion = s32[1024]{0:T(1024)S(1)} fusion(s32[1024]{0:T(1024)S(1)} %add_bitcast_fusion, s32[1024]{0:T(1024)S(1)} %broadcast_clamp_fusion), kind=kCustom, calls=%fused_computation | custom fusion | bytes 12288 | tf_op jit(solution)/shard_map/jit(_take)/gather | solution.py:53
  73.7 33.3 %all-to-all-done.1 = f32[2,8,8,16,160]{4,3,2,0,1:T(8,128)S(1)} async-done(((f32[2,8,8,16,160]{4,3,2,0,1:T(8,128)}), f32[2,8,8,16,160]{4,3,2,0,1:T(8,128)S(1)}, u32[]{:S(2)}, u32[]{:S(2)}) %all-to-all-start.1) | async-done | bytes 1310752 | tf_op jit(solution)/shard_map/all_to_all | solution.py:47
  107.2 2.9 copy.42
  110.2 5.7 %gather_fusion.2 = f32[1024,2,160]{2,1,0:T(2,128)S(1)} fusion(f32[2,1024,160]{2,0,1:T(2,128)} %copy.42, s32[1024]{0:T(1024)S(1)} %fusion.6), kind=kCustom, calls=%fused_computation.2 | custom fusion | bytes 2625536 | tf_op jit(solution)/shard_map/jit(_take)/gather | solution.py:53
  115.9 4.5 %select_bitcast_fusion = f32[2,160,1024]{1,0,2:T(2,128)} fusion(f32[1024,2,160]{2,1,0:T(2,128)S(1)} %gather_fusion.2, pred[1024]{0:T(1024)(128)(4,1)S(1)} %compare_and_fusion.1), kind=kLoop, calls=%fused_computation.6 | loop fusion | flops 327680 | bytes 2622464 | tf_op jit(solution)/shard_map/jit(_take)/select_n | solution.py:53
  120.4 49.8 %all-gather.4.cloned.1.call-done = f32[2560,1024]{1,0:T(8,128)} async-done(((f32[320,1024]{1,0:T(8,128)}), f32[2560,1024]{1,0:T(8,128)}) %all-gather.4.cloned.1.call-update) | async-done | bytes 10485776 | tf_op jit(solution)/shard_map/all_gather | solution.py:127
  170.2 1.8 slice_bitcast_fusion
  171.9 1.9 copy.44
  175.0 1.4 slice_bitcast_fusion.1
  178.1 69.1 %all-gather.6.cloned.1.call-done = f32[2560,1280]{1,0:T(8,128)} async-done(((f32[160,1280]{1,0:T(8,128)}), f32[2560,1280]{1,0:T(8,128)}) %all-gather.6.cloned.1.call-update) | async-done | bytes 13107216 | tf_op jit(solution)/shard_map/all_gather | solution.py:144
  247.3 26.8 %fusion.11 = f32[1280,1024]{1,0:T(8,128)S(1)} fusion(f32[2560,1280]{1,0:T(8,128)} %all-gather.6.cloned.1.call-done, f32[2560,1024]{1,0:T(8,128)} %all-gather.4.cloned.1.call-done), kind=kOutput, calls=%fused_computation.55 | convolution fusion | flops 20132659200 | bytes 28835840 | tf_op jit(solution)/shard_map/dot_general | solution.py:133
  275.0 52.9 %all_to_all.28 = f32[2,16,40,512]{3,2,0,1:T(8,128)S(1)} all-to-all(f32[2,16,40,512]{3,2,0,1:T(8,128)S(1)} %pad_maximum_fusion), channel_id=1, replica_groups=mesh['xh'=2,'z'=4,'xl'=2,'y'=4,'core'=2] {'xl','y','core'}, dimensions={1} | all-to-all | bytes 5242880 | tf_op jit(solution)/shard_map/all_to_all | solution.py:155
  328.1 16.7 %fusion.12 = f32[768,1024]{1,0:T(8,128)S(1)} fusion(f32[2560,768]{1,0:T(8,128)} %all-gather.8.cloned.1.call-done, f32[2560,1024]{1,0:T(8,128)} %all-gather.4.cloned.1.call-done), kind=kOutput, calls=%fused_computation.56 | convolution fusion | flops 12079595520 | bytes 21495808 | tf_op jit(solution)/shard_map/dot_general | solution.py:133
  345.2 1.3 pad_maximum_fusion.1.tile_ref
  346.5 24.5 %shard_map.55 = f32[2,24,8192]{2,1,0:T(8,128)} custom-call(f32[16,2,24,512]{3,2,1,0:T(8,128)} %pad_maximum_fusion.1.tile_ref), custom_call_target="tpu_custom_call" | custom-call | tf_op jit(solution)/shard_map/pallas_call | solution.py:107
  371.1 3.8 %maximum_bitcast_fusion = f32[2,64,8192]{2,1,0:T(8,128)} fusion(f32[2,1,24,8192]{3,2,0,1:T(8,128)} %bitcast.64, f32[2,1,40,8192]{3,2,0,1:T(8,128)S(1)} %bitcast.58), kind=kLoop, calls=%fused_computation.3 | loop fusion | flops 1048576 | bytes 8388608 | tf_op jit(solution)/shard_map/reshape | solution.py:157
  (37 shorter events, 6.0 us)
Async XLA Ops:
  6.5 2.7 copy-start
  6.5 163.6 %all-gather.4.cloned.1.call-start = ((), (), s32[]{:S(2)}) async-start(), calls=%async_computation.3 | async-start | bytes 11796480 | tf_op jit(solution)/shard_map/all_gather | solution.py:127
  11.6 8.5 %copy-start.2 = (s32[64]{0:T(128)S(1)}, s32[64]{0:T(128)}, u32[]{:S(2)}) copy-start(s32[64]{0:T(128)} %param.7) | copy-start | bytes 772
  11.6 8.7 %copy-start.3 = (s32[7]{0:T(128)S(1)}, s32[7]{0:T(128)}, u32[]{:S(2)}) copy-start(s32[7]{0:T(128)} %param.8) | copy-start | bytes 88
  11.6 47.9 %all-to-all-start = ((f32[2,8,8,16,160]{4,3,1,0,2:T(8,128)}), f32[2,8,8,16,160]{4,3,1,0,2:T(8,128)S(1)}, u32[]{:S(2)}, u32[]{:S(2)}) async-start(f32[2,8,8,16,160]{4,3,1,0,2:T(8,128)} %copy.38), calls=%async_computation | async-start | bytes 4194304 | tf_op jit(solution)/shard_map/all_to_all | solution.py:41
  64.9 4.3 %copy-start.1 = (s32[1024]{0:T(1024)S(1)}, s32[1024]{0:T(1024)}, u32[]{:S(2)}) copy-start(s32[1024]{0:T(1024)} %constant.116) | copy-start | bytes 12292
  64.9 42.1 %all-to-all-start.1 = ((f32[2,8,8,16,160]{4,3,2,0,1:T(8,128)}), f32[2,8,8,16,160]{4,3,2,0,1:T(8,128)S(1)}, u32[]{:S(2)}, u32[]{:S(2)}) async-start(f32[2,8,8,16,160]{4,3,2,0,1:T(8,128)} %copy_select_fusion), calls=%async_computation.1 | async-start | bytes 4194304 | tf_op jit(solution)/shard_map/all_to_all | solution.py:47
  69.0 178.3 %all-gather.6.cloned.1.call-start = ((), (), s32[]{:S(2)}) async-start(), calls=%async_computation.4 | async-start | bytes 13926400 | tf_op jit(solution)/shard_map/all_gather | solution.py:144
  174.8 153.3 %all-gather.8.cloned.1.call-start = ((), (), s32[]{:S(2)}) async-start(), calls=%async_computation.5 | async-start | bytes 8355840 | tf_op jit(solution)/shard_map/all_gather | solution.py:144
Sparse Core Ops, SparseCore 0:
  9.7 160.4 all-gather.3
  174.9 72.3 all-gather.5
  249.0 78.6 all-gather.7

commit v16 on v14

--- a/solution.py
+++ b/solution.py
@@ -102,7 +102,7 @@
         c.wait()
 
 
-def scatter_cols(tile, ncol, cid):
+def scatter_cols(tile, ncol):
     _, b, q, w = tile.shape
     return pl.pallas_call(
         functools.partial(scatter_kernel, ncol),
@@ -114,7 +114,7 @@
             pltpu.SemaphoreType.DMA((ncol,)),
             pltpu.SemaphoreType.DMA((1,)),
         ],
-        compiler_params=pltpu.CompilerParams(collective_id=cid, has_side_effects=True),
+        compiler_params=pltpu.CompilerParams(collective_id=0, has_side_effects=True),
     )(tile)
 
 
@@ -146,10 +146,9 @@
         q = dot(lall, rall)
         re = q[:part, :cols] - q[part:, cols:]
         im = q[:part, cols:] + q[part:, :cols]
-        tile = jnp.stack([re.reshape(col_count, qp, cols), im.reshape(col_count, qp, cols)], axis=1)
-        outs.append(scatter_cols(tile, col_count, len(outs)).reshape(2, 1, qp, col_count * cols))
-    out = jnp.concatenate(outs, axis=2)
-    return out.reshape(2, rows // col_count, col_count * cols)
+        outs.append(jnp.stack([re.reshape(col_count, qp, cols), im.reshape(col_count, qp, cols)], axis=1))
+    tile = jnp.concatenate(outs, axis=2)
+    return scatter_cols(tile, col_count)
 
 
 def solution(mesh):

time: 390 us -> 395 us (1.013)
  waiting for transfers between devices: 204 us -> 214 us
  Pallas kernels: 69.5 us -> 62.9 us
  local copies, waits for them, and re-layouts: 29.5 us -> 34.1 us
  other arithmetic: 14 us -> 9.85 us
    all_gather x2, waiting for transfers between devices: 82.2 us -> 91.9 us  [body(): lall = lax.all_gather(piece, COL, axis=0, tiled=True)]
    pallas_call x2 -> x1, Pallas kernels: 69.5 us -> 62.9 us  [scatter_cols(): pl.pallas_call(functools.partial(scatter_kernel, ncol), out_shape=jax.Sha...]
    unnamed x13 -> x12, local copies, waits for them, and re-layouts: 2.58 us -> 7.18 us
  transfers between devices with their start and end apart: 5 -> 5, of which waited for: 4 -> 5; matrix products, arithmetic and copies ran while one was open for 16% -> 16% of each run, Pallas kernels for 13% -> 0%
where the time goes in v16:
time: 395 us; the launch traced here: 391 us
  waiting for transfers between devices  214 us (54%)
  Pallas kernels  62.9 us (16%)
  matrix products  43.7 us (11%)
  local copies, waits for them, and re-layouts  34.1 us (9%)
  between operations  13.3 us (3%)
  starting transfers between devices  12.8 us (3%)
  other arithmetic  9.85 us (2%)
    all_gather x2, waiting for transfers between devices, body(): lall = lax.all_gather(piece, COL, axis=0, tiled=True)  91.9 us
    pallas_call x1, Pallas kernels, scatter_cols(): pl.pallas_call(functools.partial(scatter_kernel, ncol), out_shape=jax.Sha...  62.9 us
    all_gather x1, waiting for transfers between devices, body(): rall = lax.all_gather(rpiece, ROW, axis=0, tiled=True)  49.8 us
    dot_general x2, matrix products, body(): lax.dot_general(a, b, dims, preferred_element_type=jnp.float32, precision...  43.7 us
    all_to_all x1, waiting for transfers between devices, permute_left(): x = lax.all_to_all(x, ROW, split_axis=2, concat_axis=2, tiled=True)  39.1 us
    all_to_all x1, waiting for transfers between devices, permute_left(): y = lax.all_to_all(y, ROW, split_axis=1, concat_axis=1, tiled=True)  33.3 us
    gather x2, local copies, waits for them, and re-layouts, permute_left(): return jnp.take(y, jnp.take(idx, part_order(rows, col_count)), axis=1)  10.3 us
    all_to_all x1, starting transfers between devices, permute_left(): x = lax.all_to_all(x, ROW, split_axis=2, concat_axis=2, tiled=True)  8.45 us
  transfers between devices with their start and end apart: 5, of which 5 were waited for; matrix products, arithmetic and copies ran while one was open for 16% of the time, Pallas kernels for 0%

profile of v16, /device:TPU:1, one launch (start us, length us, event | category | flops | bytes accessed | tf_op | source)
XLA Modules:
  0.0 390.7 jit_solution(17936378710999088290)
XLA Ops:
  6.5 2.6 copy.30
  10.0 1.6 copy.22
  11.6 8.5 %all-to-all-start = ((f32[2,8,8,16,160]{4,3,1,0,2:T(8,128)}), f32[2,8,8,16,160]{4,3,1,0,2:T(8,128)S(1)}, u32[]{:S(2)}, u32[]{:S(2)}) async-start(f32[2,8,8,16,160]{4,3,1,0,2:T(8,128)} %copy.22), calls=%async_computation | async-start | bytes 4194304 | tf_op jit(solution)/shard_map/all_to_all | solution.py:41
  20.4 39.1 %all-to-all-done = f32[2,8,8,16,160]{4,3,1,0,2:T(8,128)S(1)} async-done(((f32[2,8,8,16,160]{4,3,1,0,2:T(8,128)}), f32[2,8,8,16,160]{4,3,1,0,2:T(8,128)S(1)}, u32[]{:S(2)}, u32[]{:S(2)}) %all-to-all-start) | async-done | bytes 1310752 | tf_op jit(solution)/shard_map/all_to_all | solution.py:41
  59.5 1.6 copy.23
  61.1 2.3 gather_fusion.1
  63.3 1.5 copy_select_fusion
  64.9 4.1 %all-to-all-start.1 = ((f32[2,8,8,16,160]{4,3,2,0,1:T(8,128)}), f32[2,8,8,16,160]{4,3,2,0,1:T(8,128)S(1)}, u32[]{:S(2)}, u32[]{:S(2)}) async-start(f32[2,8,8,16,160]{4,3,2,0,1:T(8,128)} %copy_select_fusion), calls=%async_computation.1 | async-start | bytes 4194304 | tf_op jit(solution)/shard_map/all_to_all | solution.py:47
  69.1 4.5 %gather_fusion = s32[1024]{0:T(1024)S(1)} fusion(s32[1024]{0:T(1024)S(1)} %add_bitcast_fusion, s32[1024]{0:T(1024)S(1)} %broadcast_clamp_fusion), kind=kCustom, calls=%fused_computation | custom fusion | bytes 12288 | tf_op jit(solution)/shard_map/jit(_take)/gather | solution.py:53
  73.7 33.3 %all-to-all-done.1 = f32[2,8,8,16,160]{4,3,2,0,1:T(8,128)S(1)} async-done(((f32[2,8,8,16,160]{4,3,2,0,1:T(8,128)}), f32[2,8,8,16,160]{4,3,2,0,1:T(8,128)S(1)}, u32[]{:S(2)}, u32[]{:S(2)}) %all-to-all-start.1) | async-done | bytes 1310752 | tf_op jit(solution)/shard_map/all_to_all | solution.py:47
  107.2 2.9 copy.26
  110.2 5.8 %gather_fusion.2 = f32[1024,2,160]{2,1,0:T(2,128)S(1)} fusion(f32[2,1024,160]{2,0,1:T(2,128)} %copy.26, s32[1024]{0:T(1024)S(1)} %fusion.6), kind=kCustom, calls=%fused_computation.2 | custom fusion | bytes 2625536 | tf_op jit(solution)/shard_map/jit(_take)/gather | solution.py:53
  115.9 4.5 %select_bitcast_fusion = f32[2,160,1024]{1,0,2:T(2,128)} fusion(f32[1024,2,160]{2,1,0:T(2,128)S(1)} %gather_fusion.2, pred[1024]{0:T(1024)(128)(4,1)S(1)} %compare_and_fusion.1), kind=kLoop, calls=%fused_computation.5 | loop fusion | flops 327680 | bytes 2622464 | tf_op jit(solution)/shard_map/jit(_take)/select_n | solution.py:53
  120.4 49.8 %all-gather.4.cloned.1.call-done = f32[2560,1024]{1,0:T(8,128)} async-done(((f32[320,1024]{1,0:T(8,128)}), f32[2560,1024]{1,0:T(8,128)}) %all-gather.4.cloned.1.call-update) | async-done | bytes 10485776 | tf_op jit(solution)/shard_map/all_gather | solution.py:127
  170.2 1.9 slice_bitcast_fusion
  172.1 1.8 copy.28
  175.1 1.2 slice_bitcast_fusion.1
  177.6 82.2 %all-gather.6.cloned.1.call-done = f32[2560,1536]{1,0:T(8,128)} async-done(((f32[160,1536]{1,0:T(8,128)}), f32[2560,1536]{1,0:T(8,128)}) %all-gather.6.cloned.1.call-update) | async-done | bytes 15728656 | tf_op jit(solution)/shard_map/all_gather | solution.py:144
  259.8 31.6 %fusion.11 = f32[1536,1024]{1,0:T(8,128)S(1)} fusion(f32[2560,1536]{1,0:T(8,128)} %all-gather.6.cloned.1.call-done, f32[2560,1024]{1,0:T(8,128)} %all-gather.4.cloned.1.call-done), kind=kOutput, calls=%fused_computation.53 | convolution fusion | flops 24159191040 | bytes 32505856 | tf_op jit(solution)/shard_map/dot_general | solution.py:133
  292.1 9.7 %all-gather.8.cloned.1.call-done = f32[2560,512]{1,0:T(8,128)} async-done(((f32[160,512]{1,0:T(8,128)}), f32[2560,512]{1,0:T(8,128)}) %all-gather.8.cloned.1.call-update) | async-done | bytes 5242896 | tf_op jit(solution)/shard_map/all_gather | solution.py:144
  301.8 12.1 %fusion.12 = f32[512,1024]{1,0:T(8,128)S(1)} fusion(f32[2560,512]{1,0:T(8,128)} %all-gather.8.cloned.1.call-done, f32[2560,1024]{1,0:T(8,128)} %all-gather.4.cloned.1.call-done), kind=kOutput, calls=%fused_computation.54 | convolution fusion | flops 8053063680 | bytes 17825792 | tf_op jit(solution)/shard_map/dot_general | solution.py:133
  314.2 2.6 maximum_maximum_fusion.tile_ref
  316.7 62.9 %shard_map.55 = f32[2,64,8192]{2,1,0:T(8,128)} custom-call(f32[16,2,64,512]{3,2,1,0:T(8,128)} %maximum_maximum_fusion.tile_ref), custom_call_target="tpu_custom_call" | custom-call | tf_op jit(solution)/shard_map/pallas_call | solution.py:107
  379.6 4.6 %copy.35 = f32[2,64,8192]{2,1,0:T(8,128)} copy(f32[2,64,8192]{2,1,0:T(8,128)} %shard_map.55) | data formatting | bytes 8388608
  (34 shorter events, 4.9 us)
Async XLA Ops:
  6.5 2.7 copy-start
  6.5 163.6 %all-gather.4.cloned.1.call-start = ((), (), s32[]{:S(2)}) async-start(), calls=%async_computation.2 | async-start | bytes 11796480 | tf_op jit(solution)/shard_map/all_gather | solution.py:127
  11.6 8.5 %copy-start.2 = (s32[64]{0:T(128)S(1)}, s32[64]{0:T(128)}, u32[]{:S(2)}) copy-start(s32[64]{0:T(128)} %param.7) | copy-start | bytes 772
  11.6 8.7 %copy-start.3 = (s32[7]{0:T(128)S(1)}, s32[7]{0:T(128)}, u32[]{:S(2)}) copy-start(s32[7]{0:T(128)} %param.8) | copy-start | bytes 88
  11.6 47.9 %all-to-all-start = ((f32[2,8,8,16,160]{4,3,1,0,2:T(8,128)}), f32[2,8,8,16,160]{4,3,1,0,2:T(8,128)S(1)}, u32[]{:S(2)}, u32[]{:S(2)}) async-start(f32[2,8,8,16,160]{4,3,1,0,2:T(8,128)} %copy.22), calls=%async_computation | async-start | bytes 4194304 | tf_op jit(solution)/shard_map/all_to_all | solution.py:41
  64.9 4.3 %copy-start.1 = (s32[1024]{0:T(1024)S(1)}, s32[1024]{0:T(1024)}, u32[]{:S(2)}) copy-start(s32[1024]{0:T(1024)} %constant.116) | copy-start | bytes 12292
  64.9 42.1 %all-to-all-start.1 = ((f32[2,8,8,16,160]{4,3,2,0,1:T(8,128)}), f32[2,8,8,16,160]{4,3,2,0,1:T(8,128)S(1)}, u32[]{:S(2)}, u32[]{:S(2)}) async-start(f32[2,8,8,16,160]{4,3,2,0,1:T(8,128)} %copy_select_fusion), calls=%async_computation.1 | async-start | bytes 4194304 | tf_op jit(solution)/shard_map/all_to_all | solution.py:47
  69.0 190.8 %all-gather.6.cloned.1.call-start = ((), (), s32[]{:S(2)}) async-start(), calls=%async_computation.3 | async-start | bytes 16711680 | tf_op jit(solution)/shard_map/all_gather | solution.py:144
  174.9 126.9 %all-gather.8.cloned.1.call-start = ((), (), s32[]{:S(2)}) async-start(), calls=%async_computation.4 | async-start | bytes 5570560 | tf_op jit(solution)/shard_map/all_gather | solution.py:144
Sparse Core Ops, SparseCore 0:
  9.7 160.4 all-gather.3
  175.0 84.6 all-gather.5
  261.4 40.3 all-gather.7

commit v17 on v13

--- a/solution.py
+++ b/solution.py
@@ -152,7 +152,8 @@
         else:
             tile = jnp.stack([re, im], axis=0)
             tile = tile.reshape(2, col_count, qp, cols)
-            outs.append(lax.all_to_all(tile, COL, split_axis=1, concat_axis=3, tiled=True))
+            got = lax.all_to_all(tile, COL, split_axis=1, concat_axis=1, tiled=True)
+            outs.append(jnp.swapaxes(got, 1, 2).reshape(2, 1, qp, col_count * cols))
     out = jnp.concatenate(outs, axis=2)
     return out.reshape(2, rows // col_count, col_count * cols)
 

time: 377 us -> 381 us (1.011)
  transfers between devices with their start and end apart: 5 -> 5, of which waited for: 4 -> 4; matrix products, arithmetic and copies ran while one was open for 16% -> 17% of each run, Pallas kernels for 0% -> 0%
where the time goes in v17:
time: 381 us; the launch traced here: 379 us
  waiting for transfers between devices  204 us (54%)
  matrix products  43.7 us (11%)
  blocking collectives  42.7 us (11%)
  local copies, waits for them, and re-layouts  33.6 us (9%)
  Pallas kernels  16.6 us (4%)
  between operations  13.3 us (3%)
  starting transfers between devices  12.8 us (3%)
  other arithmetic  12.2 us (3%)
    all_gather x2, waiting for transfers between devices, body(): lall = lax.all_gather(piece, COL, axis=0, tiled=True)  82.2 us
    all_gather x1, waiting for transfers between devices, body(): rall = lax.all_gather(rpiece, ROW, axis=0, tiled=True)  49.8 us
    dot_general x2, matrix products, body(): lax.dot_general(a, b, dims, preferred_element_type=jnp.float32, precision...  43.7 us
    all_to_all x1, blocking collectives, body(): got = lax.all_to_all(tile, COL, split_axis=1, concat_axis=1, tiled=True)  42.7 us
    all_to_all x1, waiting for transfers between devices, permute_left(): x = lax.all_to_all(x, ROW, split_axis=2, concat_axis=2, tiled=True)  39.1 us
    all_to_all x1, waiting for transfers between devices, permute_left(): y = lax.all_to_all(y, ROW, split_axis=1, concat_axis=1, tiled=True)  33.3 us
    pallas_call x1, Pallas kernels, scatter_cols(): pl.pallas_call(functools.partial(scatter_kernel, ncol), out_shape=jax.Sha...  16.6 us
    gather x2, local copies, waits for them, and re-layouts, permute_left(): return jnp.take(y, jnp.take(idx, part_order(rows, col_count)), axis=1)  10.3 us
  transfers between devices with their start and end apart: 5, of which 4 were waited for; matrix products, arithmetic and copies ran while one was open for 17% of the time, Pallas kernels for 0%

profile of v17, /device:TPU:1, one launch (start us, length us, event | category | flops | bytes accessed | tf_op | source)
XLA Modules:
  0.0 379.4 jit_solution(9698104804243809642)
XLA Ops:
  6.5 2.6 copy.49
  10.0 1.6 copy.38
  11.6 8.5 %all-to-all-start = ((f32[2,8,8,16,160]{4,3,1,0,2:T(8,128)}), f32[2,8,8,16,160]{4,3,1,0,2:T(8,128)S(1)}, u32[]{:S(2)}, u32[]{:S(2)}) async-start(f32[2,8,8,16,160]{4,3,1,0,2:T(8,128)} %copy.38), calls=%async_computation | async-start | bytes 4194304 | tf_op jit(solution)/shard_map/all_to_all | solution.py:41
  20.4 39.1 %all-to-all-done = f32[2,8,8,16,160]{4,3,1,0,2:T(8,128)S(1)} async-done(((f32[2,8,8,16,160]{4,3,1,0,2:T(8,128)}), f32[2,8,8,16,160]{4,3,1,0,2:T(8,128)S(1)}, u32[]{:S(2)}, u32[]{:S(2)}) %all-to-all-start) | async-done | bytes 1310752 | tf_op jit(solution)/shard_map/all_to_all | solution.py:41
  59.5 1.6 copy.39
  61.1 2.3 gather_fusion.1
  63.3 1.5 copy_select_fusion
  64.9 4.1 %all-to-all-start.1 = ((f32[2,8,8,16,160]{4,3,2,0,1:T(8,128)}), f32[2,8,8,16,160]{4,3,2,0,1:T(8,128)S(1)}, u32[]{:S(2)}, u32[]{:S(2)}) async-start(f32[2,8,8,16,160]{4,3,2,0,1:T(8,128)} %copy_select_fusion), calls=%async_computation.1 | async-start | bytes 4194304 | tf_op jit(solution)/shard_map/all_to_all | solution.py:47
  69.1 4.5 %gather_fusion = s32[1024]{0:T(1024)S(1)} fusion(s32[1024]{0:T(1024)S(1)} %add_bitcast_fusion, s32[1024]{0:T(1024)S(1)} %broadcast_clamp_fusion), kind=kCustom, calls=%fused_computation | custom fusion | bytes 12288 | tf_op jit(solution)/shard_map/jit(_take)/gather | solution.py:53
  73.7 33.3 %all-to-all-done.1 = f32[2,8,8,16,160]{4,3,2,0,1:T(8,128)S(1)} async-done(((f32[2,8,8,16,160]{4,3,2,0,1:T(8,128)}), f32[2,8,8,16,160]{4,3,2,0,1:T(8,128)S(1)}, u32[]{:S(2)}, u32[]{:S(2)}) %all-to-all-start.1) | async-done | bytes 1310752 | tf_op jit(solution)/shard_map/all_to_all | solution.py:47
  107.2 2.9 copy.42
  110.2 5.7 %gather_fusion.2 = f32[1024,2,160]{2,1,0:T(2,128)S(1)} fusion(f32[2,1024,160]{2,0,1:T(2,128)} %copy.42, s32[1024]{0:T(1024)S(1)} %fusion.6), kind=kCustom, calls=%fused_computation.2 | custom fusion | bytes 2625536 | tf_op jit(solution)/shard_map/jit(_take)/gather | solution.py:53
  115.9 4.5 %select_bitcast_fusion = f32[2,160,1024]{1,0,2:T(2,128)} fusion(f32[1024,2,160]{2,1,0:T(2,128)S(1)} %gather_fusion.2, pred[1024]{0:T(1024)(128)(4,1)S(1)} %compare_and_fusion.1), kind=kLoop, calls=%fused_computation.6 | loop fusion | flops 327680 | bytes 2622464 | tf_op jit(solution)/shard_map/jit(_take)/select_n | solution.py:53
  120.4 49.8 %all-gather.4.cloned.1.call-done = f32[2560,1024]{1,0:T(8,128)} async-done(((f32[320,1024]{1,0:T(8,128)}), f32[2560,1024]{1,0:T(8,128)}) %all-gather.4.cloned.1.call-update) | async-done | bytes 10485776 | tf_op jit(solution)/shard_map/all_gather | solution.py:127
  170.2 1.9 slice_bitcast_fusion
  172.1 1.8 copy.44
  177.6 82.2 %all-gather.6.cloned.1.call-done = f32[2560,1536]{1,0:T(8,128)} async-done(((f32[160,1536]{1,0:T(8,128)}), f32[2560,1536]{1,0:T(8,128)}) %all-gather.6.cloned.1.call-update) | async-done | bytes 15728656 | tf_op jit(solution)/shard_map/all_gather | solution.py:144
  259.7 31.6 %fusion.11 = f32[1536,1024]{1,0:T(8,128)S(1)} fusion(f32[2560,1536]{1,0:T(8,128)} %all-gather.6.cloned.1.call-done, f32[2560,1024]{1,0:T(8,128)} %all-gather.4.cloned.1.call-done), kind=kOutput, calls=%fused_computation.55 | convolution fusion | flops 24159191040 | bytes 32505856 | tf_op jit(solution)/shard_map/dot_general | solution.py:133
  292.4 42.7 %all_to_all.15 = f32[2,16,48,512]{3,2,0,1:T(8,128)S(1)} all-to-all(f32[2,16,48,512]{3,2,0,1:T(8,128)S(1)} %pad_maximum_fusion), channel_id=1, replica_groups=mesh['xh'=2,'z'=4,'xl'=2,'y'=4,'core'=2] {'xl','y','core'}, dimensions={1} | all-to-all | bytes 6291456 | tf_op jit(solution)/shard_map/all_to_all | solution.py:155
  335.1 1.8 copy.47
  336.9 2.3 reshape.216
  339.3 12.1 %fusion.12 = f32[512,1024]{1,0:T(8,128)S(1)} fusion(f32[2560,512]{1,0:T(8,128)} %all-gather.8.cloned.1.call-done, f32[2560,1024]{1,0:T(8,128)} %all-gather.4.cloned.1.call-done), kind=kOutput, calls=%fused_computation.56 | convolution fusion | flops 8053063680 | bytes 17825792 | tf_op jit(solution)/shard_map/dot_general | solution.py:133
  352.7 16.6 %shard_map.55 = f32[2,16,8192]{2,1,0:T(8,128)} custom-call(f32[16,2,16,512]{3,2,1,0:T(8,128)} %pad_maximum_fusion.1.tile_ref), custom_call_target="tpu_custom_call" | custom-call | tf_op jit(solution)/shard_map/pallas_call | solution.py:107
  369.3 3.5 maximum_bitcast_fusion
  (40 shorter events, 7.5 us)
Async XLA Ops:
  6.5 2.7 copy-start.1
  6.5 163.6 %all-gather.4.cloned.1.call-start = ((), (), s32[]{:S(2)}) async-start(), calls=%async_computation.3 | async-start | bytes 11796480 | tf_op jit(solution)/shard_map/all_gather | solution.py:127
  11.6 8.5 %copy-start.3 = (s32[64]{0:T(128)S(1)}, s32[64]{0:T(128)}, u32[]{:S(2)}) copy-start(s32[64]{0:T(128)} %param.7) | copy-start | bytes 772
  11.6 8.7 %copy-start.4 = (s32[7]{0:T(128)S(1)}, s32[7]{0:T(128)}, u32[]{:S(2)}) copy-start(s32[7]{0:T(128)} %param.8) | copy-start | bytes 88
  11.6 47.9 %all-to-all-start = ((f32[2,8,8,16,160]{4,3,1,0,2:T(8,128)}), f32[2,8,8,16,160]{4,3,1,0,2:T(8,128)S(1)}, u32[]{:S(2)}, u32[]{:S(2)}) async-start(f32[2,8,8,16,160]{4,3,1,0,2:T(8,128)} %copy.38), calls=%async_computation | async-start | bytes 4194304 | tf_op jit(solution)/shard_map/all_to_all | solution.py:41
  64.9 4.3 %copy-start.2 = (s32[1024]{0:T(1024)S(1)}, s32[1024]{0:T(1024)}, u32[]{:S(2)}) copy-start(s32[1024]{0:T(1024)} %constant.116) | copy-start | bytes 12292
  64.9 42.1 %all-to-all-start.1 = ((f32[2,8,8,16,160]{4,3,2,0,1:T(8,128)}), f32[2,8,8,16,160]{4,3,2,0,1:T(8,128)S(1)}, u32[]{:S(2)}, u32[]{:S(2)}) async-start(f32[2,8,8,16,160]{4,3,2,0,1:T(8,128)} %copy_select_fusion), calls=%async_computation.1 | async-start | bytes 4194304 | tf_op jit(solution)/shard_map/all_to_all | solution.py:47
  69.0 190.7 %all-gather.6.cloned.1.call-start = ((), (), s32[]{:S(2)}) async-start(), calls=%async_computation.4 | async-start | bytes 16711680 | tf_op jit(solution)/shard_map/all_gather | solution.py:144
  174.9 164.4 %all-gather.8.cloned.1.call-start = ((), (), s32[]{:S(2)}) async-start(), calls=%async_computation.5 | async-start | bytes 5570560 | tf_op jit(solution)/shard_map/all_gather | solution.py:144
  351.6 17.7 %copy-start = (f32[2,1,48,8192]{3,2,0,1:T(8,128)S(1)}, f32[2,1,48,8192]{3,2,0,1:T(8,128)}, u32[]{:S(2)}) copy-start(f32[2,1,48,8192]{3,2,0,1:T(8,128)} %reshape.216) | copy-start | bytes 9437188
Sparse Core Ops, SparseCore 0:
  9.7 160.4 all-gather.3
  175.0 84.6 all-gather.5
  261.4 40.5 all-gather.7

commit v18 on v15

--- a/solution.py
+++ b/solution.py
@@ -54,7 +54,7 @@
 
 
 def part_sizes(q_total):
-    return [q_total * 5 // 8, q_total - q_total * 5 // 8]
+    return [q_total * 13 // 16, q_total - q_total * 13 // 16]
 
 
 def part_order(rows, col_count):

time: 383 us -> 409 us (1.068)
  waiting for transfers between devices: 191 us -> 211 us
  local copies, waits for them, and re-layouts: 30.3 us -> 48.6 us
  Pallas kernels: 24.5 us -> 16.5 us
  blocking collectives: 52.9 us -> 45.7 us
    all_gather x2, waiting for transfers between devices: 69.1 us -> 88.5 us  [body(): lall = lax.all_gather(piece, COL, axis=0, tiled=True)]
    another operation x0 -> x5, local copies, waits for them, and re-layouts: none -> 9.18 us  [the longest x3 5.51 us: body(): tile = jnp.stack([re, im], axis=0)]
    reshape x0 -> x4, local copies, waits for them, and re-layouts: none -> 9.03 us  [the longest x1 4.44 us: body(): return out.reshape(2, rows // col_count, col_count * cols)]
    pallas_call x1, Pallas kernels: 24.5 us -> 16.5 us  [scatter_cols(): pl.pallas_call(functools.partial(scatter_kernel, ncol), out_shape=jax.Sha...]
    all_to_all x1, blocking collectives: 52.9 us -> 45.7 us  [body(): lax.all_to_all(tile, COL, split_axis=1, concat_axis=3, tiled=True)]
  transfers between devices with their start and end apart: 5 -> 5, of which waited for: 4 -> 4; matrix products, arithmetic and copies ran while one was open for 15% -> 18% of each run, Pallas kernels for 0% -> 0%
where the time goes in v18:
time: 409 us; the launch traced here: 408 us
  waiting for transfers between devices  211 us (52%)
  local copies, waits for them, and re-layouts  48.6 us (12%)
  blocking collectives  45.7 us (11%)
  matrix products  44.2 us (11%)
  Pallas kernels  16.5 us (4%)
  other arithmetic  16 us (4%)
  between operations  13.3 us (3%)
  starting transfers between devices  12.8 us (3%)
    all_gather x2, waiting for transfers between devices, body(): lall = lax.all_gather(piece, COL, axis=0, tiled=True)  88.5 us
    all_gather x1, waiting for transfers between devices, body(): rall = lax.all_gather(rpiece, ROW, axis=0, tiled=True)  49.8 us
    all_to_all x1, blocking collectives, body(): lax.all_to_all(tile, COL, split_axis=1, concat_axis=3, tiled=True)  45.7 us
    dot_general x2, matrix products, body(): lax.dot_general(a, b, dims, preferred_element_type=jnp.float32, precision...  44.2 us
    all_to_all x1, waiting for transfers between devices, permute_left(): x = lax.all_to_all(x, ROW, split_axis=2, concat_axis=2, tiled=True)  39.1 us
    all_to_all x1, waiting for transfers between devices, permute_left(): y = lax.all_to_all(y, ROW, split_axis=1, concat_axis=1, tiled=True)  33.3 us
    pallas_call x1, Pallas kernels, scatter_cols(): pl.pallas_call(functools.partial(scatter_kernel, ncol), out_shape=jax.Sha...  16.5 us
    gather x2, local copies, waits for them, and re-layouts, permute_left(): return jnp.take(y, jnp.take(idx, part_order(rows, col_count)), axis=1)  10.3 us
  transfers between devices with their start and end apart: 5, of which 4 were waited for; matrix products, arithmetic and copies ran while one was open for 18% of the time, Pallas kernels for 0%

profile of v18, /device:TPU:1, one launch (start us, length us, event | category | flops | bytes accessed | tf_op | source)
XLA Modules:
  0.0 407.9 jit_solution(14763377683013562612)
XLA Ops:
  6.5 2.6 copy.48
  11.6 8.5 %all-to-all-start = ((f32[2,8,8,16,160]{4,3,1,0,2:T(8,128)}), f32[2,8,8,16,160]{4,3,1,0,2:T(8,128)S(1)}, u32[]{:S(2)}, u32[]{:S(2)}) async-start(f32[2,8,8,16,160]{4,3,1,0,2:T(8,128)} %copy.34), calls=%async_computation | async-start | bytes 4194304 | tf_op jit(solution)/shard_map/all_to_all | solution.py:41
  20.4 39.1 %all-to-all-done = f32[2,8,8,16,160]{4,3,1,0,2:T(8,128)S(1)} async-done(((f32[2,8,8,16,160]{4,3,1,0,2:T(8,128)}), f32[2,8,8,16,160]{4,3,1,0,2:T(8,128)S(1)}, u32[]{:S(2)}, u32[]{:S(2)}) %all-to-all-start) | async-done | bytes 1310752 | tf_op jit(solution)/shard_map/all_to_all | solution.py:41
  61.1 2.3 gather_fusion.1
  64.9 4.1 %all-to-all-start.1 = ((f32[2,8,8,16,160]{4,3,2,0,1:T(8,128)}), f32[2,8,8,16,160]{4,3,2,0,1:T(8,128)S(1)}, u32[]{:S(2)}, u32[]{:S(2)}) async-start(f32[2,8,8,16,160]{4,3,2,0,1:T(8,128)} %copy_select_fusion), calls=%async_computation.1 | async-start | bytes 4194304 | tf_op jit(solution)/shard_map/all_to_all | solution.py:47
  69.1 4.5 %gather_fusion = s32[1024]{0:T(1024)S(1)} fusion(s32[1024]{0:T(1024)S(1)} %add_bitcast_fusion, s32[1024]{0:T(1024)S(1)} %broadcast_clamp_fusion), kind=kCustom, calls=%fused_computation | custom fusion | bytes 12288 | tf_op jit(solution)/shard_map/jit(_take)/gather | solution.py:53
  73.7 33.3 %all-to-all-done.1 = f32[2,8,8,16,160]{4,3,2,0,1:T(8,128)S(1)} async-done(((f32[2,8,8,16,160]{4,3,2,0,1:T(8,128)}), f32[2,8,8,16,160]{4,3,2,0,1:T(8,128)S(1)}, u32[]{:S(2)}, u32[]{:S(2)}) %all-to-all-start.1) | async-done | bytes 1310752 | tf_op jit(solution)/shard_map/all_to_all | solution.py:47
  107.2 2.9 copy.38
  110.2 5.8 %gather_fusion.2 = f32[1024,2,160]{2,1,0:T(2,128)S(1)} fusion(f32[2,1024,160]{2,0,1:T(2,128)} %copy.38, s32[1024]{0:T(1024)S(1)} %fusion.6), kind=kCustom, calls=%fused_computation.2 | custom fusion | bytes 2625536 | tf_op jit(solution)/shard_map/jit(_take)/gather | solution.py:53
  115.9 4.5 %select_bitcast_fusion = f32[2,160,1024]{1,0,2:T(2,128)} fusion(f32[1024,2,160]{2,1,0:T(2,128)S(1)} %gather_fusion.2, pred[1024]{0:T(1024)(128)(4,1)S(1)} %compare_and_fusion.1), kind=kLoop, calls=%fused_computation.6 | loop fusion | flops 327680 | bytes 2622464 | tf_op jit(solution)/shard_map/jit(_take)/select_n | solution.py:53
  120.4 49.8 %all-gather.4.cloned.1.call-done = f32[2560,1024]{1,0:T(8,128)} async-done(((f32[320,1024]{1,0:T(8,128)}), f32[2560,1024]{1,0:T(8,128)}) %all-gather.4.cloned.1.call-update) | async-done | bytes 10485776 | tf_op jit(solution)/shard_map/all_gather | solution.py:127
  170.2 2.0 slice_bitcast_fusion
  172.2 2.7 copy.40
  179.3 88.5 %all-gather.6.cloned.1.call-done = f32[2560,1664]{1,0:T(8,128)} async-done(((f32[160,1664]{1,0:T(8,128)}), f32[2560,1664]{1,0:T(8,128)}) %all-gather.6.cloned.1.call-update) | async-done | bytes 17039376 | tf_op jit(solution)/shard_map/all_gather | solution.py:144
  267.8 33.8 %fusion.11 = f32[1664,1024]{1,0:T(8,128)S(1)} fusion(f32[2560,1664]{1,0:T(8,128)} %all-gather.6.cloned.1.call-done, f32[2560,1024]{1,0:T(8,128)} %all-gather.4.cloned.1.call-done), kind=kOutput, calls=%fused_computation.55 | convolution fusion | flops 26172456960 | bytes 34340864 | tf_op jit(solution)/shard_map/dot_general | solution.py:133
  301.6 2.0 slice_subtract_fusion
  308.4 2.6 copy.41
  311.0 45.7 %all_to_all.28 = f32[2,16,52,512]{3,0,2,1:T(2,128)S(1)} all-to-all(f32[2,16,52,512]{3,0,2,1:T(2,128)S(1)} %copy.41), channel_id=1, replica_groups=mesh['xh'=2,'z'=4,'xl'=2,'y'=4,'core'=2] {'xl','y','core'}, dimensions={1} | all-to-all | bytes 6815744 | tf_op jit(solution)/shard_map/all_to_all | solution.py:155
  356.7 2.0 copy.49
  358.7 10.4 %fusion.12 = f32[384,1024]{1,0:T(8,128)S(1)} fusion(f32[2560,384]{1,0:T(8,128)} %all-gather.8.cloned.1.call-done, f32[2560,1024]{1,0:T(8,128)} %all-gather.4.cloned.1.call-done), kind=kOutput, calls=%fused_computation.56 | convolution fusion | flops 6039797760 | bytes 15990784 | tf_op jit(solution)/shard_map/dot_general | solution.py:133
  373.8 2.3 pad_maximum_fusion.1.tile_ref
  376.1 16.5 %shard_map.55 = f32[2,12,8192]{2,1,0:T(8,128)} custom-call(f32[16,2,12,512]{3,2,1,0:T(8,128)} %pad_maximum_fusion.1.tile_ref), custom_call_target="tpu_custom_call" | custom-call | tf_op jit(solution)/shard_map/pallas_call | solution.py:107
  394.5 2.5 maximum_bitcast_fusion
  396.9 4.4 %copy.47 = f32[2,64,8192]{2,1,0:T(8,128)} copy(f32[2,64,8192]{2,0,1:T(2,128)S(1)} %maximum_bitcast_fusion) | data formatting | bytes 8388608 | tf_op jit(solution)/shard_map/reshape | solution.py:157
  (44 shorter events, 21.9 us)
Async XLA Ops:
  6.5 2.7 copy-start
  6.5 163.6 %all-gather.4.cloned.1.call-start = ((), (), s32[]{:S(2)}) async-start(), calls=%async_computation.3 | async-start | bytes 11796480 | tf_op jit(solution)/shard_map/all_gather | solution.py:127
  11.6 8.5 %copy-start.2 = (s32[64]{0:T(128)S(1)}, s32[64]{0:T(128)}, u32[]{:S(2)}) copy-start(s32[64]{0:T(128)} %param.7) | copy-start | bytes 772
  11.6 8.7 %copy-start.3 = (s32[7]{0:T(128)S(1)}, s32[7]{0:T(128)}, u32[]{:S(2)}) copy-start(s32[7]{0:T(128)} %param.8) | copy-start | bytes 88
  11.6 47.9 %all-to-all-start = ((f32[2,8,8,16,160]{4,3,1,0,2:T(8,128)}), f32[2,8,8,16,160]{4,3,1,0,2:T(8,128)S(1)}, u32[]{:S(2)}, u32[]{:S(2)}) async-start(f32[2,8,8,16,160]{4,3,1,0,2:T(8,128)} %copy.34), calls=%async_computation | async-start | bytes 4194304 | tf_op jit(solution)/shard_map/all_to_all | solution.py:41
  64.9 4.3 %copy-start.1 = (s32[1024]{0:T(1024)S(1)}, s32[1024]{0:T(1024)}, u32[]{:S(2)}) copy-start(s32[1024]{0:T(1024)} %constant.116) | copy-start | bytes 12292
  64.9 42.1 %all-to-all-start.1 = ((f32[2,8,8,16,160]{4,3,2,0,1:T(8,128)}), f32[2,8,8,16,160]{4,3,2,0,1:T(8,128)S(1)}, u32[]{:S(2)}, u32[]{:S(2)}) async-start(f32[2,8,8,16,160]{4,3,2,0,1:T(8,128)} %copy_select_fusion), calls=%async_computation.1 | async-start | bytes 4194304 | tf_op jit(solution)/shard_map/all_to_all | solution.py:47
  69.0 198.8 %all-gather.6.cloned.1.call-start = ((), (), s32[]{:S(2)}) async-start(), calls=%async_computation.4 | async-start | bytes 18104320 | tf_op jit(solution)/shard_map/all_gather | solution.py:144
  176.7 182.0 %all-gather.8.cloned.1.call-start = ((), (), s32[]{:S(2)}) async-start(), calls=%async_computation.5 | async-start | bytes 4177920 | tf_op jit(solution)/shard_map/all_gather | solution.py:144
Sparse Core Ops, SparseCore 0:
  9.7 160.4 all-gather.3
  176.9 90.8 all-gather.5
  269.4 38.0 all-gather.7

commit v19 on v18

--- a/solution.py
+++ b/solution.py
@@ -54,7 +54,7 @@
 
 
 def part_sizes(q_total):
-    return [q_total * 13 // 16, q_total - q_total * 13 // 16]
+    return [q_total * 7 // 8, q_total - q_total * 7 // 8]
 
 
 def part_order(rows, col_count):

time: 409 us -> 394 us (0.963)
  local copies, waits for them, and re-layouts: 48.6 us -> 34.3 us
  Pallas kernels: 16.5 us -> 11 us
  waiting for transfers between devices: 211 us -> 216 us
    another operation x5 -> x0, local copies, waits for them, and re-layouts: 9.18 us -> none  [the longest x3 5.51 us: body(): tile = jnp.stack([re, im], axis=0)]
    reshape x4 -> x0, local copies, waits for them, and re-layouts: 9.03 us -> none  [the longest x1 4.44 us: body(): return out.reshape(2, rows // col_count, col_count * cols)]
    all_gather x2, waiting for transfers between devices: 88.5 us -> 96.1 us  [body(): lall = lax.all_gather(piece, COL, axis=0, tiled=True)]
    pallas_call x1, Pallas kernels: 16.5 us -> 11 us  [scatter_cols(): pl.pallas_call(functools.partial(scatter_kernel, ncol), out_shape=jax.Sha...]
where the time goes in v19:
time: 394 us
  waiting for transfers between devices  216 us (55%)
  blocking collectives  48.3 us (12%)
  matrix products  44.5 us (11%)
  local copies, waits for them, and re-layouts  34.3 us (9%)
  other arithmetic  14 us (4%)
  between operations  13.3 us (3%)
  starting transfers between devices  12.8 us (3%)
  Pallas kernels  11 us (3%)
    all_gather x2, waiting for transfers between devices, body(): lall = lax.all_gather(piece, COL, axis=0, tiled=True)  96.1 us
    all_to_all x1, blocking collectives, body(): lax.all_to_all(tile, COL, split_axis=1, concat_axis=3, tiled=True)  48.3 us
    all_gather x1, waiting for transfers between devices, body(): rall = lax.all_gather(rpiece, ROW, axis=0, tiled=True)  47.2 us
    dot_general x2, matrix products, body(): lax.dot_general(a, b, dims, preferred_element_type=jnp.float32, precision...  44.5 us
    all_to_all x1, waiting for transfers between devices, permute_left(): x = lax.all_to_all(x, ROW, split_axis=2, concat_axis=2, tiled=True)  39.1 us
    all_to_all x1, waiting for transfers between devices, permute_left(): y = lax.all_to_all(y, ROW, split_axis=1, concat_axis=1, tiled=True)  33.3 us
    gather x2, local copies, waits for them, and re-layouts, permute_left(): return jnp.take(y, jnp.take(idx, part_order(rows, col_count)), axis=1)  13.4 us
    pallas_call x1, Pallas kernels, scatter_cols(): pl.pallas_call(functools.partial(scatter_kernel, ncol), out_shape=jax.Sha...  11 us
  transfers between devices with their start and end apart: 5, of which 4 were waited for; matrix products, arithmetic and copies ran while one was open for 18% of the time, Pallas kernels for 0%

profile of v19, /device:TPU:1, one launch (start us, length us, event | category | flops | bytes accessed | tf_op | source)
XLA Modules:
  0.0 393.9 jit_solution(7778309797960416506)
XLA Ops:
  6.5 2.6 copy.49
  10.0 1.6 copy.38
  11.6 8.5 %all-to-all-start = ((f32[2,8,8,16,160]{4,3,1,0,2:T(8,128)}), f32[2,8,8,16,160]{4,3,1,0,2:T(8,128)S(1)}, u32[]{:S(2)}, u32[]{:S(2)}) async-start(f32[2,8,8,16,160]{4,3,1,0,2:T(8,128)} %copy.38), calls=%async_computation | async-start | bytes 4194304 | tf_op jit(solution)/shard_map/all_to_all | solution.py:41
  20.4 39.1 %all-to-all-done = f32[2,8,8,16,160]{4,3,1,0,2:T(8,128)S(1)} async-done(((f32[2,8,8,16,160]{4,3,1,0,2:T(8,128)}), f32[2,8,8,16,160]{4,3,1,0,2:T(8,128)S(1)}, u32[]{:S(2)}, u32[]{:S(2)}) %all-to-all-start) | async-done | bytes 1310752 | tf_op jit(solution)/shard_map/all_to_all | solution.py:41
  59.5 1.6 copy.39
  61.1 2.3 gather_fusion.1
  63.3 1.5 copy_select_fusion
  64.9 4.1 %all-to-all-start.1 = ((f32[2,8,8,16,160]{4,3,2,0,1:T(8,128)}), f32[2,8,8,16,160]{4,3,2,0,1:T(8,128)S(1)}, u32[]{:S(2)}, u32[]{:S(2)}) async-start(f32[2,8,8,16,160]{4,3,2,0,1:T(8,128)} %copy_select_fusion), calls=%async_computation.1 | async-start | bytes 4194304 | tf_op jit(solution)/shard_map/all_to_all | solution.py:47
  69.1 4.5 %gather_fusion = s32[1024]{0:T(1024)S(1)} fusion(s32[1024]{0:T(1024)S(1)} %add_bitcast_fusion, s32[1024]{0:T(1024)S(1)} %broadcast_clamp_fusion), kind=kCustom, calls=%fused_computation | custom fusion | bytes 12288 | tf_op jit(solution)/shard_map/jit(_take)/gather | solution.py:53
  73.7 33.3 %all-to-all-done.1 = f32[2,8,8,16,160]{4,3,2,0,1:T(8,128)S(1)} async-done(((f32[2,8,8,16,160]{4,3,2,0,1:T(8,128)}), f32[2,8,8,16,160]{4,3,2,0,1:T(8,128)S(1)}, u32[]{:S(2)}, u32[]{:S(2)}) %all-to-all-start.1) | async-done | bytes 1310752 | tf_op jit(solution)/shard_map/all_to_all | solution.py:47
  107.2 1.6 copy.42
  108.9 8.9 %gather_fusion.2 = f32[1024,2,160]{2,1,0:T(2,128)} fusion(f32[2,1024,160]{2,0,1:T(2,128)S(1)} %copy.42, s32[1024]{0:T(1024)S(1)} %fusion.8), kind=kCustom, calls=%fused_computation.2 | custom fusion | bytes 2625536 | tf_op jit(solution)/shard_map/jit(_take)/gather | solution.py:53
  117.7 5.2 %select_bitcast_fusion = f32[2,160,1024]{1,0,2:T(2,128)S(1)} fusion(f32[1024,2,160]{2,1,0:T(2,128)} %gather_fusion.2, pred[1024]{0:T(1024)(128)(4,1)S(1)} %compare_and_fusion.1), kind=kLoop, calls=%fused_computation.6 | loop fusion | flops 327680 | bytes 2622464 | tf_op jit(solution)/shard_map/jit(_take)/select_n | solution.py:53
  123.0 47.2 %all-gather.4.cloned.1.call-done = f32[2560,1024]{1,0:T(8,128)} async-done(((f32[320,1024]{1,0:T(8,128)}), f32[2560,1024]{1,0:T(8,128)}) %all-gather.4.cloned.1.call-update) | async-done | bytes 10485776 | tf_op jit(solution)/shard_map/all_gather | solution.py:127
  170.2 1.9 slice_bitcast_fusion
  172.0 4.2 %copy.44 = f32[160,2,896]{2,1,0:T(2,128)S(1)} copy(f32[160,2,896]{0,1,2:T(2,128)} %slice_bitcast_fusion) | data formatting | bytes 2293760 | tf_op jit(solution)/shard_map/transpose | solution.py:141
  176.2 1.1 copy.51
  178.4 96.1 %all-gather.6.cloned.1.call-done = f32[2560,1792]{1,0:T(8,128)} async-done(((f32[160,1792]{1,0:T(8,128)}), f32[2560,1792]{1,0:T(8,128)}) %all-gather.6.cloned.1.call-update) | async-done | bytes 18350096 | tf_op jit(solution)/shard_map/all_gather | solution.py:144
  274.5 36.5 %fusion.13 = f32[1792,1024]{1,0:T(8,128)S(1)} fusion(f32[2560,1792]{1,0:T(8,128)} %all-gather.6.cloned.1.call-done, f32[2560,1024]{1,0:T(8,128)} %all-gather.4.cloned.1.call-done), kind=kOutput, calls=%fused_computation.58 | convolution fusion | flops 28185722880 | bytes 36175872 | tf_op jit(solution)/shard_map/dot_general | solution.py:133
  312.4 48.3 %all_to_all.28 = f32[2,16,56,512]{3,2,0,1:T(8,128)S(1)} all-to-all(f32[2,16,56,512]{3,2,0,1:T(8,128)S(1)} %pad_maximum_fusion), channel_id=1, replica_groups=mesh['xh'=2,'z'=4,'xl'=2,'y'=4,'core'=2] {'xl','y','core'}, dimensions={1} | all-to-all | bytes 7340032 | tf_op jit(solution)/shard_map/all_to_all | solution.py:155
  360.7 2.2 copy.50
  362.9 7.9 %fusion.14 = f32[256,1024]{1,0:T(8,128)S(1)} fusion(f32[2560,256]{1,0:T(8,128)} %all-gather.8.cloned.1.call-done, f32[2560,1024]{1,0:T(8,128)} %all-gather.4.cloned.1.call-done), kind=kOutput, calls=%fused_computation.59 | convolution fusion | flops 4026531840 | bytes 14155776 | tf_op jit(solution)/shard_map/dot_general | solution.py:133
  371.8 11.0 %shard_map.55 = f32[2,8,8192]{2,1,0:T(8,128)} custom-call(f32[16,2,8,512]{3,2,1,0:T(8,128)} %pad_maximum_fusion.1.tile_ref), custom_call_target="tpu_custom_call" | custom-call | tf_op jit(solution)/shard_map/pallas_call | solution.py:107
  382.8 4.6 %maximum_bitcast_fusion = f32[2,64,8192]{2,1,0:T(8,128)} fusion(f32[2,1,8,8192]{3,2,0,1:T(8,128)} %bitcast.73, f32[2,1,56,8192]{3,2,0,1:T(8,128)} %bitcast.63), kind=kLoop, calls=%fused_computation.3 | loop fusion | flops 1048576 | bytes 8388608 | tf_op jit(solution)/shard_map/reshape | solution.py:157
  (37 shorter events, 4.9 us)
Async XLA Ops:
  6.5 2.7 copy-start
  6.5 163.6 %all-gather.4.cloned.1.call-start = ((), (), s32[]{:S(2)}) async-start(), calls=%async_computation.3 | async-start | bytes 11796480 | tf_op jit(solution)/shard_map/all_gather | solution.py:127
  11.6 8.5 %copy-start.2 = (s32[64]{0:T(128)S(1)}, s32[64]{0:T(128)}, u32[]{:S(2)}) copy-start(s32[64]{0:T(128)} %param.7) | copy-start | bytes 772
  11.6 8.7 %copy-start.3 = (s32[7]{0:T(128)S(1)}, s32[7]{0:T(128)}, u32[]{:S(2)}) copy-start(s32[7]{0:T(128)} %param.8) | copy-start | bytes 88
  11.6 47.9 %all-to-all-start = ((f32[2,8,8,16,160]{4,3,1,0,2:T(8,128)}), f32[2,8,8,16,160]{4,3,1,0,2:T(8,128)S(1)}, u32[]{:S(2)}, u32[]{:S(2)}) async-start(f32[2,8,8,16,160]{4,3,1,0,2:T(8,128)} %copy.38), calls=%async_computation | async-start | bytes 4194304 | tf_op jit(solution)/shard_map/all_to_all | solution.py:41
  64.9 4.3 %copy-start.1 = (s32[1024]{0:T(1024)S(1)}, s32[1024]{0:T(1024)}, u32[]{:S(2)}) copy-start(s32[1024]{0:T(1024)} %constant.116) | copy-start | bytes 12292
  64.9 42.1 %all-to-all-start.1 = ((f32[2,8,8,16,160]{4,3,2,0,1:T(8,128)}), f32[2,8,8,16,160]{4,3,2,0,1:T(8,128)S(1)}, u32[]{:S(2)}, u32[]{:S(2)}) async-start(f32[2,8,8,16,160]{4,3,2,0,1:T(8,128)} %copy_select_fusion), calls=%async_computation.1 | async-start | bytes 4194304 | tf_op jit(solution)/shard_map/all_to_all | solution.py:47
  69.0 205.5 %all-gather.6.cloned.1.call-start = ((), (), s32[]{:S(2)}) async-start(), calls=%async_computation.4 | async-start | bytes 19496960 | tf_op jit(solution)/shard_map/all_gather | solution.py:144
  177.3 185.6 %all-gather.8.cloned.1.call-start = ((), (), s32[]{:S(2)}) async-start(), calls=%async_computation.5 | async-start | bytes 2785280 | tf_op jit(solution)/shard_map/all_gather | solution.py:144
Sparse Core Ops, SparseCore 0:
  9.7 160.4 all-gather.3
  177.4 97.0 all-gather.5
  276.2 35.9 all-gather.7

commit v20 on v13

--- a/solution.py
+++ b/solution.py
@@ -127,12 +127,11 @@
     rall = lax.all_gather(rpiece, ROW, axis=0, tiled=True)
     lp = permute_left(left, prefix_owner, qubit_order, row_count, col_count)
     lt = jnp.swapaxes(lp, 1, 2)
-    lt = lax.optimization_barrier((lt, rall))[0]
     high = lax.Precision.HIGH
     dims = (((0,), (0,)), ((), ()))
     dot = lambda a, b: lax.dot_general(a, b, dims, preferred_element_type=jnp.float32, precision=high)
     outs = []
-    prev = None
+    prev = rall
     start = 0
     for qp in part_sizes(rows // col_count):
         part = qp * col_count

time: 377 us -> 374 us (level)
  waiting for transfers between devices: 204 us -> 199 us
    all_gather x1, waiting for transfers between devices: 49.8 us -> 41.5 us  [body(): rall = lax.all_gather(rpiece, ROW, axis=0, tiled=True)]
  transfers between devices with their start and end apart: 5 -> 5, of which waited for: 4 -> 4; matrix products, arithmetic and copies ran while one was open for 16% -> 18% of each run, Pallas kernels for 0% -> 0%
where the time goes in v20:
time: 374 us; the launch traced here: 372 us
  waiting for transfers between devices  199 us (53%)
  matrix products  43.7 us (12%)
  blocking collectives  42.7 us (11%)
  local copies, waits for them, and re-layouts  31.5 us (8%)
  Pallas kernels  16.6 us (4%)
  between operations  13.3 us (4%)
  other arithmetic  13 us (3%)
  starting transfers between devices  12.8 us (3%)
    all_gather x2, waiting for transfers between devices, body(): lall = lax.all_gather(piece, COL, axis=0, tiled=True)  84.8 us
    dot_general x2, matrix products, body(): lax.dot_general(a, b, dims, preferred_element_type=jnp.float32, precision...  43.7 us
    all_to_all x1, blocking collectives, body(): lax.all_to_all(tile, COL, split_axis=1, concat_axis=3, tiled=True)  42.7 us
    all_gather x1, waiting for transfers between devices, body(): rall = lax.all_gather(rpiece, ROW, axis=0, tiled=True)  41.5 us
    all_to_all x1, waiting for transfers between devices, permute_left(): x = lax.all_to_all(x, ROW, split_axis=2, concat_axis=2, tiled=True)  39.1 us
    all_to_all x1, waiting for transfers between devices, permute_left(): y = lax.all_to_all(y, ROW, split_axis=1, concat_axis=1, tiled=True)  33.3 us
    pallas_call x1, Pallas kernels, scatter_cols(): pl.pallas_call(functools.partial(scatter_kernel, ncol), out_shape=jax.Sha...  16.6 us
    gather x2, local copies, waits for them, and re-layouts, permute_left(): return jnp.take(y, jnp.take(idx, part_order(rows, col_count)), axis=1)  13.4 us
  transfers between devices with their start and end apart: 5, of which 4 were waited for; matrix products, arithmetic and copies ran while one was open for 18% of the time, Pallas kernels for 0%

profile of v20, /device:TPU:1, one launch (start us, length us, event | category | flops | bytes accessed | tf_op | source)
XLA Modules:
  0.0 372.4 jit_solution(15579245797216481862)
XLA Ops:
  6.5 2.6 copy.49
  10.0 1.6 copy.38
  11.6 8.5 %all-to-all-start = ((f32[2,8,8,16,160]{4,3,1,0,2:T(8,128)}), f32[2,8,8,16,160]{4,3,1,0,2:T(8,128)S(1)}, u32[]{:S(2)}, u32[]{:S(2)}) async-start(f32[2,8,8,16,160]{4,3,1,0,2:T(8,128)} %copy.38), calls=%async_computation | async-start | bytes 4194304 | tf_op jit(solution)/shard_map/all_to_all | solution.py:41
  20.4 39.1 %all-to-all-done = f32[2,8,8,16,160]{4,3,1,0,2:T(8,128)S(1)} async-done(((f32[2,8,8,16,160]{4,3,1,0,2:T(8,128)}), f32[2,8,8,16,160]{4,3,1,0,2:T(8,128)S(1)}, u32[]{:S(2)}, u32[]{:S(2)}) %all-to-all-start) | async-done | bytes 1310752 | tf_op jit(solution)/shard_map/all_to_all | solution.py:41
  59.5 1.6 copy.39
  61.1 2.3 gather_fusion.1
  63.3 1.5 copy_select_fusion
  64.9 4.1 %all-to-all-start.1 = ((f32[2,8,8,16,160]{4,3,2,0,1:T(8,128)}), f32[2,8,8,16,160]{4,3,2,0,1:T(8,128)S(1)}, u32[]{:S(2)}, u32[]{:S(2)}) async-start(f32[2,8,8,16,160]{4,3,2,0,1:T(8,128)} %copy_select_fusion), calls=%async_computation.1 | async-start | bytes 4194304 | tf_op jit(solution)/shard_map/all_to_all | solution.py:47
  69.1 4.5 %gather_fusion = s32[1024]{0:T(1024)S(1)} fusion(s32[1024]{0:T(1024)S(1)} %add_bitcast_fusion, s32[1024]{0:T(1024)S(1)} %broadcast_clamp_fusion), kind=kCustom, calls=%fused_computation | custom fusion | bytes 12288 | tf_op jit(solution)/shard_map/jit(_take)/gather | solution.py:53
  73.7 33.3 %all-to-all-done.1 = f32[2,8,8,16,160]{4,3,2,0,1:T(8,128)S(1)} async-done(((f32[2,8,8,16,160]{4,3,2,0,1:T(8,128)}), f32[2,8,8,16,160]{4,3,2,0,1:T(8,128)S(1)}, u32[]{:S(2)}, u32[]{:S(2)}) %all-to-all-start.1) | async-done | bytes 1310752 | tf_op jit(solution)/shard_map/all_to_all | solution.py:47
  107.2 1.6 copy.42
  108.9 8.9 %gather_fusion.2 = f32[1024,2,160]{2,1,0:T(2,128)} fusion(f32[2,1024,160]{2,0,1:T(2,128)S(1)} %copy.42, s32[1024]{0:T(1024)S(1)} %fusion.6), kind=kCustom, calls=%fused_computation.2 | custom fusion | bytes 2625536 | tf_op jit(solution)/shard_map/jit(_take)/gather | solution.py:53
  117.7 5.2 %select_bitcast_fusion = f32[2,160,1024]{1,0,2:T(2,128)S(1)} fusion(f32[1024,2,160]{2,1,0:T(2,128)} %gather_fusion.2, pred[1024]{0:T(1024)(128)(4,1)S(1)} %compare_and_fusion.1), kind=kLoop, calls=%fused_computation.6 | loop fusion | flops 327680 | bytes 2622464 | tf_op jit(solution)/shard_map/jit(_take)/select_n | solution.py:53
  123.0 1.7 slice_bitcast_fusion
  124.7 3.0 copy.43
  127.6 1.0 copy.51
  128.6 41.5 %all-gather.4.cloned.1.call-done = f32[2560,1024]{1,0:T(8,128)} async-done(((f32[320,1024]{1,0:T(8,128)}), f32[2560,1024]{1,0:T(8,128)}) %all-gather.4.cloned.1.call-update) | async-done | bytes 10485776 | tf_op jit(solution)/shard_map/all_gather | solution.py:127
  171.8 84.8 %all-gather.6.cloned.1.call-done = f32[2560,1536]{1,0:T(8,128)} async-done(((f32[160,1536]{1,0:T(8,128)}), f32[2560,1536]{1,0:T(8,128)}) %all-gather.6.cloned.1.call-update) | async-done | bytes 15728656 | tf_op jit(solution)/shard_map/all_gather | solution.py:143
  256.6 31.6 %fusion.11 = f32[1536,1024]{1,0:T(8,128)S(1)} fusion(f32[2560,1536]{1,0:T(8,128)} %all-gather.6.cloned.1.call-done, f32[2560,1024]{1,0:T(8,128)} %all-gather.4.cloned.1.call-done), kind=kOutput, calls=%fused_computation.55 | convolution fusion | flops 24159191040 | bytes 32505856 | tf_op jit(solution)/shard_map/dot_general | solution.py:132
  289.3 42.7 %all_to_all.28 = f32[2,16,48,512]{3,2,0,1:T(8,128)S(1)} all-to-all(f32[2,16,48,512]{3,2,0,1:T(8,128)S(1)} %pad_maximum_fusion), channel_id=1, replica_groups=mesh['xh'=2,'z'=4,'xl'=2,'y'=4,'core'=2] {'xl','y','core'}, dimensions={1} | all-to-all | bytes 6291456 | tf_op jit(solution)/shard_map/all_to_all | solution.py:154
  332.3 12.1 %fusion.12 = f32[512,1024]{1,0:T(8,128)S(1)} fusion(f32[2560,512]{1,0:T(8,128)} %all-gather.8.cloned.1.call-done, f32[2560,1024]{1,0:T(8,128)} %all-gather.4.cloned.1.call-done), kind=kOutput, calls=%fused_computation.56 | convolution fusion | flops 8053063680 | bytes 17825792 | tf_op jit(solution)/shard_map/dot_general | solution.py:132
  344.7 1.0 pad_maximum_fusion.1.tile_ref
  345.7 16.6 %shard_map.55 = f32[2,16,8192]{2,1,0:T(8,128)} custom-call(f32[16,2,16,512]{3,2,1,0:T(8,128)} %pad_maximum_fusion.1.tile_ref), custom_call_target="tpu_custom_call" | custom-call | tf_op jit(solution)/shard_map/pallas_call | solution.py:107
  362.3 3.5 maximum_bitcast_fusion
  (37 shorter events, 4.7 us)
Async XLA Ops:
  6.5 2.7 copy-start
  6.5 163.6 %all-gather.4.cloned.1.call-start = ((), (), s32[]{:S(2)}) async-start(), calls=%async_computation.3 | async-start | bytes 11796480 | tf_op jit(solution)/shard_map/all_gather | solution.py:127
  11.6 8.5 %copy-start.2 = (s32[64]{0:T(128)S(1)}, s32[64]{0:T(128)}, u32[]{:S(2)}) copy-start(s32[64]{0:T(128)} %param.7) | copy-start | bytes 772
  11.6 8.7 %copy-start.3 = (s32[7]{0:T(128)S(1)}, s32[7]{0:T(128)}, u32[]{:S(2)}) copy-start(s32[7]{0:T(128)} %param.8) | copy-start | bytes 88
  11.6 47.9 %all-to-all-start = ((f32[2,8,8,16,160]{4,3,1,0,2:T(8,128)}), f32[2,8,8,16,160]{4,3,1,0,2:T(8,128)S(1)}, u32[]{:S(2)}, u32[]{:S(2)}) async-start(f32[2,8,8,16,160]{4,3,1,0,2:T(8,128)} %copy.38), calls=%async_computation | async-start | bytes 4194304 | tf_op jit(solution)/shard_map/all_to_all | solution.py:41
  64.9 4.3 %copy-start.1 = (s32[1024]{0:T(1024)S(1)}, s32[1024]{0:T(1024)}, u32[]{:S(2)}) copy-start(s32[1024]{0:T(1024)} %constant.116) | copy-start | bytes 12292
  64.9 42.1 %all-to-all-start.1 = ((f32[2,8,8,16,160]{4,3,2,0,1:T(8,128)}), f32[2,8,8,16,160]{4,3,2,0,1:T(8,128)S(1)}, u32[]{:S(2)}, u32[]{:S(2)}) async-start(f32[2,8,8,16,160]{4,3,2,0,1:T(8,128)} %copy_select_fusion), calls=%async_computation.1 | async-start | bytes 4194304 | tf_op jit(solution)/shard_map/all_to_all | solution.py:47
  69.0 187.6 %all-gather.6.cloned.1.call-start = ((), (), s32[]{:S(2)}) async-start(), calls=%async_computation.4 | async-start | bytes 16711680 | tf_op jit(solution)/shard_map/all_gather | solution.py:143
  170.2 162.1 %all-gather.8.cloned.1.call-start = ((), (), s32[]{:S(2)}) async-start(), calls=%async_computation.5 | async-start | bytes 5570560 | tf_op jit(solution)/shard_map/all_gather | solution.py:143
Sparse Core Ops, SparseCore 0:
  9.7 160.4 all-gather.3
  171.9 84.6 all-gather.5
  258.3 41.0 all-gather.7
